TPU v7x, 32 devices: a whole 2x2x4 slice. The times are simulated.
32 devices in a mesh: dp: 4 (over y, x), expert: 8 (over z, core).
Axes of the slice: x: 2, y: 2, z: 4, core: 2. Of those that a mesh axis runs over, the one named last changes fastest.
Arguments:
- tokens: bfloat16 [4096, 1024], P(('dp', 'expert')), may hold values from -6 to 6
- routes: int32 [4096, 8], P(('dp', 'expert')), may hold values from 0 to 15, all different within a row; in each aligned block of 128 rows (0 to 127, 128 to 255, ...) at most 80 rows name the same one
- route_weights: float32 [4096, 8], P(('dp', 'expert')), may hold values from 0.03 to 0.5
- gate_weight: bfloat16 [16, 1024, 512], P('expert'), may hold values from -0.1875 to 0.1875
- up_weight: bfloat16 [16, 1024, 512], P('expert'), may hold values from -0.1875 to 0.1875
- down_weight: bfloat16 [16, 512, 1024], P('expert'), may hold values from -0.25 to 0.25
- cotangent: bfloat16 [4096, 1024], P(('dp', 'expert')), may hold values from -6 to 6
Outputs:
- layer_out: bfloat16 [4096, 1024], P(('dp', 'expert'))
- token_grads: bfloat16 [4096, 1024], P(('dp', 'expert'))
- route_grads: float32 [4096, 8], P(('dp', 'expert'))
- gate_grads: float32 [16, 1024, 512], P('expert', 'dp')
- up_grads: float32 [16, 1024, 512], P('expert', 'dp')
- down_grads: float32 [16, 512, 1024], P('expert', 'dp')
Inputs may be any that keep to these rules, and one draw needn't show every extreme that they name: `routes`: A token names 8 different experts. Among the token-route pairs of one device's 128 tokens (aligned blocks of rows), no expert is named more than 80 times, a bound that some block reaches.
All inputs are finite; a program needn't handle non-finite values.
Results may differ from a plain program's by a relative error of at most 0.0065.
Values may be sent and summed in bfloat16 or wider, within the bound.
No kernel may reach another device: no remote copies, remote signals or barrier semaphores. Data moves between devices by JAX's collectives and lax.ppermute only.
A program may use at most 128 MiB of HBM per device.

v0:
```python
import math

import jax
import jax.numpy as jnp
from jax import lax
from jax.experimental import pallas as pl
from jax.experimental.pallas import tpu as pltpu
from jax.sharding import PartitionSpec as P

BF = jnp.bfloat16
F32 = jnp.float32
VMEM = pl.BlockSpec(memory_space=pltpu.VMEM)
SMEM = pl.BlockSpec(memory_space=pltpu.SMEM)
NT = (((1,), (1,)), ((), ()))


def mm(a, b):
    return jnp.dot(a, b, preferred_element_type=F32)


def mm_nt(a, b):
    return lax.dot_general(a, b, NT, preferred_element_type=F32)


def size(s):
    return math.prod(s.shape) * jnp.dtype(s.dtype).itemsize


def on_chip(body, operands, out_shape, flops, name, scalars=0, scratch=()):
    total = sum(size(s) for s in list(operands) + list(out_shape))
    limit = min(60 * 2**20, total // 3 + sum(size(s) for s in scratch) + 4 * 2**20)
    return pl.pallas_call(
        body,
        in_specs=[SMEM] * scalars + [VMEM] * (len(operands) - scalars),
        out_specs=[VMEM] * len(out_shape),
        out_shape=out_shape,
        scratch_shapes=list(scratch),
        compiler_params=pltpu.CompilerParams(vmem_limit_bytes=limit),
        cost_estimate=pl.CostEstimate(
            flops=10**10, bytes_accessed=total, transcendentals=0
        ),
        name=name,
    )(*operands)


def extra_rows(e_total, T, D):
    return -(-3 * e_total * T // (8 * D)) * 8


def thirds(v):
    hi = v.astype(BF).astype(F32)
    mid = (v - hi).astype(BF).astype(F32)
    return hi, mid, v - hi - mid


def pack_tokens(tokens, routes_t, weights_t, e_total):
    T, D = tokens.shape
    extra = extra_rows(e_total, T, D)
    per = D // T

    def body(tok_ref, routes_ref, weights_ref, out_ref, buf):
        expert = lax.broadcasted_iota(jnp.int32, (e_total, T), 0)
        dense = jnp.zeros((e_total, T), F32)
        for k in range(routes_t.shape[0]):
            dense = dense + jnp.where(
                routes_ref[k : k + 1, :] == expert, weights_ref[k : k + 1, :], 0.0
            )
        buf[...] = jnp.zeros_like(buf)
        for p, part in enumerate(thirds(dense)):
            for i in range(e_total):
                row = p * (e_total // per) + i // per
                at = slice(i % per * T, (i % per + 1) * T)
                buf[row : row + 1, at] = part[i : i + 1, :]
        out_ref[:T, :] = tok_ref[...]
        out_ref[T:, :] = buf[...].astype(BF)

    return on_chip(
        body,
        [tokens, routes_t, weights_t],
        [jax.ShapeDtypeStruct((T + extra, D), BF)],
        0,
        "pack_tokens",
        scratch=[pltpu.VMEM((extra, D), F32)],
    )[0]


def collect(blocks, *earlier):
    nb, h = len(blocks), blocks[0].shape[0]

    def body(*refs):
        for i in range(nb):
            refs[-1][i * h : (i + 1) * h, :] = refs[i][...]

    shape = jax.ShapeDtypeStruct((nb * h, blocks[0].shape[1]), BF)
    return on_chip(body, [*blocks, *earlier], [shape], 0, "collect")[0]


TOKEN = jax.ShapeDtypeStruct((8, 128), F32)


def forward(place, near, far, gate, up, down, T, e_total):
    E, D, F = gate.shape
    step = T + extra_rows(e_total, T, D)
    nb = near.shape[0] // step
    rows, wide, per = 2 * nb * T, E * F, e_total * T // D

    def body(place_ref, near_in, far_in, gate_ref, up_ref, down_ref, *refs):
        hid_refs, wa_refs, wb_refs = refs[0:2], refs[2:4], refs[4:6]
        hwt_ref, tokt_ref, near_ref, far_ref, token_ref, buf = refs[6:]
        token_ref[...] = jnp.zeros_like(token_ref)
        diagonal = lax.broadcasted_iota(jnp.int32, (T, T), 0) == lax.broadcasted_iota(
            jnp.int32, (T, T), 1
        )
        sublane = lax.broadcasted_iota(jnp.int32, (buf.shape[0], T), 0)
        buf[...] = jnp.zeros_like(buf)
        for side, source in enumerate((near_in, far_in)):
            for i in range(0, nb, 2):
                xs, ws = [], [[] for _ in range(E)]
                for b in (i, i + 1):
                    xs.append(source[b * step : b * step + T, :])
                    packed = source[b * step + T : (b + 1) * step, :].astype(F32)
                    buf[:per, :] = (
                        packed[:per] + packed[per : 2 * per] + packed[2 * per : 3 * per]
                    )
                    for j in range(E):
                        flat = (place_ref[2] * E + j) * T
                        at = pl.ds(pl.multiple_of(flat % D, T), T)
                        row = jnp.where(sublane == flat // D, buf[:, at], 0.0)
                        row = jnp.broadcast_to(jnp.sum(row, axis=0, keepdims=True), (T, T))
                        ws[j].append(
                            jnp.sum(jnp.where(diagonal, row, 0.0), axis=1, keepdims=True)
                        )
                x = jnp.concatenate(xs, axis=0)
                here = slice(i * T, (i + 2) * T)
                at = slice((side * nb + i) * T, (side * nb + i + 2) * T)
                tokt_ref[:, at] = x.T
                part = jnp.zeros((2 * T, D), F32)
                for j in range(E):
                    cols = slice(j * F, (j + 1) * F)
                    g = mm(x, gate_ref[j])
                    u = mm(x, up_ref[j])
                    w = jnp.concatenate(ws[j], axis=0)
                    s = jax.nn.sigmoid(g)
                    a = g * s
                    hid = a * u
                    hid_refs[side][here, cols] = hid.astype(BF)
                    wa_refs[side][here, cols] = (w * a).astype(BF)
                    wb_refs[side][here, cols] = (w * (u * s * (1.0 + g * (1.0 - s)))).astype(BF)
                    scaled = (w * hid).astype(BF)
                    hwt_ref[cols, at] = scaled.T
                    part = part + mm(scaled, down_ref[j])
                if side == 0:
                    near_ref[here, :] = part
                else:
                    far_ref[here, :] = part.astype(BF)

    out_shape = [jax.ShapeDtypeStruct((rows // 2, wide), BF)] * 6 + [
        jax.ShapeDtypeStruct((wide, rows), BF),
        jax.ShapeDtypeStruct((D, rows), BF),
        jax.ShapeDtypeStruct((rows // 2, D), F32),
        jax.ShapeDtypeStruct((rows // 2, D), BF),
        TOKEN,
    ]
    return on_chip(
        body,
        [place, near, far, gate, up, down],
        out_shape,
        6 * rows * D * wide,
        "forward",
        scalars=1,
        scratch=[pltpu.VMEM((-(-per // 8) * 8, D), F32)],
    )


def hidden_grads(cot, hid, wa, wb, down, *earlier):
    E, F, D = down.shape
    rows, wide = cot.shape[0], E * F
    step = 256

    def body(*refs):
        cot_ref, hid_ref, wa_ref, wb_ref, down_ref = refs[:5]
        gg_ref, ug_ref, rg_ref, token_ref = refs[5 + len(earlier) :]
        token_ref[...] = jnp.zeros_like(token_ref)
        lane = lax.broadcasted_iota(jnp.int32, (step, 128), 1)
        for m in range(0, rows, step):
            at = slice(m, m + step)
            c = cot_ref[at, :]
            total = jnp.zeros((step, 128), F32)
            for j in range(E):
                cols = slice(j * F, (j + 1) * F)
                h = mm_nt(c, down_ref[j])
                gg_ref[at, cols] = (h * wb_ref[at, cols].astype(F32)).astype(BF)
                ug_ref[at, cols] = (h * wa_ref[at, cols].astype(F32)).astype(BF)
                r = jnp.sum(h * hid_ref[at, cols].astype(F32), axis=1, keepdims=True)
                total = jnp.where(lane == j, r, total)
            rg_ref[at, :] = total

    out_shape = [jax.ShapeDtypeStruct((rows, wide), BF)] * 2 + [
        jax.ShapeDtypeStruct((rows, 128), F32),
        TOKEN,
    ]
    return on_chip(
        body,
        [cot, hid, wa, wb, down, *earlier],
        out_shape,
        2 * rows * D * wide,
        "hidden_grads",
    )


def token_partials(place, gg, ug, rg, gate, up, T, e_total, *earlier):
    half, wide = gg[0].shape
    E, D, F = gate.shape
    extra = extra_rows(e_total, T, D)
    step, nb, per = T + extra, half // T, e_total * T // D

    def body(*refs):
        place_ref = refs[0]
        gg_refs, ug_refs, rg_refs = refs[1:3], refs[3:5], refs[5:7]
        gate_ref, up_ref = refs[7:9]
        near_ref, far_ref, buf = refs[9 + len(earlier) :]
        sublane = lax.broadcasted_iota(jnp.int32, (extra, T), 0)
        for side in range(2):
            for i in range(0, nb, 2):
                at = slice(i * T, (i + 2) * T)
                part = jnp.zeros((2 * T, D), F32)
                for j in range(E):
                    cols = slice(j * F, (j + 1) * F)
                    part = part + mm_nt(gg_refs[side][at, cols], gate_ref[j])
                    part = part + mm_nt(ug_refs[side][at, cols], up_ref[j])
                for b in (i, i + 1):
                    buf[...] = jnp.zeros_like(buf)
                    turned = rg_refs[side][b * T : (b + 1) * T, :].T
                    for p, third in enumerate(thirds(turned[:8, :])):
                        for j in range(E):
                            flat = (place_ref[2] * E + j) * T
                            lanes = pl.ds(pl.multiple_of(flat % D, T), T)
                            mine = jnp.broadcast_to(third[j : j + 1, :], (extra, T))
                            row = sublane == p * per + flat // D
                            buf[:, lanes] = jnp.where(row, mine, buf[:, lanes])
                    mine = part[(b - i) * T : (b - i + 1) * T]
                    if side == 0:
                        near_ref[b * step : b * step + T, :] = mine
                        near_ref[b * step + T : (b + 1) * step, :] = buf[...]
                    else:
                        far_ref[b * step : b * step + T, :] = mine.astype(BF)
                        far_ref[b * step + T : (b + 1) * step, :] = buf[...].astype(BF)

    out_shape = [
        jax.ShapeDtypeStruct((nb * step, D), F32),
        jax.ShapeDtypeStruct((nb * step, D), BF),
    ]
    return on_chip(
        body,
        [place, *gg, *ug, *rg, gate, up, *earlier],
        out_shape,
        8 * half * D * wide,
        "token_partials",
        scalars=1,
        scratch=[pltpu.VMEM((extra, D), F32)],
    )


def weight_partials(place, lhs_t, rhs, experts, n, out_rows, name, *earlier):
    r = out_rows // (n * n)
    rows = lhs_t.shape[1]
    half = rows // 2
    joined = lhs_t.shape[0] != out_rows
    width = rhs[0].shape[1] // (1 if joined else experts)
    per = n * n if joined else 0

    def body(place_ref, left_ref, *refs):
        xi, yi = place_ref[0], place_ref[1]
        outs = refs[2 + len(earlier) : -1]
        refs[-1][...] = jnp.zeros_like(refs[-1])
        for k in [*range(1, n), 0]:
            for j in range(experts):
                left = []
                for q in range(n):
                    a, b = (k, q) if j % 2 == 0 else (q, k)
                    block = j * per + ((yi + b) % n) * n + (xi + a) % n
                    left.append(left_ref[pl.ds(pl.multiple_of(block * r, r), r), :])
                left = jnp.concatenate(left, axis=0)
                cols = slice(0, width) if joined else slice(j * width, (j + 1) * width)
                part = mm(left[:, :half], refs[0][:, cols]) + mm(left[:, half:], refs[1][:, cols])
                part = part.reshape(n, r, width)
                if k:
                    outs[2 * j][k - 1] = part.astype(BF)
                else:
                    outs[2 * j + 1][...] = part

    out_shape = [
        jax.ShapeDtypeStruct((n - 1, n, r, width), BF),
        jax.ShapeDtypeStruct((n, r, width), F32),
    ] * experts + [TOKEN]
    outs = on_chip(
        body,
        [place, lhs_t, *rhs, *earlier],
        out_shape,
        2 * experts * out_rows * width * rows,
        name,
        scalars=1,
    )
    return [(outs[2 * j], outs[2 * j + 1]) for j in range(experts)], outs[-1]


def add_first(parts, got, n, name, *earlier):
    E = len(parts)
    _, r, width = parts[0][1].shape

    def body(*refs):
        ins, outs = refs[: E * n], refs[E * n + len(earlier) :]
        outs[-1][...] = jnp.zeros_like(outs[-1])
        for j in range(E):
            for q in range(n):
                total = ins[j * n][q]
                for k in range(1, n):
                    total = total + ins[j * n + k][q].astype(F32)
                out = outs[j * n + q]
                out[...] = total.astype(out.dtype)

    operands = [v for j in range(E) for v in (parts[j][1], *got[j])]
    shapes = [jax.ShapeDtypeStruct((r, width), F32 if q == 0 else BF) for q in range(n)] * E
    outs = on_chip(body, [*operands, *earlier], shapes + [TOKEN], 0, name)
    return [outs[j * n : (j + 1) * n] for j in range(E)], outs[-1]


def add_second(totals, got, n, name, *earlier):
    E = len(totals)
    r, width = totals[0][0].shape

    def body(*refs):
        ins, (out_ref, token_ref) = refs[: E * n], refs[E * n + len(earlier) :]
        token_ref[...] = jnp.zeros_like(token_ref)
        for j in range(E):
            total = ins[j * n][...]
            for k in range(1, n):
                total = total + ins[j * n + k][...].astype(F32)
            out_ref[j] = total

    operands = [v for j in range(E) for v in (totals[j][0], *got[j])]
    return on_chip(
        body,
        [*operands, *earlier],
        [jax.ShapeDtypeStruct((E, r, width), F32), TOKEN],
        0,
        name,
    )


def add_sides(place, near, far, nz, name, *earlier):
    step, D = near.shape[0] // nz, near.shape[1]

    def body(place_ref, near_ref, far_ref, *refs):
        out_ref, token_ref = refs[len(earlier) :]
        token_ref[...] = jnp.zeros_like(token_ref)
        z = place_ref[2] // 2
        for k in range(nz):
            at = slice(k * step, (k + 1) * step)
            total = near_ref[at, :] + far_ref[at, :].astype(F32)
            to = pl.multiple_of((z - k + nz) % nz * step, step)
            out_ref[pl.ds(to, step), :] = total.astype(BF)

    shapes = [jax.ShapeDtypeStruct((nz * step, D), BF), TOKEN]
    return on_chip(body, [place, near, far, *earlier], shapes, 0, name, scalars=1)


def split_sides(near, far, nz, name, *earlier):
    step, D = near.shape[0] // nz, near.shape[1]

    def body(near_ref, far_ref, *refs):
        outs = refs[len(earlier) :]
        for k in range(nz):
            at = slice(k * step, (k + 1) * step)
            total = near_ref[at, :] + far_ref[at, :].astype(F32)
            outs[k][...] = total.astype(outs[k].dtype)

    shapes = [jax.ShapeDtypeStruct((step, D), F32 if k == 0 else BF) for k in range(nz)]
    return on_chip(body, [near, far, *earlier], shapes, 0, name)


def sum_rows(own, got, name, *earlier):
    def body(*refs):
        total = refs[0][...]
        for g in refs[1 : 1 + len(got)]:
            total = total + g[...].astype(F32)
        refs[-2][...] = total.astype(BF)
        refs[-1][...] = jnp.zeros_like(refs[-1])

    shapes = [jax.ShapeDtypeStruct(own.shape, BF), TOKEN]
    return on_chip(body, [own, *got, *earlier], shapes, 0, name)


def sum_rows_and_routes(got, routes_t, nz, e_total, name):
    top, T = routes_t.shape
    step, D = got.shape[0] // nz, got.shape[1]
    per, lanes = e_total * T // D, D // T

    def body(*refs):
        routes_ref, got_ref, rows_ref, routes_out, token_ref = refs
        token_ref[...] = jnp.zeros_like(token_ref)
        total = got_ref[:step, :].astype(F32)
        for k in range(1, nz):
            total = total + got_ref[k * step : (k + 1) * step, :].astype(F32)
        rows_ref[...] = total[:T].astype(BF)
        packed = total[T:]
        packed = packed[:per] + packed[per : 2 * per] + packed[2 * per : 3 * per]
        grads = jnp.zeros((top, T), F32)
        for i in range(e_total):
            at = slice(i % lanes * T, (i % lanes + 1) * T)
            row = packed[i // lanes : i // lanes + 1, at]
            grads = jnp.where(routes_ref[...] == i, row, grads)
        routes_out[...] = grads

    shapes = [
        jax.ShapeDtypeStruct((T, D), BF),
        jax.ShapeDtypeStruct((top, T), F32),
        TOKEN,
    ]
    return on_chip(body, [routes_t, got], shapes, 0, name)


def local(tokens, routes, route_weights, gate_weight, up_weight, down_weight, cotangent):
    dp = lax.axis_size("dp")
    ne = lax.axis_size("expert")
    n = math.isqrt(dp)
    nz = ne // 2
    T, D = tokens.shape
    E, _, F = gate_weight.shape
    e_total = E * ne
    d = lax.axis_index("dp")
    e = lax.axis_index("expert")
    place = jnp.stack([d % n, d // n, e]).astype(jnp.int32)

    def swap(v):
        return lax.ppermute(v, "expert", [(i, i ^ 1) for i in range(ne)])

    def move_z(v, k):
        pairs = [(2 * z + c, 2 * ((z + k) % nz) + c) for z in range(nz) for c in range(2)]
        return lax.ppermute(v, "expert", pairs)

    def move_x(v, k):
        pairs = [(y * n + x, y * n + (x + k) % n) for y in range(n) for x in range(n)]
        return lax.ppermute(v, "dp", pairs)

    def move_y(v, k):
        pairs = [(y * n + x, ((y + k) % n) * n + x) for y in range(n) for x in range(n)]
        return lax.ppermute(v, "dp", pairs)

    def gather_near(v):
        return [v] + [move_z(v, k) for k in range(1, nz)]

    packed = pack_tokens(tokens, routes.T, route_weights.T, e_total)
    token_near = collect(gather_near(packed))
    cot_blocks = gather_near(cotangent)
    token_far = swap(token_near)
    *saved, hw_t, tok_t, out_near, out_far, forward_done = forward(
        place, token_near, token_far, gate_weight, up_weight, down_weight, T, e_total
    )
    hid, wa, wb = saved[0:2], saved[2:4], saved[4:6]
    out_far = swap(out_far)
    cot_near = collect(cot_blocks, forward_done)
    cot_far = swap(cot_near)

    def send_first(parts):
        got = []
        for j, (sent, _) in enumerate(parts):
            move = move_x if j % 2 == 0 else move_y
            got.append([move(sent[k - 1], k) for k in range(1, n)])
        return got

    def send_second(totals):
        got = []
        for j, total in enumerate(totals):
            move = move_y if j % 2 == 0 else move_x
            got.append([move(total[k], k) for k in range(1, n)])
        return got

    z_groups = [[2 * z + c for z in range(nz)] for c in range(2)]

    def send_home(parts):
        return lax.all_to_all(
            parts,
            "expert",
            split_axis=0,
            concat_axis=0,
            tiled=True,
            axis_index_groups=z_groups,
        )

    gg0, ug0, rg0, near_done = hidden_grads(cot_near, hid[0], wa[0], wb[0], down_weight)
    down_part, down_done = weight_partials(
        place, hw_t, [cot_near, cot_far], E, n, F, "down_partials", near_done
    )
    down_got = send_first(down_part)
    gg1, ug1, rg1, _ = hidden_grads(cot_far, hid[1], wa[1], wb[1], down_weight, down_done)
    gate_part, gate_done = weight_partials(place, tok_t, [gg0, gg1], E, n, D, "gate_partials")
    gate_got = send_first(gate_part)
    out_parts = split_sides(out_near, out_far, nz, "out_sides", down_done)
    out_got = [move_z(out_parts[k], -k) for k in range(1, nz)]
    down_totals, down_mid = add_first(down_part, down_got, n, "down_first", gate_done)
    tg_near, tg_far = token_partials(
        place,
        [gg0, gg1],
        [ug0, ug1],
        [rg0, rg1],
        gate_weight,
        up_weight,
        T,
        e_total,
        down_mid,
    )
    tg_far = swap(tg_far)
    layer_out, out_done = sum_rows(out_parts[0], out_got, "out_rows", tg_near[:8, :128])
    up_part, up_done = weight_partials(
        place, tok_t, [ug0, ug1], E, n, D, "up_partials", tg_near[:8, :128], out_done
    )
    up_got = send_first(up_part)
    down_got = send_second(down_totals)
    tg_parts, tg_done = add_sides(place, tg_near, tg_far, nz, "token_sides", up_done)
    tg_got = send_home(tg_parts)
    gate_totals, gate_mid = add_first(gate_part, gate_got, n, "gate_first", tg_done)
    gate_got = send_second(gate_totals)
    up_totals, up_mid = add_first(up_part, up_got, n, "up_first", gate_mid)
    up_got = send_second(up_totals)
    down_grads, down_done = add_second(down_totals, down_got, n, "down_second", up_mid)
    gate_grads, gate_done = add_second(gate_totals, gate_got, n, "gate_second", down_done)
    token_grads, route_grads_t, rows_done = sum_rows_and_routes(
        tg_got, routes.T, nz, e_total, "token_rows"
    )
    up_grads, _ = add_second(up_totals, up_got, n, "up_second", gate_done, rows_done)
    route_grads = route_grads_t.T

    return (layer_out, token_grads, route_grads, gate_grads, up_grads, down_grads)


def solution(mesh):
    rows = P(("dp", "expert"), None)
    weight = P("expert", None, None)
    grad = P("expert", "dp", None)
    return jax.shard_map(
        local,
        mesh=mesh,
        in_specs=(rows, rows, rows, weight, weight, weight, rows),
        out_specs=(rows, rows, rows, grad, grad, grad),
        check_vma=False,
    )
```

profile of v0, /device:TPU:0, one launch (start us, length us, event | category | flops | bytes accessed | tf_op | source)
XLA Modules:
  0.0 135.2 jit_solution(13885149127733326308)
XLA Ops:
  0.6 0.9 copy-done.6
  1.6 0.7 copy-done.8
  2.3 0.7 copy-done.9
  3.0 5.1 %collective-permute-start.2 = (bf16[136,1024]{1,0:T(8,128)(2,1)S(1)}, bf16[136,1024]{1,0:T(8,128)(2,1)S(1)}, u32[]{:S(2)}, u32[]{:S(2)}) collective-permute-start(bf16[136,1024]{1,0:T(8,128)(2,1)S(1)} %pack_tokens.1.refs_0_), channel_id=1, source_target_pairs={{0,6},{1,7},{2,0},{3,1},{4,2},{5,3},{6,4},{7,5},{8,14},{9,15},{10,... | collective-permute-start | bytes 835592 | tf_op jit(solution)/shard_map/ppermute | solution.py:440
  8.1 1.0 collective-permute-start
  9.1 6.1 %collective-permute-done.2.refs_3_ = bf16[136,1024]{1,0:T(8,128)(2,1)S(1)} collective-permute-done((bf16[136,1024]{1,0:T(8,128)(2,1)S(1)}, bf16[136,1024]{1,0:T(8,128)(2,1)S(1)}, u32[]{:S(2)}, u32[]{:S(2)}) %collective-permute-start.2) | collective-permute-done | bytes 278560 | tf_op jit(solution)/shard_map/ppermute | solution.py:440
  15.2 16.6 %collective-permute-done.1.refs_2_ = bf16[136,1024]{1,0:T(8,128)(2,1)S(1)} collective-permute-done((bf16[136,1024]{1,0:T(8,128)(2,1)S(1)}, bf16[136,1024]{1,0:T(8,128)(2,1)S(1)}, u32[]{:S(2)}, u32[]{:S(2)}) %collective-permute-start.1) | collective-permute-done | bytes 278560 | tf_op jit(solution)/shard_map/ppermute | solution.py:440
  31.8 0.1 collect.2.near_in
  31.9 0.1 collective-permute-start.3
  32.0 2.9 %collective-permute-start.6 = (bf16[128,1024]{1,0:T(8,128)(2,1)S(1)}, bf16[128,1024]{1,0:T(8,128)(2,1)}, u32[]{:S(2)}, u32[]{:S(2)}) collective-permute-start(bf16[128,1024]{1,0:T(8,128)(2,1)S(1)} %copy-done.7), channel_id=1, source_target_pairs={{0,4},{1,5},{2,6},{3,7},{4,0},{5,1},{6,2},{7,3},{8,12},{9,13},{10,... | collective-permute-start | bytes 786440 | tf_op jit(solution)/shard_map/ppermute | solution.py:440
  34.9 3.8 %collective-permute-start.7 = (bf16[128,1024]{1,0:T(8,128)(2,1)S(1)}, bf16[128,1024]{1,0:T(8,128)(2,1)}, u32[]{:S(2)}, u32[]{:S(2)}) collective-permute-start(bf16[128,1024]{1,0:T(8,128)(2,1)S(1)} %copy-done.7), channel_id=1, source_target_pairs={{0,6},{1,7},{2,0},{3,1},{4,2},{5,3},{6,4},{7,5},{8,14},{9,15},{10,... | collective-permute-start | bytes 786440 | tf_op jit(solution)/shard_map/ppermute | solution.py:440
  38.7 0.1 pad_add_fusion.place_ref.refs_0_
  38.8 1.6 %copy-done.1 = bf16[2,1024,512]{2,1,0:T(8,128)(2,1)S(1)} copy-done((bf16[2,1024,512]{2,1,0:T(8,128)(2,1)S(1)}, bf16[2,1024,512]{2,1,0:T(8,128)(2,1)}, u32[]{:S(2)}) %copy-start.1) | copy-done | bytes 2097176
  40.4 1.6 %copy-done.3 = bf16[2,1024,512]{2,1,0:T(8,128)(2,1)S(1)} copy-done((bf16[2,1024,512]{2,1,0:T(8,128)(2,1)S(1)}, bf16[2,1024,512]{2,1,0:T(8,128)(2,1)}, u32[]{:S(2)}) %copy-start.3) | copy-done | bytes 2097176
  42.0 10.0 %forward.1 = (bf16[512,1024]{1,0:T(8,128)(2,1)S(1)}, bf16[512,1024]{1,0:T(8,128)(2,1)S(1)}, bf16[512,1024]{1,0:T(8,128)(2,1)S(1)}, bf16[512,1024]{1,0:T(8,128)(2...) custom-call(s32[3]{0:T(128)S(1)} %pad_add_fusion.place_ref.refs_0_, ...), custom_call_target="tpu_custom_call" | custom-call | flops 10000000000 | bytes 22155276 | tf_op jit(solution)/shard_map/forward/pallas_call | solution.py:32
  52.0 1.4 %collective-permute-done.6.refs_2_ = bf16[128,1024]{1,0:T(8,128)(2,1)} collective-permute-done((bf16[128,1024]{1,0:T(8,128)(2,1)S(1)}, bf16[128,1024]{1,0:T(8,128)(2,1)}, u32[]{:S(2)}, u32[]{:S(2)}) %collective-permute-start.6) | collective-permute-done | bytes 262176 | tf_op jit(solution)/shard_map/ppermute | solution.py:440
  53.4 0.9 collective-permute-done.7.refs_3_
  54.3 1.2 collect.3.refs_0_
  55.5 0.1 collective-permute-start.8
  55.6 0.5 collective-permute-start.4
  56.1 1.8 %hidden_grads.2 = (bf16[512,1024]{1,0:T(8,128)(2,1)S(1)}, bf16[512,1024]{1,0:T(8,128)(2,1)S(1)}, f32[512,128]{1,0:T(8,128)S(1)}, f32[8,128]{1,0:T(8,128)S(1)}) custom-call(bf16[512,1024]{1,0:T(8,128)(2,1)S(1)} %collect.3.refs_0_, bf16[512,1024]{1,0:T(8,128)(2,1)S(1)} %get-tuple-element.76.refs_1_, bf16[512,1024]{1,0:T(8,128)(2,1)S(1)} %get-tuple-element.77.refs_2_, ...), custom_call_target="tpu_custom_call" | custom-call | flops 10000000000 | bytes 8654848 | tf_op jit(solution)/shard_map/hidden_grads/pallas_call | solution.py:32
  57.9 0.3 collective-permute-done.8.refs_1_.refs_0_
  58.2 2.9 %down_partials.1 = (bf16[1,2,128,1024]{3,2,1,0:T(8,128)(2,1)S(1)}, f32[2,128,1024]{2,1,0:T(8,128)S(1)}, bf16[1,2,128,1024]{3,2,1,0:T(8,128)(2,1)S(1)}, f32[2,128,1024]{2,1,0:T(8,128)S(1)}, f32[8,128]{1,0:T(8,128)S(1)}) custom-call(s32[3]{0:T(128)S(1)} %pad_add_fusion.place_ref.refs_0_, bf16[1024,1024]{1,0:T(8,128)(2,1)S(1)} %get-tuple-element.74.left_ref, ...), custom_call_target="tpu_custom_call" | custom-call | flops 10000000000 | bytes 7348236 | tf_op jit(solution)/shard_map/down_partials/pallas_call | solution.py:32
  61.1 1.6 %collective-permute-start.12 = (bf16[2,128,1024]{2,1,0:T(8,128)(2,1)S(1)}, bf16[2,128,1024]{2,1,0:T(8,128)(2,1)S(1)}, u32[]{:S(2)}, u32[]{:S(2)}) collective-permute-start(bf16[2,128,1024]{2,1,0:T(8,128)(2,1)S(1)} %bitcast.19), channel_id=1, source_target_pairs={{0,8},{8,0},{16,24},{24,16},{1,9},{9,1},{17,25},{25,17},{2,10},{10... | collective-permute-start | bytes 1572872 | tf_op jit(solution)/shard_map/ppermute | solution.py:444
  62.7 1.5 %collective-permute-start.13 = (bf16[2,128,1024]{2,1,0:T(8,128)(2,1)S(1)}, bf16[2,128,1024]{2,1,0:T(8,128)(2,1)S(1)}, u32[]{:S(2)}, u32[]{:S(2)}) collective-permute-start(bf16[2,128,1024]{2,1,0:T(8,128)(2,1)S(1)} %bitcast.18), channel_id=1, source_target_pairs={{0,16},{8,24},{16,0},{24,8},{1,17},{9,25},{17,1},{25,9},{2,18},{10... | collective-permute-start | bytes 1572872 | tf_op jit(solution)/shard_map/ppermute | solution.py:448
  64.2 0.2 out_sides.1
  64.4 2.6 %collective-permute-start.9 = (bf16[128,1024]{1,0:T(8,128)(2,1)S(1)}, bf16[128,1024]{1,0:T(8,128)(2,1)S(1)}, u32[]{:S(2)}, u32[]{:S(2)}) collective-permute-start(bf16[128,1024]{1,0:T(8,128)(2,1)S(1)} %get-tuple-element.82), channel_id=1, source_target_pairs={{0,6},{1,7},{2,0},{3,1},{4,2},{5,3},{6,4},{7,5},{8,14},{9,15},{10,... | collective-permute-start | bytes 786440 | tf_op jit(solution)/shard_map/ppermute | solution.py:440
  67.0 4.0 %collective-permute-start.10 = (bf16[128,1024]{1,0:T(8,128)(2,1)S(1)}, bf16[128,1024]{1,0:T(8,128)(2,1)S(1)}, u32[]{:S(2)}, u32[]{:S(2)}) collective-permute-start(bf16[128,1024]{1,0:T(8,128)(2,1)S(1)} %get-tuple-element.83), channel_id=1, source_target_pairs={{0,4},{1,5},{2,6},{3,7},{4,0},{5,1},{6,2},{7,3},{8,12},{9,13},{10,... | collective-permute-start | bytes 786440 | tf_op jit(solution)/shard_map/ppermute | solution.py:440
  71.0 2.3 %hidden_grads.3 = (bf16[512,1024]{1,0:T(8,128)(2,1)S(1)}, bf16[512,1024]{1,0:T(8,128)(2,1)S(1)}, f32[512,128]{1,0:T(8,128)S(1)}, f32[8,128]{1,0:T(8,128)}) custom-call(bf16[512,1024]{1,0:T(8,128)(2,1)S(1)} %collective-permute-done.8.refs_1_.refs_0_, bf16[512,1024]{1,0:T(8,128)(2,1)S(1)} %get-tuple-element.86.refs_1_, ...), custom_call_target="tpu_custom_call" | custom-call | flops 10000000000 | bytes 8658944 | tf_op jit(solution)/shard_map/hidden_grads/pallas_call | solution.py:32
  73.3 2.9 %gate_partials.1 = (bf16[1,2,256,512]{3,2,1,0:T(8,128)(2,1)S(1)}, f32[2,256,512]{2,1,0:T(8,128)S(1)}, bf16[1,2,256,512]{3,2,1,0:T(8,128)(2,1)S(1)}, f32[2,256,512]{2,1,0:T(8,128)S(1)}, f32[8,128]{1,0:T(8,128)S(1)}) custom-call(s32[3]{0:T(128)S(1)} %pad_add_fusion.place_ref.refs_0_, bf16[1024,1024]{1,0:T(8,128)(2,1)S(1)} %get-tuple-element.98.left_ref, ...), custom_call_target="tpu_custom_call" | custom-call | flops 10000000000 | bytes 7344140 | tf_op jit(solution)/shard_map/gate_partials/pallas_call | solution.py:32
  76.2 1.0 copy-done.17
  77.2 0.5 collective-permute-start.15
  77.7 0.5 collective-permute-start.16
  78.3 0.9 down_first.1
  79.1 0.8 copy-done.19
  79.9 0.8 copy-done.21
  80.8 5.1 %token_partials.1 = (f32[544,1024]{1,0:T(8,128)S(1)}, bf16[544,1024]{1,0:T(8,128)(2,1)S(1)}) custom-call(s32[3]{0:T(128)S(1)} %pad_add_fusion.place_ref.refs_0_, bf16[512,1024]{1,0:T(8,128)(2,1)S(1)} %get-tuple-element.85.refs_0_.refs_1_, bf16[512,1024]{1,0:T(8,128)(2,1)S(1)} %get-tuple-element.89.refs_1_.refs_2_, ...), custom_call_target="tpu_custom_call" | custom-call | flops 10000000000 | bytes 12259340 | tf_op jit(solution)/shard_map/token_partials/pallas_call | solution.py:32
  85.9 1.6 %collective-permute-start.19 = (bf16[128,1024]{1,0:T(8,128)(2,1)}, bf16[128,1024]{1,0:T(8,128)(2,1)}, u32[]{:S(2)}, u32[]{:S(2)}) collective-permute-start(bf16[128,1024]{1,0:T(8,128)(2,1)} %get-tuple-element.119), channel_id=1, source_target_pairs={{0,16},{8,24},{16,0},{24,8},{1,17},{9,25},{17,1},{25,9},{2,18},{10... | collective-permute-start | bytes 786440 | tf_op jit(solution)/shard_map/ppermute | solution.py:448
  87.5 6.1 %collective-permute-done.10.refs_2_ = bf16[128,1024]{1,0:T(8,128)(2,1)S(1)} collective-permute-done((bf16[128,1024]{1,0:T(8,128)(2,1)S(1)}, bf16[128,1024]{1,0:T(8,128)(2,1)S(1)}, u32[]{:S(2)}, u32[]{:S(2)}) %collective-permute-start.10) | collective-permute-done | bytes 262176 | tf_op jit(solution)/shard_map/ppermute | solution.py:440
  93.6 0.5 collective-permute-start.20
  94.1 0.8 out_rows.1
  95.0 3.1 %up_partials.1 = (bf16[1,2,256,512]{3,2,1,0:T(8,128)(2,1)}, f32[2,256,512]{2,1,0:T(8,128)S(1)}, bf16[1,2,256,512]{3,2,1,0:T(8,128)(2,1)S(1)}, f32[2,256,512]{2,1,0:T(8,128)S(1)}, f32[8,128]{1,0:T(8,128)S(1)}) custom-call(s32[3]{0:T(128)S(1)} %pad_add_fusion.place_ref.refs_0_, bf16[1024,1024]{1,0:T(8,128)(2,1)S(1)} %get-tuple-element.98.left_ref, ...), custom_call_target="tpu_custom_call" | custom-call | flops 10000000000 | bytes 7352332 | tf_op jit(solution)/shard_map/up_partials/pallas_call | solution.py:32
  98.1 1.6 %collective-permute-start.21 = (bf16[2,256,512]{2,1,0:T(8,128)(2,1)}, bf16[2,256,512]{2,1,0:T(8,128)(2,1)}, u32[]{:S(2)}, u32[]{:S(2)}) collective-permute-start(bf16[2,256,512]{2,1,0:T(8,128)(2,1)} %bitcast.12), channel_id=1, source_target_pairs={{0,8},{8,0},{16,24},{24,16},{1,9},{9,1},{17,25},{25,17},{2,10},{10... | collective-permute-start | bytes 1572872 | tf_op jit(solution)/shard_map/ppermute | solution.py:444
  99.6 1.8 %token_sides.1 = (bf16[544,1024]{1,0:T(8,128)(2,1)}, f32[8,128]{1,0:T(8,128)S(1)}) custom-call(s32[3]{0:T(128)S(1)} %pad_add_fusion.place_ref.refs_0_, f32[544,1024]{1,0:T(8,128)S(1)} %get-tuple-element.101.near_ref, bf16[544,1024]{1,0:T(8,128)(2,1)S(1)} %collective-permute-done.14.far_ref, f32[8,128]{1,0:T(8,128)S(1)} %get-tuple-element.105.refs_0_), custom_call_target="tpu_custom_call" | custom-call | flops 10000000000 | bytes 4464652 | tf_op jit(solution)/shard_map/token_sides/pallas_call | solution.py:32
  101.5 3.5 %all-to-all-start = ((bf16[4,136,1024]{2,1,0:T(8,128)(2,1)}), bf16[4,136,1024]{2,1,0:T(8,128)(2,1)S(1)}, u32[]{:S(2)}, u32[]{:S(2)}) async-start(bf16[4,136,1024]{2,1,0:T(8,128)(2,1)} %bitcast.7), calls=%async_computation | async-start | bytes 2228224 | tf_op jit(solution)/shard_map/all_to_all | solution.py:482
  105.0 0.6 collective-permute-start.22
  105.6 1.2 copy-done.16
  106.8 1.2 copy-done.18
  108.1 0.2 gate_first.1
  108.3 1.6 %collective-permute-start.17 = (bf16[256,512]{1,0:T(8,128)(2,1)S(1)}, bf16[256,512]{1,0:T(8,128)(2,1)S(1)}, u32[]{:S(2)}, u32[]{:S(2)}) collective-permute-start(bf16[256,512]{1,0:T(8,128)(2,1)S(1)} %get-tuple-element.115), channel_id=1, source_target_pairs={{0,16},{8,24},{16,0},{24,8},{1,17},{9,25},{17,1},{25,9},{2,18},{10... | collective-permute-start | bytes 786440 | tf_op jit(solution)/shard_map/ppermute | solution.py:448
  109.9 2.9 %collective-permute-done.21.refs_1_ = bf16[2,256,512]{2,1,0:T(8,128)(2,1)} collective-permute-done((bf16[2,256,512]{2,1,0:T(8,128)(2,1)}, bf16[2,256,512]{2,1,0:T(8,128)(2,1)}, u32[]{:S(2)}, u32[]{:S(2)}) %collective-permute-start.21) | collective-permute-done | bytes 524320 | tf_op jit(solution)/shard_map/ppermute | solution.py:444
  112.8 1.5 %collective-permute-start.18 = (bf16[256,512]{1,0:T(8,128)(2,1)S(1)}, bf16[256,512]{1,0:T(8,128)(2,1)S(1)}, u32[]{:S(2)}, u32[]{:S(2)}) collective-permute-start(bf16[256,512]{1,0:T(8,128)(2,1)S(1)} %get-tuple-element.117), channel_id=1, source_target_pairs={{0,8},{8,0},{16,24},{24,16},{1,9},{9,1},{17,25},{25,17},{2,10},{10... | collective-permute-start | bytes 786440 | tf_op jit(solution)/shard_map/ppermute | solution.py:444
  114.3 5.8 %collective-permute-done.22.refs_3_ = bf16[2,256,512]{2,1,0:T(8,128)(2,1)S(1)} collective-permute-done((bf16[2,256,512]{2,1,0:T(8,128)(2,1)}, bf16[2,256,512]{2,1,0:T(8,128)(2,1)S(1)}, u32[]{:S(2)}, u32[]{:S(2)}) %collective-permute-start.22) | collective-permute-done | bytes 524320 | tf_op jit(solution)/shard_map/ppermute | solution.py:448
  120.1 1.3 up_first.1
  121.4 0.6 collective-permute-start.23
  122.0 0.5 collective-permute-start.24
  122.6 2.1 %down_second.1 = (f32[2,128,1024]{2,1,0:T(8,128)}, f32[8,128]{1,0:T(8,128)S(1)}) custom-call(f32[128,1024]{1,0:T(8,128)S(1)} %copy-done.20, bf16[128,1024]{1,0:T(8,128)(2,1)} %collective-permute-done.19.refs_1_, f32[128,1024]{1,0:T(8,128)S(1)} %copy-done.22, bf16[128,1024]{1,0:T(8,128)(2,1)} %collective-permute-done.20.refs_3_, ...), custom_call_target="tpu_custom_call" | custom-call | flops 10000000000 | bytes 2629632 | tf_op jit(solution)/shard_map/down_second/pallas_call | solution.py:32
  124.7 1.0 collective-permute-done.17.refs_1_
  125.7 1.1 gate_second.1
  126.8 6.0 %all-to-all-done = bf16[4,136,1024]{2,1,0:T(8,128)(2,1)S(1)} async-done(((bf16[4,136,1024]{2,1,0:T(8,128)(2,1)}), bf16[4,136,1024]{2,1,0:T(8,128)(2,1)S(1)}, u32[]{:S(2)}, u32[]{:S(2)}) %all-to-all-start) | async-done | bytes 1114144 | tf_op jit(solution)/shard_map/all_to_all | solution.py:482
  132.8 0.8 token_rows.1
  133.6 0.2 copy-done.24
  133.9 0.2 copy-done.26
  134.1 1.1 up_second.1
  (64 shorter events, 0.2 us)
Async XLA Ops:
  0.6 1.0 copy-start.6
  1.6 0.7 copy-start.8
  2.3 0.7 copy-start.9
  3.0 29.0 %copy-start.7 = (bf16[128,1024]{1,0:T(8,128)(2,1)S(1)}, bf16[128,1024]{1,0:T(8,128)(2,1)}, u32[]{:S(2)}) copy-start(bf16[128,1024]{1,0:T(8,128)(2,1)} %refs_0_.1) | copy-start | bytes 786436
  3.0 35.8 %copy-start = (bf16[2,512,1024]{2,1,0:T(8,128)(2,1)S(1)}, bf16[2,512,1024]{2,1,0:T(8,128)(2,1)}, u32[]{:S(2)}) copy-start(bf16[2,512,1024]{2,1,0:T(8,128)(2,1)} %refs_4_.3) | copy-start | bytes 6291460
  3.0 12.2 %collective-permute-start.2 = (bf16[136,1024]{1,0:T(8,128)(2,1)S(1)}, bf16[136,1024]{1,0:T(8,128)(2,1)S(1)}, u32[]{:S(2)}, u32[]{:S(2)}) collective-permute-start(bf16[136,1024]{1,0:T(8,128)(2,1)S(1)} %pack_tokens.1.refs_0_), channel_id=1, source_target_pairs={{0,6},{1,7},{2,0},{3,1},{4,2},{5,3},{6,4},{7,5},{8,14},{9,15},{10,... | collective-permute-start | bytes 835592 | tf_op jit(solution)/shard_map/ppermute | solution.py:440
  8.1 23.7 %collective-permute-start.1 = (bf16[136,1024]{1,0:T(8,128)(2,1)S(1)}, bf16[136,1024]{1,0:T(8,128)(2,1)S(1)}, u32[]{:S(2)}, u32[]{:S(2)}) collective-permute-start(bf16[136,1024]{1,0:T(8,128)(2,1)S(1)} %pack_tokens.1.refs_0_), channel_id=1, source_target_pairs={{0,4},{1,5},{2,6},{3,7},{4,0},{5,1},{6,2},{7,3},{8,12},{9,13},{10,... | collective-permute-start | bytes 835592 | tf_op jit(solution)/shard_map/ppermute | solution.py:440
  8.1 23.7 %collective-permute-start = (bf16[136,1024]{1,0:T(8,128)(2,1)S(1)}, bf16[136,1024]{1,0:T(8,128)(2,1)S(1)}, u32[]{:S(2)}, u32[]{:S(2)}) collective-permute-start(bf16[136,1024]{1,0:T(8,128)(2,1)S(1)} %pack_tokens.1.refs_0_), channel_id=1, source_target_pairs={{0,2},{1,3},{2,4},{3,5},{4,6},{5,7},{6,0},{7,1},{8,10},{9,11},{10,... | collective-permute-start | bytes 835592 | tf_op jit(solution)/shard_map/ppermute | solution.py:440
  31.9 6.9 %collective-permute-start.3 = (bf16[544,1024]{1,0:T(8,128)(2,1)S(1)}, bf16[544,1024]{1,0:T(8,128)(2,1)}, u32[]{:S(2)}, u32[]{:S(2)}) collective-permute-start(bf16[544,1024]{1,0:T(8,128)(2,1)S(1)} %collect.2.near_in), channel_id=1, source_target_pairs={{0,1},{1,0},{2,3},{3,2},{4,5},{5,4},{6,7},{7,6},{8,9},{9,8},{10,11... | collective-permute-start | bytes 3342344 | tf_op jit(solution)/shard_map/ppermute | solution.py:436
  32.0 21.4 %collective-permute-start.6 = (bf16[128,1024]{1,0:T(8,128)(2,1)S(1)}, bf16[128,1024]{1,0:T(8,128)(2,1)}, u32[]{:S(2)}, u32[]{:S(2)}) collective-permute-start(bf16[128,1024]{1,0:T(8,128)(2,1)S(1)} %copy-done.7), channel_id=1, source_target_pairs={{0,4},{1,5},{2,6},{3,7},{4,0},{5,1},{6,2},{7,3},{8,12},{9,13},{10,... | collective-permute-start | bytes 786440 | tf_op jit(solution)/shard_map/ppermute | solution.py:440
  34.9 18.6 %collective-permute-start.5 = (bf16[128,1024]{1,0:T(8,128)(2,1)S(1)}, bf16[128,1024]{1,0:T(8,128)(2,1)}, u32[]{:S(2)}, u32[]{:S(2)}) collective-permute-start(bf16[128,1024]{1,0:T(8,128)(2,1)S(1)} %copy-done.7), channel_id=1, source_target_pairs={{0,2},{1,3},{2,4},{3,5},{4,6},{5,7},{6,0},{7,1},{8,10},{9,11},{10,... | collective-permute-start | bytes 786440 | tf_op jit(solution)/shard_map/ppermute | solution.py:440
  34.9 19.4 %collective-permute-start.7 = (bf16[128,1024]{1,0:T(8,128)(2,1)S(1)}, bf16[128,1024]{1,0:T(8,128)(2,1)}, u32[]{:S(2)}, u32[]{:S(2)}) collective-permute-start(bf16[128,1024]{1,0:T(8,128)(2,1)S(1)} %copy-done.7), channel_id=1, source_target_pairs={{0,6},{1,7},{2,0},{3,1},{4,2},{5,3},{6,4},{7,5},{8,14},{9,15},{10,... | collective-permute-start | bytes 786440 | tf_op jit(solution)/shard_map/ppermute | solution.py:440
  38.8 1.6 %copy-start.1 = (bf16[2,1024,512]{2,1,0:T(8,128)(2,1)S(1)}, bf16[2,1024,512]{2,1,0:T(8,128)(2,1)}, u32[]{:S(2)}) copy-start(bf16[2,1024,512]{2,1,0:T(8,128)(2,1)} %refs_7_.1) | copy-start | bytes 6291460
  40.4 1.6 %copy-start.3 = (bf16[2,1024,512]{2,1,0:T(8,128)(2,1)S(1)}, bf16[2,1024,512]{2,1,0:T(8,128)(2,1)}, u32[]{:S(2)}) copy-start(bf16[2,1024,512]{2,1,0:T(8,128)(2,1)} %refs_8_.1) | copy-start | bytes 6291460
  55.5 2.7 %collective-permute-start.8 = (bf16[512,1024]{1,0:T(8,128)(2,1)S(1)}, bf16[512,1024]{1,0:T(8,128)(2,1)S(1)}, u32[]{:S(2)}, u32[]{:S(2)}) collective-permute-start(bf16[512,1024]{1,0:T(8,128)(2,1)S(1)} %collect.3.refs_0_), channel_id=1, source_target_pairs={{0,1},{1,0},{2,3},{3,2},{4,5},{5,4},{6,7},{7,6},{8,9},{9,8},{10,11... | collective-permute-start | bytes 3145736 | tf_op jit(solution)/shard_map/ppermute | solution.py:436
  55.6 8.6 %collective-permute-start.4 = (bf16[512,1024]{1,0:T(8,128)(2,1)S(1)}, bf16[512,1024]{1,0:T(8,128)(2,1)S(1)}, u32[]{:S(2)}, u32[]{:S(2)}) collective-permute-start(bf16[512,1024]{1,0:T(8,128)(2,1)S(1)} %get-tuple-element.73), channel_id=1, source_target_pairs={{0,1},{1,0},{2,3},{3,2},{4,5},{5,4},{6,7},{7,6},{8,9},{9,8},{10,11... | collective-permute-start | bytes 3145736 | tf_op jit(solution)/shard_map/ppermute | solution.py:436
  61.1 16.1 %collective-permute-start.12 = (bf16[2,128,1024]{2,1,0:T(8,128)(2,1)S(1)}, bf16[2,128,1024]{2,1,0:T(8,128)(2,1)S(1)}, u32[]{:S(2)}, u32[]{:S(2)}) collective-permute-start(bf16[2,128,1024]{2,1,0:T(8,128)(2,1)S(1)} %bitcast.19), channel_id=1, source_target_pairs={{0,8},{8,0},{16,24},{24,16},{1,9},{9,1},{17,25},{25,17},{2,10},{10... | collective-permute-start | bytes 1572872 | tf_op jit(solution)/shard_map/ppermute | solution.py:444
  62.7 15.0 %collective-permute-start.13 = (bf16[2,128,1024]{2,1,0:T(8,128)(2,1)S(1)}, bf16[2,128,1024]{2,1,0:T(8,128)(2,1)S(1)}, u32[]{:S(2)}, u32[]{:S(2)}) collective-permute-start(bf16[2,128,1024]{2,1,0:T(8,128)(2,1)S(1)} %bitcast.18), channel_id=1, source_target_pairs={{0,16},{8,24},{16,0},{24,8},{1,17},{9,25},{17,1},{25,9},{2,18},{10... | collective-permute-start | bytes 1572872 | tf_op jit(solution)/shard_map/ppermute | solution.py:448
  64.4 21.4 %collective-permute-start.9 = (bf16[128,1024]{1,0:T(8,128)(2,1)S(1)}, bf16[128,1024]{1,0:T(8,128)(2,1)S(1)}, u32[]{:S(2)}, u32[]{:S(2)}) collective-permute-start(bf16[128,1024]{1,0:T(8,128)(2,1)S(1)} %get-tuple-element.82), channel_id=1, source_target_pairs={{0,6},{1,7},{2,0},{3,1},{4,2},{5,3},{6,4},{7,5},{8,14},{9,15},{10,... | collective-permute-start | bytes 786440 | tf_op jit(solution)/shard_map/ppermute | solution.py:440
  67.0 26.6 %collective-permute-start.10 = (bf16[128,1024]{1,0:T(8,128)(2,1)S(1)}, bf16[128,1024]{1,0:T(8,128)(2,1)S(1)}, u32[]{:S(2)}, u32[]{:S(2)}) collective-permute-start(bf16[128,1024]{1,0:T(8,128)(2,1)S(1)} %get-tuple-element.83), channel_id=1, source_target_pairs={{0,4},{1,5},{2,6},{3,7},{4,0},{5,1},{6,2},{7,3},{8,12},{9,13},{10,... | collective-permute-start | bytes 786440 | tf_op jit(solution)/shard_map/ppermute | solution.py:440
  71.0 23.2 %collective-permute-start.11 = (bf16[128,1024]{1,0:T(8,128)(2,1)S(1)}, bf16[128,1024]{1,0:T(8,128)(2,1)S(1)}, u32[]{:S(2)}, u32[]{:S(2)}) collective-permute-start(bf16[128,1024]{1,0:T(8,128)(2,1)S(1)} %get-tuple-element.84), channel_id=1, source_target_pairs={{0,2},{1,3},{2,4},{3,5},{4,6},{5,7},{6,0},{7,1},{8,10},{9,11},{10,... | collective-permute-start | bytes 786440 | tf_op jit(solution)/shard_map/ppermute | solution.py:440
  76.2 1.0 copy-start.17
  77.2 1.9 %copy-start.15 = (f32[2,256,512]{2,1,0:T(8,128)}, f32[2,256,512]{2,1,0:T(8,128)S(1)}, u32[]{:S(2)}) copy-start(f32[2,256,512]{2,1,0:T(8,128)S(1)} %get-tuple-element.109.refs_0_) | copy-start | bytes 3145732
  77.2 27.8 %collective-permute-start.15 = (bf16[2,256,512]{2,1,0:T(8,128)(2,1)S(1)}, bf16[2,256,512]{2,1,0:T(8,128)(2,1)S(1)}, u32[]{:S(2)}, u32[]{:S(2)}) collective-permute-start(bf16[2,256,512]{2,1,0:T(8,128)(2,1)S(1)} %bitcast.16), channel_id=1, source_target_pairs={{0,8},{8,0},{16,24},{24,16},{1,9},{9,1},{17,25},{25,17},{2,10},{10... | collective-permute-start | bytes 1572872 | tf_op jit(solution)/shard_map/ppermute | solution.py:444
  77.7 27.9 %collective-permute-start.16 = (bf16[2,256,512]{2,1,0:T(8,128)(2,1)S(1)}, bf16[2,256,512]{2,1,0:T(8,128)(2,1)S(1)}, u32[]{:S(2)}, u32[]{:S(2)}) collective-permute-start(bf16[2,256,512]{2,1,0:T(8,128)(2,1)S(1)} %bitcast.15), channel_id=1, source_target_pairs={{0,16},{8,24},{16,0},{24,8},{1,17},{9,25},{17,1},{25,9},{2,18},{10... | collective-permute-start | bytes 1572872 | tf_op jit(solution)/shard_map/ppermute | solution.py:448
  78.2 2.5 %copy-start.2 = (bf16[2,1024,512]{2,1,0:T(8,128)(2,1)S(1)}, bf16[2,1024,512]{2,1,0:T(8,128)(2,1)}, u32[]{:S(2)}) copy-start(bf16[2,1024,512]{2,1,0:T(8,128)(2,1)} %refs_7_.1) | copy-start | bytes 6291460
  78.3 2.5 %copy-start.4 = (bf16[2,1024,512]{2,1,0:T(8,128)(2,1)S(1)}, bf16[2,1024,512]{2,1,0:T(8,128)(2,1)}, u32[]{:S(2)}) copy-start(bf16[2,1024,512]{2,1,0:T(8,128)(2,1)} %refs_8_.1) | copy-start | bytes 6291460
  79.1 0.8 copy-start.19
  79.9 0.8 copy-start.21
  85.9 36.1 %collective-permute-start.19 = (bf16[128,1024]{1,0:T(8,128)(2,1)}, bf16[128,1024]{1,0:T(8,128)(2,1)}, u32[]{:S(2)}, u32[]{:S(2)}) collective-permute-start(bf16[128,1024]{1,0:T(8,128)(2,1)} %get-tuple-element.119), channel_id=1, source_target_pairs={{0,16},{8,24},{16,0},{24,8},{1,17},{9,25},{17,1},{25,9},{2,18},{10... | collective-permute-start | bytes 786440 | tf_op jit(solution)/shard_map/ppermute | solution.py:448
  93.6 29.0 %collective-permute-start.20 = (bf16[128,1024]{1,0:T(8,128)(2,1)S(1)}, bf16[128,1024]{1,0:T(8,128)(2,1)}, u32[]{:S(2)}, u32[]{:S(2)}) collective-permute-start(bf16[128,1024]{1,0:T(8,128)(2,1)S(1)} %get-tuple-element.121), channel_id=1, source_target_pairs={{0,8},{8,0},{16,24},{24,16},{1,9},{9,1},{17,25},{25,17},{2,10},{10... | collective-permute-start | bytes 786440 | tf_op jit(solution)/shard_map/ppermute | solution.py:444
  94.1 4.0 %collective-permute-start.14 = (bf16[544,1024]{1,0:T(8,128)(2,1)S(1)}, bf16[544,1024]{1,0:T(8,128)(2,1)S(1)}, u32[]{:S(2)}, u32[]{:S(2)}) collective-permute-start(bf16[544,1024]{1,0:T(8,128)(2,1)S(1)} %get-tuple-element.103), channel_id=1, source_target_pairs={{0,1},{1,0},{2,3},{3,2},{4,5},{5,4},{6,7},{7,6},{8,9},{9,8},{10,11... | collective-permute-start | bytes 3342344 | tf_op jit(solution)/shard_map/ppermute | solution.py:436
  98.1 3.4 %copy-start.5 = (bf16[1,2,256,512]{3,2,1,0:T(8,128)(2,1)}, bf16[1,2,256,512]{3,2,1,0:T(8,128)(2,1)S(1)}, u32[]{:S(2)}) copy-start(bf16[1,2,256,512]{3,2,1,0:T(8,128)(2,1)S(1)} %get-tuple-element.125) | copy-start | bytes 1572868
  98.1 3.4 %copy-start.11 = (f32[2,256,512]{2,1,0:T(8,128)}, f32[2,256,512]{2,1,0:T(8,128)S(1)}, u32[]{:S(2)}) copy-start(f32[2,256,512]{2,1,0:T(8,128)S(1)} %get-tuple-element.122.refs_0_) | copy-start | bytes 3145732
  98.1 3.4 %copy-start.13 = (f32[2,256,512]{2,1,0:T(8,128)}, f32[2,256,512]{2,1,0:T(8,128)S(1)}, u32[]{:S(2)}) copy-start(f32[2,256,512]{2,1,0:T(8,128)S(1)} %get-tuple-element.124.refs_2_) | copy-start | bytes 3145732
  98.1 14.7 %collective-permute-start.21 = (bf16[2,256,512]{2,1,0:T(8,128)(2,1)}, bf16[2,256,512]{2,1,0:T(8,128)(2,1)}, u32[]{:S(2)}, u32[]{:S(2)}) collective-permute-start(bf16[2,256,512]{2,1,0:T(8,128)(2,1)} %bitcast.12), channel_id=1, source_target_pairs={{0,8},{8,0},{16,24},{24,16},{1,9},{9,1},{17,25},{25,17},{2,10},{10... | collective-permute-start | bytes 1572872 | tf_op jit(solution)/shard_map/ppermute | solution.py:444
  101.5 31.3 %all-to-all-start = ((bf16[4,136,1024]{2,1,0:T(8,128)(2,1)}), bf16[4,136,1024]{2,1,0:T(8,128)(2,1)S(1)}, u32[]{:S(2)}, u32[]{:S(2)}) async-start(bf16[4,136,1024]{2,1,0:T(8,128)(2,1)} %bitcast.7), calls=%async_computation | async-start | bytes 2228224 | tf_op jit(solution)/shard_map/all_to_all | solution.py:482
  105.0 15.0 %collective-permute-start.22 = (bf16[2,256,512]{2,1,0:T(8,128)(2,1)}, bf16[2,256,512]{2,1,0:T(8,128)(2,1)S(1)}, u32[]{:S(2)}, u32[]{:S(2)}) collective-permute-start(bf16[2,256,512]{2,1,0:T(8,128)(2,1)} %bitcast.17), channel_id=1, source_target_pairs={{0,16},{8,24},{16,0},{24,8},{1,17},{9,25},{17,1},{25,9},{2,18},{10... | collective-permute-start | bytes 1572872 | tf_op jit(solution)/shard_map/ppermute | solution.py:448
  105.6 1.2 copy-start.16
  106.8 1.2 copy-start.18
  108.1 12.0 %copy-start.12 = (f32[2,256,512]{2,1,0:T(8,128)S(1)}, f32[2,256,512]{2,1,0:T(8,128)}, u32[]{:S(2)}) copy-start(f32[2,256,512]{2,1,0:T(8,128)} %copy-done.11) | copy-start | bytes 3145732
  108.1 12.0 %copy-start.14 = (f32[2,256,512]{2,1,0:T(8,128)S(1)}, f32[2,256,512]{2,1,0:T(8,128)}, u32[]{:S(2)}) copy-start(f32[2,256,512]{2,1,0:T(8,128)} %copy-done.13) | copy-start | bytes 3145732
  108.3 17.4 %collective-permute-start.17 = (bf16[256,512]{1,0:T(8,128)(2,1)S(1)}, bf16[256,512]{1,0:T(8,128)(2,1)S(1)}, u32[]{:S(2)}, u32[]{:S(2)}) collective-permute-start(bf16[256,512]{1,0:T(8,128)(2,1)S(1)} %get-tuple-element.115), channel_id=1, source_target_pairs={{0,16},{8,24},{16,0},{24,8},{1,17},{9,25},{17,1},{25,9},{2,18},{10... | collective-permute-start | bytes 786440 | tf_op jit(solution)/shard_map/ppermute | solution.py:448
  112.8 12.9 %collective-permute-start.18 = (bf16[256,512]{1,0:T(8,128)(2,1)S(1)}, bf16[256,512]{1,0:T(8,128)(2,1)S(1)}, u32[]{:S(2)}, u32[]{:S(2)}) collective-permute-start(bf16[256,512]{1,0:T(8,128)(2,1)S(1)} %get-tuple-element.117), channel_id=1, source_target_pairs={{0,8},{8,0},{16,24},{24,16},{1,9},{9,1},{17,25},{25,17},{2,10},{10... | collective-permute-start | bytes 786440 | tf_op jit(solution)/shard_map/ppermute | solution.py:444
  120.1 2.5 %copy-start.20 = (f32[128,1024]{1,0:T(8,128)S(1)}, f32[128,1024]{1,0:T(8,128)}, u32[]{:S(2)}) copy-start(f32[128,1024]{1,0:T(8,128)} %copy-done.19) | copy-start | bytes 1572868
  120.1 2.5 %copy-start.22 = (f32[128,1024]{1,0:T(8,128)S(1)}, f32[128,1024]{1,0:T(8,128)}, u32[]{:S(2)}) copy-start(f32[128,1024]{1,0:T(8,128)} %copy-done.21) | copy-start | bytes 1572868
  121.4 3.2 %copy-start.23 = (f32[256,512]{1,0:T(8,128)}, f32[256,512]{1,0:T(8,128)S(1)}, u32[]{:S(2)}) copy-start(f32[256,512]{1,0:T(8,128)S(1)} %get-tuple-element.130.refs_0_) | copy-start | bytes 1572868
  121.4 3.2 %copy-start.25 = (f32[256,512]{1,0:T(8,128)}, f32[256,512]{1,0:T(8,128)S(1)}, u32[]{:S(2)}) copy-start(f32[256,512]{1,0:T(8,128)S(1)} %get-tuple-element.132.refs_2_) | copy-start | bytes 1572868
  121.4 12.2 %collective-permute-start.23 = (bf16[256,512]{1,0:T(8,128)(2,1)S(1)}, bf16[256,512]{1,0:T(8,128)(2,1)S(1)}, u32[]{:S(2)}, u32[]{:S(2)}) collective-permute-start(bf16[256,512]{1,0:T(8,128)(2,1)S(1)} %get-tuple-element.131), channel_id=1, source_target_pairs={{0,16},{8,24},{16,0},{24,8},{1,17},{9,25},{17,1},{25,9},{2,18},{10... | collective-permute-start | bytes 786440 | tf_op jit(solution)/shard_map/ppermute | solution.py:448
  122.0 11.6 %collective-permute-start.24 = (bf16[256,512]{1,0:T(8,128)(2,1)S(1)}, bf16[256,512]{1,0:T(8,128)(2,1)S(1)}, u32[]{:S(2)}, u32[]{:S(2)}) collective-permute-start(bf16[256,512]{1,0:T(8,128)(2,1)S(1)} %get-tuple-element.133), channel_id=1, source_target_pairs={{0,8},{8,0},{16,24},{24,16},{1,9},{9,1},{17,25},{25,17},{2,10},{10... | collective-permute-start | bytes 786440 | tf_op jit(solution)/shard_map/ppermute | solution.py:444
  125.7 7.1 %copy-start.10 = (s32[128,8]{0,1:T(8,128)S(1)}, s32[128,8]{0,1:T(8,128)}, u32[]{:S(2)}) copy-start(s32[128,8]{0,1:T(8,128)} %param.8) | copy-start | bytes 12292
  132.8 1.1 copy-start.24
  132.8 1.3 copy-start.26
where the time goes:
time: 136 us; the launch traced here: 135 us
  waiting for transfers between devices  47.2 us (35%)
  Pallas kernels  39.9 us (29%)
  starting transfers between devices  36.1 us (27%)
  local copies, waits for them, and re-layouts  11.1 us (8%)
    pallas_call x20, Pallas kernels, on_chip(): pl.pallas_call(body, in_specs=[SMEM] * scalars + [VMEM] * (len(operands)...  39.9 us
    ppermute x9, waiting for transfers between devices, move_z(): return lax.ppermute(v, 'expert', pairs)  31.1 us
    ppermute x9, starting transfers between devices, move_z(): return lax.ppermute(v, 'expert', pairs)  19.3 us
    unnamed x54, local copies, waits for them, and re-layouts  11.1 us
    ppermute x6, waiting for transfers between devices, move_y(): return lax.ppermute(v, 'dp', pairs)  6.81 us
    ppermute x6, starting transfers between devices, move_y(): return lax.ppermute(v, 'dp', pairs)  6.34 us
    ppermute x6, starting transfers between devices, move_x(): return lax.ppermute(v, 'dp', pairs)  6.21 us
    all_to_all x1, waiting for transfers between devices, send_home(): lax.all_to_all(parts, 'expert', split_axis=0, concat_axis=0, tiled=True,...  5.99 us
  transfers between devices with their start and end apart: 26, of which 10 were waited for; matrix products, arithmetic and copies ran while one was open for 0% of the time, Pallas kernels for 28%

commit v1 on v0

--- a/solution.py
+++ b/solution.py
@@ -325,6 +325,21 @@
     return [outs[j * n : (j + 1) * n] for j in range(E)], outs[-1]
 
 
+def relay(totals, name, *earlier):
+    sent = [v for total in totals for v in total[1:]]
+
+    def body(*refs):
+        outs = refs[len(sent) + len(earlier) :]
+        outs[-1][...] = jnp.zeros_like(outs[-1])
+        for source, out in zip(refs, outs[:-1]):
+            out[...] = source[...]
+
+    shapes = [jax.ShapeDtypeStruct(v.shape, v.dtype) for v in sent]
+    *outs, done = on_chip(body, [*sent, *earlier], shapes + [TOKEN], 0, name)
+    per = len(sent) // len(totals)
+    return [[t[0], *outs[i * per : (i + 1) * per]] for i, t in enumerate(totals)], done
+
+
 def add_second(totals, got, n, name, *earlier):
     E = len(totals)
     r, width = totals[0][0].shape
@@ -516,10 +531,11 @@
         place, tok_t, [ug0, ug1], E, n, D, "up_partials", tg_near[:8, :128], out_done
     )
     up_got = send_first(up_part)
-    down_got = send_second(down_totals)
     tg_parts, tg_done = add_sides(place, tg_near, tg_far, nz, "token_sides", up_done)
     tg_got = send_home(tg_parts)
-    gate_totals, gate_mid = add_first(gate_part, gate_got, n, "gate_first", tg_done)
+    down_totals, down_mid = relay(down_totals, "down_relay", tg_done)
+    down_got = send_second(down_totals)
+    gate_totals, gate_mid = add_first(gate_part, gate_got, n, "gate_first", down_mid)
     gate_got = send_second(gate_totals)
     up_totals, up_mid = add_first(up_part, up_got, n, "up_first", gate_mid)
     up_got = send_second(up_totals)

time: 136 us -> 133 us (0.978)
    all_to_all x1, waiting for transfers between devices: 5.99 us -> 1.44 us  [send_home(): lax.all_to_all(parts, 'expert', split_axis=0, concat_axis=0, tiled=True,...]
    ppermute x6, waiting for transfers between devices: 6.81 us -> 10.8 us  [move_y(): return lax.ppermute(v, 'dp', pairs)]
    ppermute x9, waiting for transfers between devices: 31.1 us -> 32.5 us  [move_z(): return lax.ppermute(v, 'expert', pairs)]
    pallas_call x20 -> x21, Pallas kernels: 39.9 us -> 38.8 us  [on_chip(): pl.pallas_call(body, in_specs=[SMEM] * scalars + [VMEM] * (len(operands)...]
    unnamed x54 -> x56, local copies, waits for them, and re-layouts: 11.1 us -> 10.5 us
  transfers between devices with their start and end apart: 26 -> 26, of which waited for: 10 -> 11; matrix products, arithmetic and copies ran while one was open for 0% -> 0% of each run, Pallas kernels for 28% -> 27%
where the time goes in v1:
time: 133 us; the launch traced here: 132 us
  waiting for transfers between devices  47.3 us (36%)
  Pallas kernels  38.8 us (29%)
  starting transfers between devices  34.8 us (26%)
  local copies, waits for them, and re-layouts  10.5 us (8%)
    pallas_call x21, Pallas kernels, on_chip(): pl.pallas_call(body, in_specs=[SMEM] * scalars + [VMEM] * (len(operands)...  38.8 us
    ppermute x9, waiting for transfers between devices, move_z(): return lax.ppermute(v, 'expert', pairs)  32.5 us
    ppermute x9, starting transfers between devices, move_z(): return lax.ppermute(v, 'expert', pairs)  19.3 us
    ppermute x6, waiting for transfers between devices, move_y(): return lax.ppermute(v, 'dp', pairs)  10.8 us
    unnamed x56, local copies, waits for them, and re-layouts  10.5 us
    ppermute x6, starting transfers between devices, move_x(): return lax.ppermute(v, 'dp', pairs)  5.68 us
    ppermute x6, starting transfers between devices, move_y(): return lax.ppermute(v, 'dp', pairs)  5.53 us
    all_to_all x1, starting transfers between devices, send_home(): lax.all_to_all(parts, 'expert', split_axis=0, concat_axis=0, tiled=True,...  3.52 us
  transfers between devices with their start and end apart: 26, of which 11 were waited for; matrix products, arithmetic and copies ran while one was open for 0% of the time, Pallas kernels for 27%

profile of v1, /device:TPU:0, one launch (start us, length us, event | category | flops | bytes accessed | tf_op | source)
XLA Modules:
  0.0 132.4 jit_solution(8360735674200906875)
XLA Ops:
  0.6 0.9 copy-done.5
  1.6 0.7 copy-done.7
  2.3 0.7 copy-done.8
  3.0 5.1 %collective-permute-start.2 = (bf16[136,1024]{1,0:T(8,128)(2,1)S(1)}, bf16[136,1024]{1,0:T(8,128)(2,1)S(1)}, u32[]{:S(2)}, u32[]{:S(2)}) collective-permute-start(bf16[136,1024]{1,0:T(8,128)(2,1)S(1)} %pack_tokens.1.refs_0_), channel_id=1, source_target_pairs={{0,6},{1,7},{2,0},{3,1},{4,2},{5,3},{6,4},{7,5},{8,14},{9,15},{10,... | collective-permute-start | bytes 835592 | tf_op jit(solution)/shard_map/ppermute | solution.py:455
  8.1 1.0 collective-permute-start
  9.1 6.1 %collective-permute-done.2.refs_3_ = bf16[136,1024]{1,0:T(8,128)(2,1)S(1)} collective-permute-done((bf16[136,1024]{1,0:T(8,128)(2,1)S(1)}, bf16[136,1024]{1,0:T(8,128)(2,1)S(1)}, u32[]{:S(2)}, u32[]{:S(2)}) %collective-permute-start.2) | collective-permute-done | bytes 278560 | tf_op jit(solution)/shard_map/ppermute | solution.py:455
  15.2 16.6 %collective-permute-done.1.refs_2_ = bf16[136,1024]{1,0:T(8,128)(2,1)S(1)} collective-permute-done((bf16[136,1024]{1,0:T(8,128)(2,1)S(1)}, bf16[136,1024]{1,0:T(8,128)(2,1)S(1)}, u32[]{:S(2)}, u32[]{:S(2)}) %collective-permute-start.1) | collective-permute-done | bytes 278560 | tf_op jit(solution)/shard_map/ppermute | solution.py:455
  31.8 0.1 collect.2.near_in
  31.9 0.1 collective-permute-start.3
  32.0 2.9 %collective-permute-start.6 = (bf16[128,1024]{1,0:T(8,128)(2,1)S(1)}, bf16[128,1024]{1,0:T(8,128)(2,1)}, u32[]{:S(2)}, u32[]{:S(2)}) collective-permute-start(bf16[128,1024]{1,0:T(8,128)(2,1)S(1)} %copy-done.6), channel_id=1, source_target_pairs={{0,4},{1,5},{2,6},{3,7},{4,0},{5,1},{6,2},{7,3},{8,12},{9,13},{10,... | collective-permute-start | bytes 786440 | tf_op jit(solution)/shard_map/ppermute | solution.py:455
  34.9 3.8 %collective-permute-start.7 = (bf16[128,1024]{1,0:T(8,128)(2,1)S(1)}, bf16[128,1024]{1,0:T(8,128)(2,1)}, u32[]{:S(2)}, u32[]{:S(2)}) collective-permute-start(bf16[128,1024]{1,0:T(8,128)(2,1)S(1)} %copy-done.6), channel_id=1, source_target_pairs={{0,6},{1,7},{2,0},{3,1},{4,2},{5,3},{6,4},{7,5},{8,14},{9,15},{10,... | collective-permute-start | bytes 786440 | tf_op jit(solution)/shard_map/ppermute | solution.py:455
  38.7 0.1 pad_add_fusion.place_ref.refs_0_
  38.8 1.6 %copy-done.1 = bf16[2,1024,512]{2,1,0:T(8,128)(2,1)S(1)} copy-done((bf16[2,1024,512]{2,1,0:T(8,128)(2,1)S(1)}, bf16[2,1024,512]{2,1,0:T(8,128)(2,1)}, u32[]{:S(2)}) %copy-start.1) | copy-done | bytes 2097176
  40.4 1.6 %copy-done.3 = bf16[2,1024,512]{2,1,0:T(8,128)(2,1)S(1)} copy-done((bf16[2,1024,512]{2,1,0:T(8,128)(2,1)S(1)}, bf16[2,1024,512]{2,1,0:T(8,128)(2,1)}, u32[]{:S(2)}) %copy-start.3) | copy-done | bytes 2097176
  42.0 10.0 %forward.1 = (bf16[512,1024]{1,0:T(8,128)(2,1)S(1)}, bf16[512,1024]{1,0:T(8,128)(2,1)S(1)}, bf16[512,1024]{1,0:T(8,128)(2,1)S(1)}, bf16[512,1024]{1,0:T(8,128)(2...) custom-call(s32[3]{0:T(128)S(1)} %pad_add_fusion.place_ref.refs_0_, ...), custom_call_target="tpu_custom_call" | custom-call | flops 10000000000 | bytes 22155276 | tf_op jit(solution)/shard_map/forward/pallas_call | solution.py:32
  52.0 1.4 %collective-permute-done.6.refs_2_ = bf16[128,1024]{1,0:T(8,128)(2,1)} collective-permute-done((bf16[128,1024]{1,0:T(8,128)(2,1)S(1)}, bf16[128,1024]{1,0:T(8,128)(2,1)}, u32[]{:S(2)}, u32[]{:S(2)}) %collective-permute-start.6) | collective-permute-done | bytes 262176 | tf_op jit(solution)/shard_map/ppermute | solution.py:455
  53.4 0.9 collective-permute-done.7.refs_3_
  54.3 1.2 collect.3.refs_0_
  55.5 0.1 collective-permute-start.8
  55.6 0.5 collective-permute-start.4
  56.1 1.8 %hidden_grads.2 = (bf16[512,1024]{1,0:T(8,128)(2,1)S(1)}, bf16[512,1024]{1,0:T(8,128)(2,1)S(1)}, f32[512,128]{1,0:T(8,128)S(1)}, f32[8,128]{1,0:T(8,128)S(1)}) custom-call(bf16[512,1024]{1,0:T(8,128)(2,1)S(1)} %collect.3.refs_0_, bf16[512,1024]{1,0:T(8,128)(2,1)S(1)} %get-tuple-element.79.refs_1_, bf16[512,1024]{1,0:T(8,128)(2,1)S(1)} %get-tuple-element.80.refs_2_, ...), custom_call_target="tpu_custom_call" | custom-call | flops 10000000000 | bytes 8654848 | tf_op jit(solution)/shard_map/hidden_grads/pallas_call | solution.py:32
  57.9 0.4 collective-permute-done.8.refs_1_.refs_0_
  58.2 2.9 %down_partials.1 = (bf16[1,2,128,1024]{3,2,1,0:T(8,128)(2,1)S(1)}, f32[2,128,1024]{2,1,0:T(8,128)S(1)}, bf16[1,2,128,1024]{3,2,1,0:T(8,128)(2,1)S(1)}, f32[2,128,1024]{2,1,0:T(8,128)S(1)}, f32[8,128]{1,0:T(8,128)S(1)}) custom-call(s32[3]{0:T(128)S(1)} %pad_add_fusion.place_ref.refs_0_, bf16[1024,1024]{1,0:T(8,128)(2,1)S(1)} %get-tuple-element.77.left_ref, ...), custom_call_target="tpu_custom_call" | custom-call | flops 10000000000 | bytes 7348236 | tf_op jit(solution)/shard_map/down_partials/pallas_call | solution.py:32
  61.1 1.6 %collective-permute-start.12 = (bf16[2,128,1024]{2,1,0:T(8,128)(2,1)S(1)}, bf16[2,128,1024]{2,1,0:T(8,128)(2,1)S(1)}, u32[]{:S(2)}, u32[]{:S(2)}) collective-permute-start(bf16[2,128,1024]{2,1,0:T(8,128)(2,1)S(1)} %bitcast.18), channel_id=1, source_target_pairs={{0,8},{8,0},{16,24},{24,16},{1,9},{9,1},{17,25},{25,17},{2,10},{10... | collective-permute-start | bytes 1572872 | tf_op jit(solution)/shard_map/ppermute | solution.py:459
  62.7 1.5 %collective-permute-start.13 = (bf16[2,128,1024]{2,1,0:T(8,128)(2,1)S(1)}, bf16[2,128,1024]{2,1,0:T(8,128)(2,1)S(1)}, u32[]{:S(2)}, u32[]{:S(2)}) collective-permute-start(bf16[2,128,1024]{2,1,0:T(8,128)(2,1)S(1)} %bitcast.17), channel_id=1, source_target_pairs={{0,16},{8,24},{16,0},{24,8},{1,17},{9,25},{17,1},{25,9},{2,18},{10... | collective-permute-start | bytes 1572872 | tf_op jit(solution)/shard_map/ppermute | solution.py:463
  64.2 0.2 out_sides.1
  64.4 2.6 %collective-permute-start.9 = (bf16[128,1024]{1,0:T(8,128)(2,1)S(1)}, bf16[128,1024]{1,0:T(8,128)(2,1)S(1)}, u32[]{:S(2)}, u32[]{:S(2)}) collective-permute-start(bf16[128,1024]{1,0:T(8,128)(2,1)S(1)} %get-tuple-element.85), channel_id=1, source_target_pairs={{0,6},{1,7},{2,0},{3,1},{4,2},{5,3},{6,4},{7,5},{8,14},{9,15},{10,... | collective-permute-start | bytes 786440 | tf_op jit(solution)/shard_map/ppermute | solution.py:455
  67.0 4.0 %collective-permute-start.10 = (bf16[128,1024]{1,0:T(8,128)(2,1)S(1)}, bf16[128,1024]{1,0:T(8,128)(2,1)S(1)}, u32[]{:S(2)}, u32[]{:S(2)}) collective-permute-start(bf16[128,1024]{1,0:T(8,128)(2,1)S(1)} %get-tuple-element.86), channel_id=1, source_target_pairs={{0,4},{1,5},{2,6},{3,7},{4,0},{5,1},{6,2},{7,3},{8,12},{9,13},{10,... | collective-permute-start | bytes 786440 | tf_op jit(solution)/shard_map/ppermute | solution.py:455
  71.0 2.3 %hidden_grads.3 = (bf16[512,1024]{1,0:T(8,128)(2,1)S(1)}, bf16[512,1024]{1,0:T(8,128)(2,1)S(1)}, f32[512,128]{1,0:T(8,128)S(1)}, f32[8,128]{1,0:T(8,128)}) custom-call(bf16[512,1024]{1,0:T(8,128)(2,1)S(1)} %collective-permute-done.8.refs_1_.refs_0_, bf16[512,1024]{1,0:T(8,128)(2,1)S(1)} %get-tuple-element.89.refs_1_, ...), custom_call_target="tpu_custom_call" | custom-call | flops 10000000000 | bytes 8658944 | tf_op jit(solution)/shard_map/hidden_grads/pallas_call | solution.py:32
  73.3 2.9 %gate_partials.1 = (bf16[1,2,256,512]{3,2,1,0:T(8,128)(2,1)S(1)}, f32[2,256,512]{2,1,0:T(8,128)S(1)}, bf16[1,2,256,512]{3,2,1,0:T(8,128)(2,1)S(1)}, f32[2,256,512]{2,1,0:T(8,128)S(1)}, f32[8,128]{1,0:T(8,128)S(1)}) custom-call(s32[3]{0:T(128)S(1)} %pad_add_fusion.place_ref.refs_0_, bf16[1024,1024]{1,0:T(8,128)(2,1)S(1)} %get-tuple-element.101.left_ref, ...), custom_call_target="tpu_custom_call" | custom-call | flops 10000000000 | bytes 7344140 | tf_op jit(solution)/shard_map/gate_partials/pallas_call | solution.py:32
  76.2 0.6 collective-permute-start.15
  76.8 1.3 %collective-permute-start.16 = (bf16[2,256,512]{2,1,0:T(8,128)(2,1)S(1)}, bf16[2,256,512]{2,1,0:T(8,128)(2,1)S(1)}, u32[]{:S(2)}, u32[]{:S(2)}) collective-permute-start(bf16[2,256,512]{2,1,0:T(8,128)(2,1)S(1)} %bitcast.15), channel_id=1, source_target_pairs={{0,16},{8,24},{16,0},{24,8},{1,17},{9,25},{17,1},{25,9},{2,18},{10... | collective-permute-start | bytes 1572872 | tf_op jit(solution)/shard_map/ppermute | solution.py:463
  78.2 0.2 down_first.1
  78.4 0.8 copy-done.18
  79.2 0.7 copy-done.2
  80.0 0.9 copy-done.4
  80.9 5.1 %token_partials.1 = (f32[544,1024]{1,0:T(8,128)S(1)}, bf16[544,1024]{1,0:T(8,128)(2,1)S(1)}) custom-call(s32[3]{0:T(128)S(1)} %pad_add_fusion.place_ref.refs_0_, bf16[512,1024]{1,0:T(8,128)(2,1)S(1)} %get-tuple-element.88.refs_0_.refs_1_, bf16[512,1024]{1,0:T(8,128)(2,1)S(1)} %get-tuple-element.92.refs_1_.refs_2_, ...), custom_call_target="tpu_custom_call" | custom-call | flops 10000000000 | bytes 12259340 | tf_op jit(solution)/shard_map/token_partials/pallas_call | solution.py:32
  86.0 0.1 collective-permute-start.14
  86.1 7.5 %collective-permute-done.10.refs_2_ = bf16[128,1024]{1,0:T(8,128)(2,1)S(1)} collective-permute-done((bf16[128,1024]{1,0:T(8,128)(2,1)S(1)}, bf16[128,1024]{1,0:T(8,128)(2,1)S(1)}, u32[]{:S(2)}, u32[]{:S(2)}) %collective-permute-start.10) | collective-permute-done | bytes 262176 | tf_op jit(solution)/shard_map/ppermute | solution.py:455
  93.6 0.8 out_rows.1
  94.4 3.6 %up_partials.1 = (bf16[1,2,256,512]{3,2,1,0:T(8,128)(2,1)}, f32[2,256,512]{2,1,0:T(8,128)S(1)}, bf16[1,2,256,512]{3,2,1,0:T(8,128)(2,1)}, f32[2,256,512]{2,1,0:T(8,128)S(1)}, f32[8,128]{1,0:T(8,128)S(1)}) custom-call(s32[3]{0:T(128)S(1)} %pad_add_fusion.place_ref.refs_0_, bf16[1024,1024]{1,0:T(8,128)(2,1)S(1)} %get-tuple-element.101.left_ref, ...), custom_call_target="tpu_custom_call" | custom-call | flops 10000000000 | bytes 7352332 | tf_op jit(solution)/shard_map/up_partials/pallas_call | solution.py:32
  98.0 0.5 collective-permute-start.21
  98.5 0.5 collective-permute-start.22
  99.1 1.8 %token_sides.1 = (bf16[544,1024]{1,0:T(8,128)(2,1)}, f32[8,128]{1,0:T(8,128)S(1)}) custom-call(s32[3]{0:T(128)S(1)} %pad_add_fusion.place_ref.refs_0_, f32[544,1024]{1,0:T(8,128)S(1)} %get-tuple-element.104.near_ref, bf16[544,1024]{1,0:T(8,128)(2,1)S(1)} %collective-permute-done.14.far_ref, f32[8,128]{1,0:T(8,128)S(1)} %get-tuple-element.108.refs_0_), custom_call_target="tpu_custom_call" | custom-call | flops 10000000000 | bytes 4464652 | tf_op jit(solution)/shard_map/token_sides/pallas_call | solution.py:32
  100.8 3.5 %all-to-all-start = ((bf16[4,136,1024]{2,1,0:T(8,128)(2,1)}), bf16[4,136,1024]{2,1,0:T(8,128)(2,1)S(1)}, u32[]{:S(2)}, u32[]{:S(2)}) async-start(bf16[4,136,1024]{2,1,0:T(8,128)(2,1)} %bitcast.7), calls=%async_computation | async-start | bytes 2228224 | tf_op jit(solution)/shard_map/all_to_all | solution.py:497
  104.4 0.9 copy-done.27
  105.4 1.2 copy-done.15
  106.5 0.3 copy-done.17
  106.9 0.2 gate_first.1
  107.1 1.6 %collective-permute-start.17 = (bf16[256,512]{1,0:T(8,128)(2,1)S(1)}, bf16[256,512]{1,0:T(8,128)(2,1)S(1)}, u32[]{:S(2)}, u32[]{:S(2)}) collective-permute-start(bf16[256,512]{1,0:T(8,128)(2,1)S(1)} %get-tuple-element.121), channel_id=1, source_target_pairs={{0,16},{8,24},{16,0},{24,8},{1,17},{9,25},{17,1},{25,9},{2,18},{10... | collective-permute-start | bytes 786440 | tf_op jit(solution)/shard_map/ppermute | solution.py:463
  108.7 1.5 %collective-permute-start.18 = (bf16[256,512]{1,0:T(8,128)(2,1)S(1)}, bf16[256,512]{1,0:T(8,128)(2,1)S(1)}, u32[]{:S(2)}, u32[]{:S(2)}) collective-permute-start(bf16[256,512]{1,0:T(8,128)(2,1)S(1)} %get-tuple-element.123), channel_id=1, source_target_pairs={{0,8},{8,0},{16,24},{24,16},{1,9},{9,1},{17,25},{25,17},{2,10},{10... | collective-permute-start | bytes 786440 | tf_op jit(solution)/shard_map/ppermute | solution.py:459
  110.2 0.5 collective-permute-start.19
  110.7 1.7 %collective-permute-done.21.refs_1_ = bf16[2,256,512]{2,1,0:T(8,128)(2,1)} collective-permute-done((bf16[2,256,512]{2,1,0:T(8,128)(2,1)}, bf16[2,256,512]{2,1,0:T(8,128)(2,1)}, u32[]{:S(2)}, u32[]{:S(2)}) %collective-permute-start.21) | collective-permute-done | bytes 524320 | tf_op jit(solution)/shard_map/ppermute | solution.py:459
  112.4 1.3 %collective-permute-done.22.refs_3_ = bf16[2,256,512]{2,1,0:T(8,128)(2,1)} collective-permute-done((bf16[2,256,512]{2,1,0:T(8,128)(2,1)}, bf16[2,256,512]{2,1,0:T(8,128)(2,1)}, u32[]{:S(2)}, u32[]{:S(2)}) %collective-permute-start.22) | collective-permute-done | bytes 524320 | tf_op jit(solution)/shard_map/ppermute | solution.py:463
  113.7 1.5 %up_first.1 = (f32[256,512]{1,0:T(8,128)S(1)}, bf16[256,512]{1,0:T(8,128)(2,1)S(1)}, f32[256,512]{1,0:T(8,128)S(1)}, bf16[256,512]{1,0:T(8,128)(2,1)S(1)}, f32[8,128]{1,0:T(8,128)S(1)}) custom-call(f32[2,256,512]{2,1,0:T(8,128)S(1)} %copy-done.11, bf16[2,256,512]{2,1,0:T(8,128)(2,1)} %collective-permute-done.21.refs_1_, f32[2,256,512]{2,1,0:T(8,128)S(1)} %copy-done.13, ...), custom_call_target="tpu_custom_call" | custom-call | flops 10000000000 | bytes 4726784 | tf_op jit(solution)/shard_map/up_first/pallas_call | solution.py:32
  115.3 0.1 collective-permute-start.23
  115.4 9.5 %collective-permute-done.19.refs_1_ = bf16[128,1024]{1,0:T(8,128)(2,1)S(1)} collective-permute-done((bf16[128,1024]{1,0:T(8,128)(2,1)S(1)}, bf16[128,1024]{1,0:T(8,128)(2,1)S(1)}, u32[]{:S(2)}, u32[]{:S(2)}) %collective-permute-start.19) | collective-permute-done | bytes 262176 | tf_op jit(solution)/shard_map/ppermute | solution.py:463
  124.9 1.5 %collective-permute-start.24 = (bf16[256,512]{1,0:T(8,128)(2,1)S(1)}, bf16[256,512]{1,0:T(8,128)(2,1)S(1)}, u32[]{:S(2)}, u32[]{:S(2)}) collective-permute-start(bf16[256,512]{1,0:T(8,128)(2,1)S(1)} %get-tuple-element.139), channel_id=1, source_target_pairs={{0,8},{8,0},{16,24},{24,16},{1,9},{9,1},{17,25},{25,17},{2,10},{10... | collective-permute-start | bytes 786440 | tf_op jit(solution)/shard_map/ppermute | solution.py:459
  126.4 1.1 down_second.1
  127.5 1.1 gate_second.1
  128.5 1.4 %all-to-all-done = bf16[4,136,1024]{2,1,0:T(8,128)(2,1)S(1)} async-done(((bf16[4,136,1024]{2,1,0:T(8,128)(2,1)}), bf16[4,136,1024]{2,1,0:T(8,128)(2,1)S(1)}, u32[]{:S(2)}, u32[]{:S(2)}) %all-to-all-start) | async-done | bytes 1114144 | tf_op jit(solution)/shard_map/all_to_all | solution.py:497
  130.0 0.8 token_rows.1
  130.8 0.4 collective-permute-done.24.refs_3_
  131.3 1.1 up_second.1
  (67 shorter events, 0.3 us)
Async XLA Ops:
  0.6 1.0 copy-start.5
  1.6 0.7 copy-start.7
  2.3 0.7 copy-start.8
  3.0 29.0 %copy-start.6 = (bf16[128,1024]{1,0:T(8,128)(2,1)S(1)}, bf16[128,1024]{1,0:T(8,128)(2,1)}, u32[]{:S(2)}) copy-start(bf16[128,1024]{1,0:T(8,128)(2,1)} %refs_0_.1) | copy-start | bytes 786436
  3.0 35.8 %copy-start = (bf16[2,512,1024]{2,1,0:T(8,128)(2,1)S(1)}, bf16[2,512,1024]{2,1,0:T(8,128)(2,1)}, u32[]{:S(2)}) copy-start(bf16[2,512,1024]{2,1,0:T(8,128)(2,1)} %refs_4_.3) | copy-start | bytes 6291460
  3.0 12.2 %collective-permute-start.2 = (bf16[136,1024]{1,0:T(8,128)(2,1)S(1)}, bf16[136,1024]{1,0:T(8,128)(2,1)S(1)}, u32[]{:S(2)}, u32[]{:S(2)}) collective-permute-start(bf16[136,1024]{1,0:T(8,128)(2,1)S(1)} %pack_tokens.1.refs_0_), channel_id=1, source_target_pairs={{0,6},{1,7},{2,0},{3,1},{4,2},{5,3},{6,4},{7,5},{8,14},{9,15},{10,... | collective-permute-start | bytes 835592 | tf_op jit(solution)/shard_map/ppermute | solution.py:455
  8.1 23.7 %collective-permute-start.1 = (bf16[136,1024]{1,0:T(8,128)(2,1)S(1)}, bf16[136,1024]{1,0:T(8,128)(2,1)S(1)}, u32[]{:S(2)}, u32[]{:S(2)}) collective-permute-start(bf16[136,1024]{1,0:T(8,128)(2,1)S(1)} %pack_tokens.1.refs_0_), channel_id=1, source_target_pairs={{0,4},{1,5},{2,6},{3,7},{4,0},{5,1},{6,2},{7,3},{8,12},{9,13},{10,... | collective-permute-start | bytes 835592 | tf_op jit(solution)/shard_map/ppermute | solution.py:455
  8.1 23.7 %collective-permute-start = (bf16[136,1024]{1,0:T(8,128)(2,1)S(1)}, bf16[136,1024]{1,0:T(8,128)(2,1)S(1)}, u32[]{:S(2)}, u32[]{:S(2)}) collective-permute-start(bf16[136,1024]{1,0:T(8,128)(2,1)S(1)} %pack_tokens.1.refs_0_), channel_id=1, source_target_pairs={{0,2},{1,3},{2,4},{3,5},{4,6},{5,7},{6,0},{7,1},{8,10},{9,11},{10,... | collective-permute-start | bytes 835592 | tf_op jit(solution)/shard_map/ppermute | solution.py:455
  31.9 6.9 %collective-permute-start.3 = (bf16[544,1024]{1,0:T(8,128)(2,1)S(1)}, bf16[544,1024]{1,0:T(8,128)(2,1)}, u32[]{:S(2)}, u32[]{:S(2)}) collective-permute-start(bf16[544,1024]{1,0:T(8,128)(2,1)S(1)} %collect.2.near_in), channel_id=1, source_target_pairs={{0,1},{1,0},{2,3},{3,2},{4,5},{5,4},{6,7},{7,6},{8,9},{9,8},{10,11... | collective-permute-start | bytes 3342344 | tf_op jit(solution)/shard_map/ppermute | solution.py:451
  32.0 21.4 %collective-permute-start.6 = (bf16[128,1024]{1,0:T(8,128)(2,1)S(1)}, bf16[128,1024]{1,0:T(8,128)(2,1)}, u32[]{:S(2)}, u32[]{:S(2)}) collective-permute-start(bf16[128,1024]{1,0:T(8,128)(2,1)S(1)} %copy-done.6), channel_id=1, source_target_pairs={{0,4},{1,5},{2,6},{3,7},{4,0},{5,1},{6,2},{7,3},{8,12},{9,13},{10,... | collective-permute-start | bytes 786440 | tf_op jit(solution)/shard_map/ppermute | solution.py:455
  34.9 18.6 %collective-permute-start.5 = (bf16[128,1024]{1,0:T(8,128)(2,1)S(1)}, bf16[128,1024]{1,0:T(8,128)(2,1)}, u32[]{:S(2)}, u32[]{:S(2)}) collective-permute-start(bf16[128,1024]{1,0:T(8,128)(2,1)S(1)} %copy-done.6), channel_id=1, source_target_pairs={{0,2},{1,3},{2,4},{3,5},{4,6},{5,7},{6,0},{7,1},{8,10},{9,11},{10,... | collective-permute-start | bytes 786440 | tf_op jit(solution)/shard_map/ppermute | solution.py:455
  34.9 19.4 %collective-permute-start.7 = (bf16[128,1024]{1,0:T(8,128)(2,1)S(1)}, bf16[128,1024]{1,0:T(8,128)(2,1)}, u32[]{:S(2)}, u32[]{:S(2)}) collective-permute-start(bf16[128,1024]{1,0:T(8,128)(2,1)S(1)} %copy-done.6), channel_id=1, source_target_pairs={{0,6},{1,7},{2,0},{3,1},{4,2},{5,3},{6,4},{7,5},{8,14},{9,15},{10,... | collective-permute-start | bytes 786440 | tf_op jit(solution)/shard_map/ppermute | solution.py:455
  38.8 1.6 %copy-start.1 = (bf16[2,1024,512]{2,1,0:T(8,128)(2,1)S(1)}, bf16[2,1024,512]{2,1,0:T(8,128)(2,1)}, u32[]{:S(2)}) copy-start(bf16[2,1024,512]{2,1,0:T(8,128)(2,1)} %refs_7_.1) | copy-start | bytes 6291460
  40.4 1.6 %copy-start.3 = (bf16[2,1024,512]{2,1,0:T(8,128)(2,1)S(1)}, bf16[2,1024,512]{2,1,0:T(8,128)(2,1)}, u32[]{:S(2)}) copy-start(bf16[2,1024,512]{2,1,0:T(8,128)(2,1)} %refs_8_.1) | copy-start | bytes 6291460
  55.5 2.7 %collective-permute-start.8 = (bf16[512,1024]{1,0:T(8,128)(2,1)S(1)}, bf16[512,1024]{1,0:T(8,128)(2,1)S(1)}, u32[]{:S(2)}, u32[]{:S(2)}) collective-permute-start(bf16[512,1024]{1,0:T(8,128)(2,1)S(1)} %collect.3.refs_0_), channel_id=1, source_target_pairs={{0,1},{1,0},{2,3},{3,2},{4,5},{5,4},{6,7},{7,6},{8,9},{9,8},{10,11... | collective-permute-start | bytes 3145736 | tf_op jit(solution)/shard_map/ppermute | solution.py:451
  55.6 8.6 %collective-permute-start.4 = (bf16[512,1024]{1,0:T(8,128)(2,1)S(1)}, bf16[512,1024]{1,0:T(8,128)(2,1)S(1)}, u32[]{:S(2)}, u32[]{:S(2)}) collective-permute-start(bf16[512,1024]{1,0:T(8,128)(2,1)S(1)} %get-tuple-element.76), channel_id=1, source_target_pairs={{0,1},{1,0},{2,3},{3,2},{4,5},{5,4},{6,7},{7,6},{8,9},{9,8},{10,11... | collective-permute-start | bytes 3145736 | tf_op jit(solution)/shard_map/ppermute | solution.py:451
  61.1 15.1 %collective-permute-start.12 = (bf16[2,128,1024]{2,1,0:T(8,128)(2,1)S(1)}, bf16[2,128,1024]{2,1,0:T(8,128)(2,1)S(1)}, u32[]{:S(2)}, u32[]{:S(2)}) collective-permute-start(bf16[2,128,1024]{2,1,0:T(8,128)(2,1)S(1)} %bitcast.18), channel_id=1, source_target_pairs={{0,8},{8,0},{16,24},{24,16},{1,9},{9,1},{17,25},{25,17},{2,10},{10... | collective-permute-start | bytes 1572872 | tf_op jit(solution)/shard_map/ppermute | solution.py:459
  62.7 14.1 %collective-permute-start.13 = (bf16[2,128,1024]{2,1,0:T(8,128)(2,1)S(1)}, bf16[2,128,1024]{2,1,0:T(8,128)(2,1)S(1)}, u32[]{:S(2)}, u32[]{:S(2)}) collective-permute-start(bf16[2,128,1024]{2,1,0:T(8,128)(2,1)S(1)} %bitcast.17), channel_id=1, source_target_pairs={{0,16},{8,24},{16,0},{24,8},{1,17},{9,25},{17,1},{25,9},{2,18},{10... | collective-permute-start | bytes 1572872 | tf_op jit(solution)/shard_map/ppermute | solution.py:463
  64.4 21.6 %collective-permute-start.9 = (bf16[128,1024]{1,0:T(8,128)(2,1)S(1)}, bf16[128,1024]{1,0:T(8,128)(2,1)S(1)}, u32[]{:S(2)}, u32[]{:S(2)}) collective-permute-start(bf16[128,1024]{1,0:T(8,128)(2,1)S(1)} %get-tuple-element.85), channel_id=1, source_target_pairs={{0,6},{1,7},{2,0},{3,1},{4,2},{5,3},{6,4},{7,5},{8,14},{9,15},{10,... | collective-permute-start | bytes 786440 | tf_op jit(solution)/shard_map/ppermute | solution.py:455
  67.0 26.6 %collective-permute-start.10 = (bf16[128,1024]{1,0:T(8,128)(2,1)S(1)}, bf16[128,1024]{1,0:T(8,128)(2,1)S(1)}, u32[]{:S(2)}, u32[]{:S(2)}) collective-permute-start(bf16[128,1024]{1,0:T(8,128)(2,1)S(1)} %get-tuple-element.86), channel_id=1, source_target_pairs={{0,4},{1,5},{2,6},{3,7},{4,0},{5,1},{6,2},{7,3},{8,12},{9,13},{10,... | collective-permute-start | bytes 786440 | tf_op jit(solution)/shard_map/ppermute | solution.py:455
  71.0 22.6 %collective-permute-start.11 = (bf16[128,1024]{1,0:T(8,128)(2,1)S(1)}, bf16[128,1024]{1,0:T(8,128)(2,1)S(1)}, u32[]{:S(2)}, u32[]{:S(2)}) collective-permute-start(bf16[128,1024]{1,0:T(8,128)(2,1)S(1)} %get-tuple-element.87), channel_id=1, source_target_pairs={{0,2},{1,3},{2,4},{3,5},{4,6},{5,7},{6,0},{7,1},{8,10},{9,11},{10,... | collective-permute-start | bytes 786440 | tf_op jit(solution)/shard_map/ppermute | solution.py:455
  76.2 2.2 %copy-start.14 = (f32[2,256,512]{2,1,0:T(8,128)}, f32[2,256,512]{2,1,0:T(8,128)S(1)}, u32[]{:S(2)}) copy-start(f32[2,256,512]{2,1,0:T(8,128)S(1)} %get-tuple-element.112.refs_0_) | copy-start | bytes 3145732
  76.2 2.2 %copy-start.16 = (f32[2,256,512]{2,1,0:T(8,128)}, f32[2,256,512]{2,1,0:T(8,128)S(1)}, u32[]{:S(2)}) copy-start(f32[2,256,512]{2,1,0:T(8,128)S(1)} %get-tuple-element.114.refs_2_) | copy-start | bytes 3145732
  76.2 29.1 %collective-permute-start.15 = (bf16[2,256,512]{2,1,0:T(8,128)(2,1)S(1)}, bf16[2,256,512]{2,1,0:T(8,128)(2,1)S(1)}, u32[]{:S(2)}, u32[]{:S(2)}) collective-permute-start(bf16[2,256,512]{2,1,0:T(8,128)(2,1)S(1)} %bitcast.16), channel_id=1, source_target_pairs={{0,8},{8,0},{16,24},{24,16},{1,9},{9,1},{17,25},{25,17},{2,10},{10... | collective-permute-start | bytes 1572872 | tf_op jit(solution)/shard_map/ppermute | solution.py:459
  76.8 28.5 %collective-permute-start.16 = (bf16[2,256,512]{2,1,0:T(8,128)(2,1)S(1)}, bf16[2,256,512]{2,1,0:T(8,128)(2,1)S(1)}, u32[]{:S(2)}, u32[]{:S(2)}) collective-permute-start(bf16[2,256,512]{2,1,0:T(8,128)(2,1)S(1)} %bitcast.15), channel_id=1, source_target_pairs={{0,16},{8,24},{16,0},{24,8},{1,17},{9,25},{17,1},{25,9},{2,18},{10... | collective-permute-start | bytes 1572872 | tf_op jit(solution)/shard_map/ppermute | solution.py:463
  78.2 1.8 %copy-start.2 = (bf16[2,1024,512]{2,1,0:T(8,128)(2,1)S(1)}, bf16[2,1024,512]{2,1,0:T(8,128)(2,1)}, u32[]{:S(2)}) copy-start(bf16[2,1024,512]{2,1,0:T(8,128)(2,1)} %refs_7_.1) | copy-start | bytes 6291460
  78.2 2.7 %copy-start.4 = (bf16[2,1024,512]{2,1,0:T(8,128)(2,1)S(1)}, bf16[2,1024,512]{2,1,0:T(8,128)(2,1)}, u32[]{:S(2)}) copy-start(bf16[2,1024,512]{2,1,0:T(8,128)(2,1)} %refs_8_.1) | copy-start | bytes 6291460
  78.4 0.8 copy-start.18
  79.2 6.8 %copy-start.20 = (f32[128,1024]{1,0:T(8,128)}, f32[128,1024]{1,0:T(8,128)S(1)}, u32[]{:S(2)}) copy-start(f32[128,1024]{1,0:T(8,128)S(1)} %get-tuple-element.126.refs_2_) | copy-start | bytes 1572868
  79.2 6.8 %copy-start.26 = (bf16[128,1024]{1,0:T(8,128)(2,1)}, bf16[128,1024]{1,0:T(8,128)(2,1)S(1)}, u32[]{:S(2)}) copy-start(bf16[128,1024]{1,0:T(8,128)(2,1)S(1)} %get-tuple-element.117.refs_1_) | copy-start | bytes 786436
  86.0 13.0 %collective-permute-start.14 = (bf16[544,1024]{1,0:T(8,128)(2,1)S(1)}, bf16[544,1024]{1,0:T(8,128)(2,1)S(1)}, u32[]{:S(2)}, u32[]{:S(2)}) collective-permute-start(bf16[544,1024]{1,0:T(8,128)(2,1)S(1)} %get-tuple-element.106), channel_id=1, source_target_pairs={{0,1},{1,0},{2,3},{3,2},{4,5},{5,4},{6,7},{7,6},{8,9},{9,8},{10,11... | collective-permute-start | bytes 3342344 | tf_op jit(solution)/shard_map/ppermute | solution.py:451
  98.0 2.8 %copy-start.10 = (f32[2,256,512]{2,1,0:T(8,128)}, f32[2,256,512]{2,1,0:T(8,128)S(1)}, u32[]{:S(2)}) copy-start(f32[2,256,512]{2,1,0:T(8,128)S(1)} %get-tuple-element.128.refs_0_) | copy-start | bytes 3145732
  98.0 2.8 %copy-start.12 = (f32[2,256,512]{2,1,0:T(8,128)}, f32[2,256,512]{2,1,0:T(8,128)S(1)}, u32[]{:S(2)}) copy-start(f32[2,256,512]{2,1,0:T(8,128)S(1)} %get-tuple-element.130.refs_2_) | copy-start | bytes 3145732
  98.0 14.4 %collective-permute-start.21 = (bf16[2,256,512]{2,1,0:T(8,128)(2,1)}, bf16[2,256,512]{2,1,0:T(8,128)(2,1)}, u32[]{:S(2)}, u32[]{:S(2)}) collective-permute-start(bf16[2,256,512]{2,1,0:T(8,128)(2,1)} %bitcast.12), channel_id=1, source_target_pairs={{0,8},{8,0},{16,24},{24,16},{1,9},{9,1},{17,25},{25,17},{2,10},{10... | collective-permute-start | bytes 1572872 | tf_op jit(solution)/shard_map/ppermute | solution.py:459
  98.5 15.2 %collective-permute-start.22 = (bf16[2,256,512]{2,1,0:T(8,128)(2,1)}, bf16[2,256,512]{2,1,0:T(8,128)(2,1)}, u32[]{:S(2)}, u32[]{:S(2)}) collective-permute-start(bf16[2,256,512]{2,1,0:T(8,128)(2,1)} %bitcast.13), channel_id=1, source_target_pairs={{0,16},{8,24},{16,0},{24,8},{1,17},{9,25},{17,1},{25,9},{2,18},{10... | collective-permute-start | bytes 1572872 | tf_op jit(solution)/shard_map/ppermute | solution.py:463
  100.8 29.2 %all-to-all-start = ((bf16[4,136,1024]{2,1,0:T(8,128)(2,1)}), bf16[4,136,1024]{2,1,0:T(8,128)(2,1)S(1)}, u32[]{:S(2)}, u32[]{:S(2)}) async-start(bf16[4,136,1024]{2,1,0:T(8,128)(2,1)} %bitcast.7), calls=%async_computation | async-start | bytes 2228224 | tf_op jit(solution)/shard_map/all_to_all | solution.py:497
  104.4 1.0 copy-start.27
  105.3 1.2 copy-start.15
  105.3 1.5 %copy-start.17 = (f32[2,256,512]{2,1,0:T(8,128)S(1)}, f32[2,256,512]{2,1,0:T(8,128)}, u32[]{:S(2)}) copy-start(f32[2,256,512]{2,1,0:T(8,128)} %copy-done.16) | copy-start | bytes 3145732
  106.8 6.9 %copy-start.11 = (f32[2,256,512]{2,1,0:T(8,128)S(1)}, f32[2,256,512]{2,1,0:T(8,128)}, u32[]{:S(2)}) copy-start(f32[2,256,512]{2,1,0:T(8,128)} %copy-done.10) | copy-start | bytes 3145732
  106.8 6.9 %copy-start.13 = (f32[2,256,512]{2,1,0:T(8,128)S(1)}, f32[2,256,512]{2,1,0:T(8,128)}, u32[]{:S(2)}) copy-start(f32[2,256,512]{2,1,0:T(8,128)} %copy-done.12) | copy-start | bytes 3145732
  107.1 20.4 %collective-permute-start.17 = (bf16[256,512]{1,0:T(8,128)(2,1)S(1)}, bf16[256,512]{1,0:T(8,128)(2,1)S(1)}, u32[]{:S(2)}, u32[]{:S(2)}) collective-permute-start(bf16[256,512]{1,0:T(8,128)(2,1)S(1)} %get-tuple-element.121), channel_id=1, source_target_pairs={{0,16},{8,24},{16,0},{24,8},{1,17},{9,25},{17,1},{25,9},{2,18},{10... | collective-permute-start | bytes 786440 | tf_op jit(solution)/shard_map/ppermute | solution.py:463
  108.7 18.8 %collective-permute-start.18 = (bf16[256,512]{1,0:T(8,128)(2,1)S(1)}, bf16[256,512]{1,0:T(8,128)(2,1)S(1)}, u32[]{:S(2)}, u32[]{:S(2)}) collective-permute-start(bf16[256,512]{1,0:T(8,128)(2,1)S(1)} %get-tuple-element.123), channel_id=1, source_target_pairs={{0,8},{8,0},{16,24},{24,16},{1,9},{9,1},{17,25},{25,17},{2,10},{10... | collective-permute-start | bytes 786440 | tf_op jit(solution)/shard_map/ppermute | solution.py:459
  110.2 14.7 %collective-permute-start.19 = (bf16[128,1024]{1,0:T(8,128)(2,1)S(1)}, bf16[128,1024]{1,0:T(8,128)(2,1)S(1)}, u32[]{:S(2)}, u32[]{:S(2)}) collective-permute-start(bf16[128,1024]{1,0:T(8,128)(2,1)S(1)} %get-tuple-element.125), channel_id=1, source_target_pairs={{0,16},{8,24},{16,0},{24,8},{1,17},{9,25},{17,1},{25,9},{2,18},{10... | collective-permute-start | bytes 786440 | tf_op jit(solution)/shard_map/ppermute | solution.py:463
  112.4 14.0 %collective-permute-start.20 = (bf16[128,1024]{1,0:T(8,128)(2,1)S(1)}, bf16[128,1024]{1,0:T(8,128)(2,1)S(1)}, u32[]{:S(2)}, u32[]{:S(2)}) collective-permute-start(bf16[128,1024]{1,0:T(8,128)(2,1)S(1)} %get-tuple-element.127), channel_id=1, source_target_pairs={{0,8},{8,0},{16,24},{24,16},{1,9},{9,1},{17,25},{25,17},{2,10},{10... | collective-permute-start | bytes 786440 | tf_op jit(solution)/shard_map/ppermute | solution.py:459
  113.7 12.6 %copy-start.19 = (f32[128,1024]{1,0:T(8,128)S(1)}, f32[128,1024]{1,0:T(8,128)}, u32[]{:S(2)}) copy-start(f32[128,1024]{1,0:T(8,128)} %copy-done.18) | copy-start | bytes 1572868
  113.7 12.6 %copy-start.21 = (f32[128,1024]{1,0:T(8,128)S(1)}, f32[128,1024]{1,0:T(8,128)}, u32[]{:S(2)}) copy-start(f32[128,1024]{1,0:T(8,128)} %copy-done.20) | copy-start | bytes 1572868
  115.3 12.2 %copy-start.22 = (f32[256,512]{1,0:T(8,128)}, f32[256,512]{1,0:T(8,128)S(1)}, u32[]{:S(2)}) copy-start(f32[256,512]{1,0:T(8,128)S(1)} %get-tuple-element.136.refs_0_) | copy-start | bytes 1572868
  115.3 12.2 %copy-start.24 = (f32[256,512]{1,0:T(8,128)}, f32[256,512]{1,0:T(8,128)S(1)}, u32[]{:S(2)}) copy-start(f32[256,512]{1,0:T(8,128)S(1)} %get-tuple-element.138.refs_2_) | copy-start | bytes 1572868
  115.3 15.5 %collective-permute-start.23 = (bf16[256,512]{1,0:T(8,128)(2,1)S(1)}, bf16[256,512]{1,0:T(8,128)(2,1)S(1)}, u32[]{:S(2)}, u32[]{:S(2)}) collective-permute-start(bf16[256,512]{1,0:T(8,128)(2,1)S(1)} %get-tuple-element.137), channel_id=1, source_target_pairs={{0,16},{8,24},{16,0},{24,8},{1,17},{9,25},{17,1},{25,9},{2,18},{10... | collective-permute-start | bytes 786440 | tf_op jit(solution)/shard_map/ppermute | solution.py:463
  124.9 6.4 %collective-permute-start.24 = (bf16[256,512]{1,0:T(8,128)(2,1)S(1)}, bf16[256,512]{1,0:T(8,128)(2,1)S(1)}, u32[]{:S(2)}, u32[]{:S(2)}) collective-permute-start(bf16[256,512]{1,0:T(8,128)(2,1)S(1)} %get-tuple-element.139), channel_id=1, source_target_pairs={{0,8},{8,0},{16,24},{24,16},{1,9},{9,1},{17,25},{25,17},{2,10},{10... | collective-permute-start | bytes 786440 | tf_op jit(solution)/shard_map/ppermute | solution.py:459
  127.5 2.5 %copy-start.9 = (s32[128,8]{0,1:T(8,128)S(1)}, s32[128,8]{0,1:T(8,128)}, u32[]{:S(2)}) copy-start(s32[128,8]{0,1:T(8,128)} %param.8) | copy-start | bytes 12292
  130.0 1.2 copy-start.23
  130.0 1.3 copy-start.25

commit v2 on v1

--- a/solution.py
+++ b/solution.py
@@ -58,30 +58,46 @@
     extra = extra_rows(e_total, T, D)
     per = D // T
 
-    def body(tok_ref, routes_ref, weights_ref, out_ref, buf):
+    def body(tok_hbm, routes_hbm, weights_hbm, out_ref, routes_ref, weights_ref, buf, sems):
+        copies = [
+            pltpu.make_async_copy(routes_hbm, routes_ref, sems.at[0]),
+            pltpu.make_async_copy(weights_hbm, weights_ref, sems.at[1]),
+            pltpu.make_async_copy(tok_hbm, out_ref.at[pl.ds(0, T)], sems.at[2]),
+        ]
+        for c in copies:
+            c.start()
+        buf[...] = jnp.zeros_like(buf)
         expert = lax.broadcasted_iota(jnp.int32, (e_total, T), 0)
         dense = jnp.zeros((e_total, T), F32)
+        copies[0].wait()
+        copies[1].wait()
         for k in range(routes_t.shape[0]):
             dense = dense + jnp.where(
                 routes_ref[k : k + 1, :] == expert, weights_ref[k : k + 1, :], 0.0
             )
-        buf[...] = jnp.zeros_like(buf)
         for p, part in enumerate(thirds(dense)):
             for i in range(e_total):
                 row = p * (e_total // per) + i // per
                 at = slice(i % per * T, (i % per + 1) * T)
                 buf[row : row + 1, at] = part[i : i + 1, :]
-        out_ref[:T, :] = tok_ref[...]
         out_ref[T:, :] = buf[...].astype(BF)
-
-    return on_chip(
+        copies[2].wait()
+
+    return pl.pallas_call(
         body,
-        [tokens, routes_t, weights_t],
-        [jax.ShapeDtypeStruct((T + extra, D), BF)],
-        0,
-        "pack_tokens",
-        scratch=[pltpu.VMEM((extra, D), F32)],
-    )[0]
+        in_specs=[pl.BlockSpec(memory_space=pl.ANY)] * 3,
+        out_specs=VMEM,
+        out_shape=jax.ShapeDtypeStruct((T + extra, D), BF),
+        scratch_shapes=[
+            pltpu.VMEM(routes_t.shape, jnp.int32),
+            pltpu.VMEM(weights_t.shape, F32),
+            pltpu.VMEM((extra, D), F32),
+            pltpu.SemaphoreType.DMA((3,)),
+        ],
+        compiler_params=pltpu.CompilerParams(vmem_limit_bytes=60 * 2**20),
+        cost_estimate=pl.CostEstimate(flops=10**10, bytes_accessed=2**20, transcendentals=0),
+        name="pack_tokens",
+    )(tokens, routes_t, weights_t)
 
 
 def collect(blocks, *earlier):
@@ -325,6 +341,36 @@
     return [outs[j * n : (j + 1) * n] for j in range(E)], outs[-1]
 
 
+def collect_relayed(place, own, two, up, down, relayed, *earlier):
+    h = own.shape[0]
+
+    def body(place_ref, own_ref, two_ref, up_ref, down_ref, relayed_ref, *refs):
+        out_ref = refs[-1]
+        z = place_ref[2] // 2
+        out_ref[:h, :] = own_ref[...]
+        out_ref[2 * h : 3 * h, :] = two_ref[...]
+
+        @pl.when(z == 0)
+        def _():
+            out_ref[h : 2 * h, :] = relayed_ref[...]
+
+        @pl.when(z != 0)
+        def _():
+            out_ref[h : 2 * h, :] = up_ref[...]
+
+        @pl.when(z == 3)
+        def _():
+            out_ref[3 * h :, :] = relayed_ref[...]
+
+        @pl.when(z != 3)
+        def _():
+            out_ref[3 * h :, :] = down_ref[...]
+
+    shape = jax.ShapeDtypeStruct((4 * h, own.shape[1]), BF)
+    operands = [place, own, two, up, down, relayed, *earlier]
+    return on_chip(body, operands, [shape], 0, "collect", scalars=1)[0]
+
+
 def relay(totals, name, *earlier):
     sent = [v for total in totals for v in total[1:]]
 
@@ -465,8 +511,21 @@
     def gather_near(v):
         return [v] + [move_z(v, k) for k in range(1, nz)]
 
+    def chip_pairs(pairs):
+        return [(2 * a + c, 2 * b + c) for a, b in pairs for c in range(2)]
+
+    def near_rows(v, *earlier):
+        if nz != 4:
+            return collect(gather_near(v), *earlier)
+        send = lambda u, pairs: lax.ppermute(u, "expert", chip_pairs(pairs))
+        two = move_z(v, 2)
+        up = send(v, [(0, 1), (1, 2), (2, 3)])
+        down = send(v, [(1, 0), (2, 1), (3, 2)])
+        relayed = send(two, [(2, 3), (1, 0)])
+        return collect_relayed(place, v, two, up, down, relayed, *earlier)
+
     packed = pack_tokens(tokens, routes.T, route_weights.T, e_total)
-    token_near = collect(gather_near(packed))
+    token_near = near_rows(packed)
     cot_blocks = gather_near(cotangent)
     token_far = swap(token_near)
     *saved, hw_t, tok_t, out_near, out_far, forward_done = forward(
@@ -513,7 +572,7 @@
     gate_got = send_first(gate_part)
     out_parts = split_sides(out_near, out_far, nz, "out_sides", down_done)
     out_got = [move_z(out_parts[k], -k) for k in range(1, nz)]
-    down_totals, down_mid = add_first(down_part, down_got, n, "down_first", gate_done)
+    down_totals, down_mid = add_first(down_part, down_got, n, "down_first", gate_done, out_got[0])
     tg_near, tg_far = token_partials(
         place,
         [gg0, gg1],
@@ -526,12 +585,12 @@
         down_mid,
     )
     tg_far = swap(tg_far)
-    layer_out, out_done = sum_rows(out_parts[0], out_got, "out_rows", tg_near[:8, :128])
     up_part, up_done = weight_partials(
-        place, tok_t, [ug0, ug1], E, n, D, "up_partials", tg_near[:8, :128], out_done
+        place, tok_t, [ug0, ug1], E, n, D, "up_partials", tg_near[:8, :128]
     )
     up_got = send_first(up_part)
-    tg_parts, tg_done = add_sides(place, tg_near, tg_far, nz, "token_sides", up_done)
+    layer_out, out_done = sum_rows(out_parts[0], out_got, "out_rows", up_done)
+    tg_parts, tg_done = add_sides(place, tg_near, tg_far, nz, "token_sides", out_done)
     tg_got = send_home(tg_parts)
     down_totals, down_mid = relay(down_totals, "down_relay", tg_done)
     down_got = send_second(down_totals)

time: 133 us -> 129 us (0.970)
  waiting for transfers between devices: 47.3 us -> 37.8 us
  starting transfers between devices: 34.8 us -> 43 us
  local copies, waits for them, and re-layouts: 10.5 us -> 7.41 us
    ppermute x9 -> x7, waiting for transfers between devices: 32.5 us -> 16.6 us  [move_z(): return lax.ppermute(v, 'expert', pairs)]
    ppermute x0 -> x3, waiting for transfers between devices: none -> 7.49 us  [near_rows(): send = lambda u, pairs: lax.ppermute(u, 'expert', chip_pairs(pairs))]
    ppermute x0 -> x3, starting transfers between devices: none -> 7.12 us  [near_rows(): send = lambda u, pairs: lax.ppermute(u, 'expert', chip_pairs(pairs))]
    all_to_all x1, waiting for transfers between devices: 1.44 us -> 4.98 us  [send_home(): lax.all_to_all(parts, 'expert', split_axis=0, concat_axis=0, tiled=True,...]
    unnamed x56 -> x44, local copies, waits for them, and re-layouts: 10.5 us -> 7.41 us
    ppermute x6, waiting for transfers between devices: 10.8 us -> 8.37 us  [move_y(): return lax.ppermute(v, 'dp', pairs)]
    ppermute x6, waiting for transfers between devices: 2.12 us -> 0.02 us  [move_x(): return lax.ppermute(v, 'dp', pairs)]
    pallas_call x0 -> x1, Pallas kernels: none -> 1.72 us  [pack_tokens(): pl.pallas_call(body, in_specs=[pl.BlockSpec(memory_space=pl.ANY)] * 3, ou...]
  transfers between devices with their start and end apart: 26 -> 27, of which waited for: 11 -> 9; matrix products, arithmetic and copies ran while one was open for 0% -> 0% of each run, Pallas kernels for 27% -> 28%
where the time goes in v2:
time: 129 us; the launch traced here: 128 us
  starting transfers between devices  43 us (33%)
  Pallas kernels  39.2 us (30%)
  waiting for transfers between devices  37.8 us (29%)
  local copies, waits for them, and re-layouts  7.41 us (6%)
    pallas_call x20, Pallas kernels, on_chip(): pl.pallas_call(body, in_specs=[SMEM] * scalars + [VMEM] * (len(operands)...  37.5 us
    ppermute x7, starting transfers between devices, move_z(): return lax.ppermute(v, 'expert', pairs)  18.9 us
    ppermute x7, waiting for transfers between devices, move_z(): return lax.ppermute(v, 'expert', pairs)  16.6 us
    ppermute x6, waiting for transfers between devices, move_y(): return lax.ppermute(v, 'dp', pairs)  8.37 us
    ppermute x3, waiting for transfers between devices, near_rows(): send = lambda u, pairs: lax.ppermute(u, 'expert', chip_pairs(pairs))  7.49 us
    unnamed x44, local copies, waits for them, and re-layouts  7.41 us
    ppermute x3, starting transfers between devices, near_rows(): send = lambda u, pairs: lax.ppermute(u, 'expert', chip_pairs(pairs))  7.12 us
    ppermute x6, starting transfers between devices, move_x(): return lax.ppermute(v, 'dp', pairs)  6.3 us
  transfers between devices with their start and end apart: 27, of which 9 were waited for; matrix products, arithmetic and copies ran while one was open for 0% of the time, Pallas kernels for 28%

profile of v2, /device:TPU:0, one launch (start us, length us, event | category | flops | bytes accessed | tf_op | source)
XLA Modules:
  0.0 128.4 jit_solution(4210547755733643838)
XLA Ops:
  0.6 1.7 %pack_tokens.1.own_ref = bf16[136,1024]{1,0:T(8,128)(2,1)} custom-call(bf16[128,1024]{1,0:T(8,128)(2,1)} %tok_hbm.1, s32[8,128]{1,0:T(8,128)} %bitcast.19, f32[8,128]{1,0:T(8,128)} %bitcast.21), custom_call_target="tpu_custom_call" | custom-call | flops 10000000000 | bytes 1048576 | tf_op jit(solution)/shard_map/pack_tokens/pallas_call | solution.py:86
  2.4 4.1 %collective-permute-start = (bf16[136,1024]{1,0:T(8,128)(2,1)}, bf16[136,1024]{1,0:T(8,128)(2,1)S(1)}, u32[]{:S(2)}, u32[]{:S(2)}) collective-permute-start(bf16[136,1024]{1,0:T(8,128)(2,1)} %pack_tokens.1.own_ref), channel_id=1, source_target_pairs={{0,4},{1,5},{2,6},{3,7},{4,0},{5,1},{6,2},{7,3},{8,12},{9,13},{10,... | collective-permute-start | bytes 835592 | tf_op jit(solution)/shard_map/ppermute | solution.py:501
  6.5 1.3 collective-permute-start.2
  7.7 4.6 %collective-permute-start.1 = (bf16[136,1024]{1,0:T(8,128)(2,1)}, bf16[136,1024]{1,0:T(8,128)(2,1)S(1)}, u32[]{:S(2)}, u32[]{:S(2)}) collective-permute-start(bf16[136,1024]{1,0:T(8,128)(2,1)} %pack_tokens.1.own_ref), channel_id=1, source_target_pairs={{0,2},{1,3},{2,4},{3,5},{4,6},{5,7},{8,10},{9,11},{10,12},{11,13},... | collective-permute-start | bytes 835592 | tf_op jit(solution)/shard_map/ppermute | solution.py:520
  12.3 7.9 %collective-permute-done.two_ref = bf16[136,1024]{1,0:T(8,128)(2,1)S(1)} collective-permute-done((bf16[136,1024]{1,0:T(8,128)(2,1)}, bf16[136,1024]{1,0:T(8,128)(2,1)S(1)}, u32[]{:S(2)}, u32[]{:S(2)}) %collective-permute-start) | collective-permute-done | bytes 278560 | tf_op jit(solution)/shard_map/ppermute | solution.py:501
  20.2 1.3 collective-permute-start.3
  21.5 0.1 pad_add_fusion.place_ref.refs_0_
  21.6 7.5 %collective-permute-done.3.relayed_ref = bf16[136,1024]{1,0:T(8,128)(2,1)S(1)} collective-permute-done((bf16[136,1024]{1,0:T(8,128)(2,1)S(1)}, bf16[136,1024]{1,0:T(8,128)(2,1)S(1)}, u32[]{:S(2)}, u32[]{:S(2)}) %collective-permute-start.3) | collective-permute-done | bytes 278560 | tf_op jit(solution)/shard_map/ppermute | solution.py:520
  29.1 1.0 copy-done.3
  30.0 0.6 collect.2.near_in
  30.7 0.1 collective-permute-start.4
  30.7 0.2 copy-done.4
  31.0 2.4 %collective-permute-start.7 = (bf16[128,1024]{1,0:T(8,128)(2,1)S(1)}, bf16[128,1024]{1,0:T(8,128)(2,1)S(1)}, u32[]{:S(2)}, u32[]{:S(2)}) collective-permute-start(bf16[128,1024]{1,0:T(8,128)(2,1)S(1)} %copy-done.4), channel_id=1, source_target_pairs={{0,4},{1,5},{2,6},{3,7},{4,0},{5,1},{6,2},{7,3},{8,12},{9,13},{10,... | collective-permute-start | bytes 786440 | tf_op jit(solution)/shard_map/ppermute | solution.py:501
  33.3 2.5 %collective-permute-start.6 = (bf16[128,1024]{1,0:T(8,128)(2,1)S(1)}, bf16[128,1024]{1,0:T(8,128)(2,1)S(1)}, u32[]{:S(2)}, u32[]{:S(2)}) collective-permute-start(bf16[128,1024]{1,0:T(8,128)(2,1)S(1)} %copy-done.4), channel_id=1, source_target_pairs={{0,2},{1,3},{2,4},{3,5},{4,6},{5,7},{6,0},{7,1},{8,10},{9,11},{10,... | collective-permute-start | bytes 786440 | tf_op jit(solution)/shard_map/ppermute | solution.py:501
  35.8 1.3 %collective-permute-start.8 = (bf16[128,1024]{1,0:T(8,128)(2,1)S(1)}, bf16[128,1024]{1,0:T(8,128)(2,1)S(1)}, u32[]{:S(2)}, u32[]{:S(2)}) collective-permute-start(bf16[128,1024]{1,0:T(8,128)(2,1)S(1)} %copy-done.4), channel_id=1, source_target_pairs={{0,6},{1,7},{2,0},{3,1},{4,2},{5,3},{6,4},{7,5},{8,14},{9,15},{10,... | collective-permute-start | bytes 786440 | tf_op jit(solution)/shard_map/ppermute | solution.py:501
  37.2 9.4 %forward.1 = (bf16[512,1024]{1,0:T(8,128)(2,1)S(1)}, bf16[512,1024]{1,0:T(8,128)(2,1)S(1)}, bf16[512,1024]{1,0:T(8,128)(2,1)S(1)}, bf16[512,1024]{1,0:T(8,128)(2...) custom-call(s32[3]{0:T(128)S(1)} %pad_add_fusion.place_ref.refs_0_, ...), custom_call_target="tpu_custom_call" | custom-call | flops 10000000000 | bytes 22155276 | tf_op jit(solution)/shard_map/forward/pallas_call | solution.py:32
  46.6 5.7 %collective-permute-done.7.refs_2_ = bf16[128,1024]{1,0:T(8,128)(2,1)S(1)} collective-permute-done((bf16[128,1024]{1,0:T(8,128)(2,1)S(1)}, bf16[128,1024]{1,0:T(8,128)(2,1)S(1)}, u32[]{:S(2)}, u32[]{:S(2)}) %collective-permute-start.7) | collective-permute-done | bytes 262176 | tf_op jit(solution)/shard_map/ppermute | solution.py:501
  52.3 0.9 collective-permute-done.8.refs_3_
  53.4 0.5 collective-permute-start.5
  53.9 1.8 %hidden_grads.2 = (bf16[512,1024]{1,0:T(8,128)(2,1)S(1)}, bf16[512,1024]{1,0:T(8,128)(2,1)S(1)}, f32[512,128]{1,0:T(8,128)S(1)}, f32[8,128]{1,0:T(8,128)S(1)}) custom-call(bf16[512,1024]{1,0:T(8,128)(2,1)S(1)} %collect.3.refs_0_, bf16[512,1024]{1,0:T(8,128)(2,1)S(1)} %get-tuple-element.79.refs_1_, bf16[512,1024]{1,0:T(8,128)(2,1)S(1)} %get-tuple-element.80.refs_2_, ...), custom_call_target="tpu_custom_call" | custom-call | flops 10000000000 | bytes 8654848 | tf_op jit(solution)/shard_map/hidden_grads/pallas_call | solution.py:32
  55.6 0.4 collective-permute-done.9.refs_1_.refs_0_
  56.0 2.9 %down_partials.1 = (bf16[1,2,128,1024]{3,2,1,0:T(8,128)(2,1)S(1)}, f32[2,128,1024]{2,1,0:T(8,128)S(1)}, bf16[1,2,128,1024]{3,2,1,0:T(8,128)(2,1)S(1)}, f32[2,128,1024]{2,1,0:T(8,128)S(1)}, f32[8,128]{1,0:T(8,128)S(1)}) custom-call(s32[3]{0:T(128)S(1)} %pad_add_fusion.place_ref.refs_0_, bf16[1024,1024]{1,0:T(8,128)(2,1)S(1)} %get-tuple-element.77.left_ref, ...), custom_call_target="tpu_custom_call" | custom-call | flops 10000000000 | bytes 7348236 | tf_op jit(solution)/shard_map/down_partials/pallas_call | solution.py:32
  58.9 1.4 %collective-permute-start.13 = (bf16[2,128,1024]{2,1,0:T(8,128)(2,1)S(1)}, bf16[2,128,1024]{2,1,0:T(8,128)(2,1)S(1)}, u32[]{:S(2)}, u32[]{:S(2)}) collective-permute-start(bf16[2,128,1024]{2,1,0:T(8,128)(2,1)S(1)} %bitcast.18), channel_id=1, source_target_pairs={{0,8},{8,0},{16,24},{24,16},{1,9},{9,1},{17,25},{25,17},{2,10},{10... | collective-permute-start | bytes 1572872 | tf_op jit(solution)/shard_map/ppermute | solution.py:505
  60.4 1.5 %collective-permute-start.14 = (bf16[2,128,1024]{2,1,0:T(8,128)(2,1)S(1)}, bf16[2,128,1024]{2,1,0:T(8,128)(2,1)S(1)}, u32[]{:S(2)}, u32[]{:S(2)}) collective-permute-start(bf16[2,128,1024]{2,1,0:T(8,128)(2,1)S(1)} %bitcast.17), channel_id=1, source_target_pairs={{0,16},{8,24},{16,0},{24,8},{1,17},{9,25},{17,1},{25,9},{2,18},{10... | collective-permute-start | bytes 1572872 | tf_op jit(solution)/shard_map/ppermute | solution.py:509
  61.9 0.2 out_sides.1
  62.1 1.9 %collective-permute-start.10 = (bf16[128,1024]{1,0:T(8,128)(2,1)S(1)}, bf16[128,1024]{1,0:T(8,128)(2,1)S(1)}, u32[]{:S(2)}, u32[]{:S(2)}) collective-permute-start(bf16[128,1024]{1,0:T(8,128)(2,1)S(1)} %get-tuple-element.85), channel_id=1, source_target_pairs={{0,6},{1,7},{2,0},{3,1},{4,2},{5,3},{6,4},{7,5},{8,14},{9,15},{10,... | collective-permute-start | bytes 786440 | tf_op jit(solution)/shard_map/ppermute | solution.py:501
  64.0 4.7 %collective-permute-start.11 = (bf16[128,1024]{1,0:T(8,128)(2,1)S(1)}, bf16[128,1024]{1,0:T(8,128)(2,1)S(1)}, u32[]{:S(2)}, u32[]{:S(2)}) collective-permute-start(bf16[128,1024]{1,0:T(8,128)(2,1)S(1)} %get-tuple-element.86), channel_id=1, source_target_pairs={{0,4},{1,5},{2,6},{3,7},{4,0},{5,1},{6,2},{7,3},{8,12},{9,13},{10,... | collective-permute-start | bytes 786440 | tf_op jit(solution)/shard_map/ppermute | solution.py:501
  68.7 1.9 %collective-permute-start.12 = (bf16[128,1024]{1,0:T(8,128)(2,1)S(1)}, bf16[128,1024]{1,0:T(8,128)(2,1)S(1)}, u32[]{:S(2)}, u32[]{:S(2)}) collective-permute-start(bf16[128,1024]{1,0:T(8,128)(2,1)S(1)} %get-tuple-element.87), channel_id=1, source_target_pairs={{0,2},{1,3},{2,4},{3,5},{4,6},{5,7},{6,0},{7,1},{8,10},{9,11},{10,... | collective-permute-start | bytes 786440 | tf_op jit(solution)/shard_map/ppermute | solution.py:501
  70.7 2.3 %hidden_grads.3 = (bf16[512,1024]{1,0:T(8,128)(2,1)S(1)}, bf16[512,1024]{1,0:T(8,128)(2,1)S(1)}, f32[512,128]{1,0:T(8,128)S(1)}, f32[8,128]{1,0:T(8,128)}) custom-call(bf16[512,1024]{1,0:T(8,128)(2,1)S(1)} %collective-permute-done.9.refs_1_.refs_0_, bf16[512,1024]{1,0:T(8,128)(2,1)S(1)} %get-tuple-element.90.refs_1_, ...), custom_call_target="tpu_custom_call" | custom-call | flops 10000000000 | bytes 8658944 | tf_op jit(solution)/shard_map/hidden_grads/pallas_call | solution.py:32
  72.9 2.9 %gate_partials.1 = (bf16[1,2,256,512]{3,2,1,0:T(8,128)(2,1)S(1)}, f32[2,256,512]{2,1,0:T(8,128)S(1)}, bf16[1,2,256,512]{3,2,1,0:T(8,128)(2,1)S(1)}, f32[2,256,512]{2,1,0:T(8,128)S(1)}, f32[8,128]{1,0:T(8,128)S(1)}) custom-call(s32[3]{0:T(128)S(1)} %pad_add_fusion.place_ref.refs_0_, bf16[1024,1024]{1,0:T(8,128)(2,1)S(1)} %get-tuple-element.88.left_ref, ...), custom_call_target="tpu_custom_call" | custom-call | flops 10000000000 | bytes 7344140 | tf_op jit(solution)/shard_map/gate_partials/pallas_call | solution.py:32
  75.8 1.0 copy-done.12
  76.8 0.5 collective-permute-start.16
  77.4 0.5 collective-permute-start.17
  77.9 0.2 down_first.1
  78.1 0.8 copy-done.14
  78.8 0.8 copy-done.16
  79.6 5.1 %token_partials.1 = (f32[544,1024]{1,0:T(8,128)S(1)}, bf16[544,1024]{1,0:T(8,128)(2,1)S(1)}) custom-call(s32[3]{0:T(128)S(1)} %pad_add_fusion.place_ref.refs_0_, bf16[512,1024]{1,0:T(8,128)(2,1)S(1)} %get-tuple-element.94.refs_0_.refs_1_, bf16[512,1024]{1,0:T(8,128)(2,1)S(1)} %get-tuple-element.95.refs_1_.refs_2_, ...), custom_call_target="tpu_custom_call" | custom-call | flops 10000000000 | bytes 12259340 | tf_op jit(solution)/shard_map/token_partials/pallas_call | solution.py:32
  84.8 3.6 %up_partials.1 = (bf16[1,2,256,512]{3,2,1,0:T(8,128)(2,1)}, f32[2,256,512]{2,1,0:T(8,128)S(1)}, bf16[1,2,256,512]{3,2,1,0:T(8,128)(2,1)}, f32[2,256,512]{2,1,0:T(8,128)S(1)}, f32[8,128]{1,0:T(8,128)S(1)}) custom-call(s32[3]{0:T(128)S(1)} %pad_add_fusion.place_ref.refs_0_, bf16[1024,1024]{1,0:T(8,128)(2,1)S(1)} %get-tuple-element.88.left_ref, ...), custom_call_target="tpu_custom_call" | custom-call | flops 10000000000 | bytes 7348236 | tf_op jit(solution)/shard_map/up_partials/pallas_call | solution.py:32
  88.4 1.0 copy-done.8
  89.4 2.1 %collective-permute-done.11.refs_2_ = bf16[128,1024]{1,0:T(8,128)(2,1)S(1)} collective-permute-done((bf16[128,1024]{1,0:T(8,128)(2,1)S(1)}, bf16[128,1024]{1,0:T(8,128)(2,1)S(1)}, u32[]{:S(2)}, u32[]{:S(2)}) %collective-permute-start.11) | collective-permute-done | bytes 262176 | tf_op jit(solution)/shard_map/ppermute | solution.py:501
  91.5 0.5 collective-permute-start.22
  92.1 0.5 collective-permute-start.23
  92.6 0.8 out_rows.1
  93.4 1.8 %token_sides.1 = (bf16[544,1024]{1,0:T(8,128)(2,1)}, f32[8,128]{1,0:T(8,128)S(1)}) custom-call(s32[3]{0:T(128)S(1)} %pad_add_fusion.place_ref.refs_0_, f32[544,1024]{1,0:T(8,128)S(1)} %get-tuple-element.104.near_ref, bf16[544,1024]{1,0:T(8,128)(2,1)S(1)} %collective-permute-done.15.far_ref, f32[8,128]{1,0:T(8,128)S(1)} %get-tuple-element.108.refs_0_), custom_call_target="tpu_custom_call" | custom-call | flops 10000000000 | bytes 4464652 | tf_op jit(solution)/shard_map/token_sides/pallas_call | solution.py:32
  95.2 3.9 %all-to-all-start = ((bf16[4,136,1024]{2,1,0:T(8,128)(2,1)}), bf16[4,136,1024]{2,1,0:T(8,128)(2,1)S(1)}, u32[]{:S(2)}, u32[]{:S(2)}) async-start(bf16[4,136,1024]{2,1,0:T(8,128)(2,1)} %bitcast.7), calls=%async_computation | async-start | bytes 2228224 | tf_op jit(solution)/shard_map/all_to_all | solution.py:556
  99.1 0.9 copy-done.21
  100.1 1.2 copy-done.11
  101.3 0.3 copy-done.13
  101.6 0.2 gate_first.1
  101.8 1.6 %collective-permute-start.18 = (bf16[256,512]{1,0:T(8,128)(2,1)S(1)}, bf16[256,512]{1,0:T(8,128)(2,1)S(1)}, u32[]{:S(2)}, u32[]{:S(2)}) collective-permute-start(bf16[256,512]{1,0:T(8,128)(2,1)S(1)} %get-tuple-element.121), channel_id=1, source_target_pairs={{0,16},{8,24},{16,0},{24,8},{1,17},{9,25},{17,1},{25,9},{2,18},{10... | collective-permute-start | bytes 786440 | tf_op jit(solution)/shard_map/ppermute | solution.py:509
  103.4 1.1 collective-permute-start.19
  104.5 0.5 collective-permute-start.20
  105.0 0.9 collective-permute-start.21
  105.9 0.3 collective-permute-done.23.refs_3_
  106.2 1.5 %up_first.1 = (f32[256,512]{1,0:T(8,128)S(1)}, bf16[256,512]{1,0:T(8,128)(2,1)S(1)}, f32[256,512]{1,0:T(8,128)S(1)}, bf16[256,512]{1,0:T(8,128)(2,1)S(1)}, f32[8,128]{1,0:T(8,128)S(1)}) custom-call(f32[2,256,512]{2,1,0:T(8,128)S(1)} %copy-done.7, bf16[2,256,512]{2,1,0:T(8,128)(2,1)} %collective-permute-done.22.refs_1_, f32[2,256,512]{2,1,0:T(8,128)S(1)} %copy-done.9, ...), custom_call_target="tpu_custom_call" | custom-call | flops 10000000000 | bytes 4726784 | tf_op jit(solution)/shard_map/up_first/pallas_call | solution.py:32
  107.8 1.5 %collective-permute-start.24 = (bf16[256,512]{1,0:T(8,128)(2,1)S(1)}, bf16[256,512]{1,0:T(8,128)(2,1)S(1)}, u32[]{:S(2)}, u32[]{:S(2)}) collective-permute-start(bf16[256,512]{1,0:T(8,128)(2,1)S(1)} %get-tuple-element.137), channel_id=1, source_target_pairs={{0,16},{8,24},{16,0},{24,8},{1,17},{9,25},{17,1},{25,9},{2,18},{10... | collective-permute-start | bytes 786440 | tf_op jit(solution)/shard_map/ppermute | solution.py:509
  109.3 8.1 %collective-permute-done.20.refs_1_ = bf16[128,1024]{1,0:T(8,128)(2,1)S(1)} collective-permute-done((bf16[128,1024]{1,0:T(8,128)(2,1)S(1)}, bf16[128,1024]{1,0:T(8,128)(2,1)S(1)}, u32[]{:S(2)}, u32[]{:S(2)}) %collective-permute-start.20) | collective-permute-done | bytes 262176 | tf_op jit(solution)/shard_map/ppermute | solution.py:509
  117.4 1.8 %collective-permute-start.25 = (bf16[256,512]{1,0:T(8,128)(2,1)S(1)}, bf16[256,512]{1,0:T(8,128)(2,1)S(1)}, u32[]{:S(2)}, u32[]{:S(2)}) collective-permute-start(bf16[256,512]{1,0:T(8,128)(2,1)S(1)} %get-tuple-element.139), channel_id=1, source_target_pairs={{0,8},{8,0},{16,24},{24,16},{1,9},{9,1},{17,25},{25,17},{2,10},{10... | collective-permute-start | bytes 786440 | tf_op jit(solution)/shard_map/ppermute | solution.py:505
  119.1 1.1 down_second.1
  120.2 1.1 gate_second.1
  121.3 5.0 %all-to-all-done = bf16[4,136,1024]{2,1,0:T(8,128)(2,1)S(1)} async-done(((bf16[4,136,1024]{2,1,0:T(8,128)(2,1)}), bf16[4,136,1024]{2,1,0:T(8,128)(2,1)S(1)}, u32[]{:S(2)}, u32[]{:S(2)}) %all-to-all-start) | async-done | bytes 1114144 | tf_op jit(solution)/shard_map/all_to_all | solution.py:556
  126.3 0.8 token_rows.1
  127.2 0.2 copy-done.19
  127.4 1.1 up_second.1
  (57 shorter events, 0.4 us)
Async XLA Ops:
  2.4 17.8 %collective-permute-start = (bf16[136,1024]{1,0:T(8,128)(2,1)}, bf16[136,1024]{1,0:T(8,128)(2,1)S(1)}, u32[]{:S(2)}, u32[]{:S(2)}) collective-permute-start(bf16[136,1024]{1,0:T(8,128)(2,1)} %pack_tokens.1.own_ref), channel_id=1, source_target_pairs={{0,4},{1,5},{2,6},{3,7},{4,0},{5,1},{6,2},{7,3},{8,12},{9,13},{10,... | collective-permute-start | bytes 835592 | tf_op jit(solution)/shard_map/ppermute | solution.py:501
  6.5 15.1 %collective-permute-start.2 = (bf16[136,1024]{1,0:T(8,128)(2,1)}, bf16[136,1024]{1,0:T(8,128)(2,1)S(1)}, u32[]{:S(2)}, u32[]{:S(2)}) collective-permute-start(bf16[136,1024]{1,0:T(8,128)(2,1)} %pack_tokens.1.own_ref), channel_id=1, source_target_pairs={{2,0},{3,1},{4,2},{5,3},{6,4},{7,5},{10,8},{11,9},{12,10},{13,11},... | collective-permute-start | bytes 835592 | tf_op jit(solution)/shard_map/ppermute | solution.py:520
  7.7 13.8 %collective-permute-start.1 = (bf16[136,1024]{1,0:T(8,128)(2,1)}, bf16[136,1024]{1,0:T(8,128)(2,1)S(1)}, u32[]{:S(2)}, u32[]{:S(2)}) collective-permute-start(bf16[136,1024]{1,0:T(8,128)(2,1)} %pack_tokens.1.own_ref), channel_id=1, source_target_pairs={{0,2},{1,3},{2,4},{3,5},{4,6},{5,7},{8,10},{9,11},{10,12},{11,13},... | collective-permute-start | bytes 835592 | tf_op jit(solution)/shard_map/ppermute | solution.py:520
  20.2 8.9 %collective-permute-start.3 = (bf16[136,1024]{1,0:T(8,128)(2,1)S(1)}, bf16[136,1024]{1,0:T(8,128)(2,1)S(1)}, u32[]{:S(2)}, u32[]{:S(2)}) collective-permute-start(bf16[136,1024]{1,0:T(8,128)(2,1)S(1)} %collective-permute-done.two_ref), channel_id=1, source_target_pairs={{4,6},{5,7},{2,0},{3,1},{12,14},{13,15},{10,8},{11,9},{20,22},{21,... | collective-permute-start | bytes 835592 | tf_op jit(solution)/shard_map/ppermute | solution.py:520
  21.6 15.6 %copy-start = (bf16[2,512,1024]{2,1,0:T(8,128)(2,1)S(1)}, bf16[2,512,1024]{2,1,0:T(8,128)(2,1)}, u32[]{:S(2)}) copy-start(bf16[2,512,1024]{2,1,0:T(8,128)(2,1)} %refs_4_.3) | copy-start | bytes 6291460
  21.6 15.6 %copy-start.1 = (bf16[2,1024,512]{2,1,0:T(8,128)(2,1)S(1)}, bf16[2,1024,512]{2,1,0:T(8,128)(2,1)}, u32[]{:S(2)}) copy-start(bf16[2,1024,512]{2,1,0:T(8,128)(2,1)} %refs_7_.1) | copy-start | bytes 6291460
  21.6 15.6 %copy-start.2 = (bf16[2,1024,512]{2,1,0:T(8,128)(2,1)S(1)}, bf16[2,1024,512]{2,1,0:T(8,128)(2,1)}, u32[]{:S(2)}) copy-start(bf16[2,1024,512]{2,1,0:T(8,128)(2,1)} %refs_8_.1) | copy-start | bytes 6291460
  29.1 1.0 copy-start.3
  30.0 0.9 copy-start.4
  30.7 6.5 %collective-permute-start.4 = (bf16[544,1024]{1,0:T(8,128)(2,1)S(1)}, bf16[544,1024]{1,0:T(8,128)(2,1)S(1)}, u32[]{:S(2)}, u32[]{:S(2)}) collective-permute-start(bf16[544,1024]{1,0:T(8,128)(2,1)S(1)} %collect.2.near_in), channel_id=1, source_target_pairs={{0,1},{1,0},{2,3},{3,2},{4,5},{5,4},{6,7},{7,6},{8,9},{9,8},{10,11... | collective-permute-start | bytes 3342344 | tf_op jit(solution)/shard_map/ppermute | solution.py:497
  31.0 21.3 %collective-permute-start.7 = (bf16[128,1024]{1,0:T(8,128)(2,1)S(1)}, bf16[128,1024]{1,0:T(8,128)(2,1)S(1)}, u32[]{:S(2)}, u32[]{:S(2)}) collective-permute-start(bf16[128,1024]{1,0:T(8,128)(2,1)S(1)} %copy-done.4), channel_id=1, source_target_pairs={{0,4},{1,5},{2,6},{3,7},{4,0},{5,1},{6,2},{7,3},{8,12},{9,13},{10,... | collective-permute-start | bytes 786440 | tf_op jit(solution)/shard_map/ppermute | solution.py:501
  33.3 19.0 %collective-permute-start.6 = (bf16[128,1024]{1,0:T(8,128)(2,1)S(1)}, bf16[128,1024]{1,0:T(8,128)(2,1)S(1)}, u32[]{:S(2)}, u32[]{:S(2)}) collective-permute-start(bf16[128,1024]{1,0:T(8,128)(2,1)S(1)} %copy-done.4), channel_id=1, source_target_pairs={{0,2},{1,3},{2,4},{3,5},{4,6},{5,7},{6,0},{7,1},{8,10},{9,11},{10,... | collective-permute-start | bytes 786440 | tf_op jit(solution)/shard_map/ppermute | solution.py:501
  35.8 17.4 %collective-permute-start.8 = (bf16[128,1024]{1,0:T(8,128)(2,1)S(1)}, bf16[128,1024]{1,0:T(8,128)(2,1)S(1)}, u32[]{:S(2)}, u32[]{:S(2)}) collective-permute-start(bf16[128,1024]{1,0:T(8,128)(2,1)S(1)} %copy-done.4), channel_id=1, source_target_pairs={{0,6},{1,7},{2,0},{3,1},{4,2},{5,3},{6,4},{7,5},{8,14},{9,15},{10,... | collective-permute-start | bytes 786440 | tf_op jit(solution)/shard_map/ppermute | solution.py:501
  53.3 2.7 %collective-permute-start.9 = (bf16[512,1024]{1,0:T(8,128)(2,1)S(1)}, bf16[512,1024]{1,0:T(8,128)(2,1)S(1)}, u32[]{:S(2)}, u32[]{:S(2)}) collective-permute-start(bf16[512,1024]{1,0:T(8,128)(2,1)S(1)} %collect.3.refs_0_), channel_id=1, source_target_pairs={{0,1},{1,0},{2,3},{3,2},{4,5},{5,4},{6,7},{7,6},{8,9},{9,8},{10,11... | collective-permute-start | bytes 3145736 | tf_op jit(solution)/shard_map/ppermute | solution.py:497
  53.4 8.5 %collective-permute-start.5 = (bf16[512,1024]{1,0:T(8,128)(2,1)S(1)}, bf16[512,1024]{1,0:T(8,128)(2,1)S(1)}, u32[]{:S(2)}, u32[]{:S(2)}) collective-permute-start(bf16[512,1024]{1,0:T(8,128)(2,1)S(1)} %get-tuple-element.76), channel_id=1, source_target_pairs={{0,1},{1,0},{2,3},{3,2},{4,5},{5,4},{6,7},{7,6},{8,9},{9,8},{10,11... | collective-permute-start | bytes 3145736 | tf_op jit(solution)/shard_map/ppermute | solution.py:497
  58.9 18.4 %collective-permute-start.13 = (bf16[2,128,1024]{2,1,0:T(8,128)(2,1)S(1)}, bf16[2,128,1024]{2,1,0:T(8,128)(2,1)S(1)}, u32[]{:S(2)}, u32[]{:S(2)}) collective-permute-start(bf16[2,128,1024]{2,1,0:T(8,128)(2,1)S(1)} %bitcast.18), channel_id=1, source_target_pairs={{0,8},{8,0},{16,24},{24,16},{1,9},{9,1},{17,25},{25,17},{2,10},{10... | collective-permute-start | bytes 1572872 | tf_op jit(solution)/shard_map/ppermute | solution.py:505
  60.4 17.5 %collective-permute-start.14 = (bf16[2,128,1024]{2,1,0:T(8,128)(2,1)S(1)}, bf16[2,128,1024]{2,1,0:T(8,128)(2,1)S(1)}, u32[]{:S(2)}, u32[]{:S(2)}) collective-permute-start(bf16[2,128,1024]{2,1,0:T(8,128)(2,1)S(1)} %bitcast.17), channel_id=1, source_target_pairs={{0,16},{8,24},{16,0},{24,8},{1,17},{9,25},{17,1},{25,9},{2,18},{10... | collective-permute-start | bytes 1572872 | tf_op jit(solution)/shard_map/ppermute | solution.py:509
  62.1 14.7 %collective-permute-start.10 = (bf16[128,1024]{1,0:T(8,128)(2,1)S(1)}, bf16[128,1024]{1,0:T(8,128)(2,1)S(1)}, u32[]{:S(2)}, u32[]{:S(2)}) collective-permute-start(bf16[128,1024]{1,0:T(8,128)(2,1)S(1)} %get-tuple-element.85), channel_id=1, source_target_pairs={{0,6},{1,7},{2,0},{3,1},{4,2},{5,3},{6,4},{7,5},{8,14},{9,15},{10,... | collective-permute-start | bytes 786440 | tf_op jit(solution)/shard_map/ppermute | solution.py:501
  64.0 27.5 %collective-permute-start.11 = (bf16[128,1024]{1,0:T(8,128)(2,1)S(1)}, bf16[128,1024]{1,0:T(8,128)(2,1)S(1)}, u32[]{:S(2)}, u32[]{:S(2)}) collective-permute-start(bf16[128,1024]{1,0:T(8,128)(2,1)S(1)} %get-tuple-element.86), channel_id=1, source_target_pairs={{0,4},{1,5},{2,6},{3,7},{4,0},{5,1},{6,2},{7,3},{8,12},{9,13},{10,... | collective-permute-start | bytes 786440 | tf_op jit(solution)/shard_map/ppermute | solution.py:501
  68.7 23.4 %collective-permute-start.12 = (bf16[128,1024]{1,0:T(8,128)(2,1)S(1)}, bf16[128,1024]{1,0:T(8,128)(2,1)S(1)}, u32[]{:S(2)}, u32[]{:S(2)}) collective-permute-start(bf16[128,1024]{1,0:T(8,128)(2,1)S(1)} %get-tuple-element.87), channel_id=1, source_target_pairs={{0,2},{1,3},{2,4},{3,5},{4,6},{5,7},{6,0},{7,1},{8,10},{9,11},{10,... | collective-permute-start | bytes 786440 | tf_op jit(solution)/shard_map/ppermute | solution.py:501
  75.8 1.0 copy-start.12
  76.8 1.2 copy-start.10
  76.8 23.3 %collective-permute-start.16 = (bf16[2,256,512]{2,1,0:T(8,128)(2,1)S(1)}, bf16[2,256,512]{2,1,0:T(8,128)(2,1)S(1)}, u32[]{:S(2)}, u32[]{:S(2)}) collective-permute-start(bf16[2,256,512]{2,1,0:T(8,128)(2,1)S(1)} %bitcast.16), channel_id=1, source_target_pairs={{0,8},{8,0},{16,24},{24,16},{1,9},{9,1},{17,25},{25,17},{2,10},{10... | collective-permute-start | bytes 1572872 | tf_op jit(solution)/shard_map/ppermute | solution.py:505
  77.4 22.7 %collective-permute-start.17 = (bf16[2,256,512]{2,1,0:T(8,128)(2,1)S(1)}, bf16[2,256,512]{2,1,0:T(8,128)(2,1)S(1)}, u32[]{:S(2)}, u32[]{:S(2)}) collective-permute-start(bf16[2,256,512]{2,1,0:T(8,128)(2,1)S(1)} %bitcast.15), channel_id=1, source_target_pairs={{0,16},{8,24},{16,0},{24,8},{1,17},{9,25},{17,1},{25,9},{2,18},{10... | collective-permute-start | bytes 1572872 | tf_op jit(solution)/shard_map/ppermute | solution.py:509
  78.0 0.8 copy-start.14
  78.8 0.8 copy-start.16
  79.6 5.1 %copy-start.20 = (bf16[128,1024]{1,0:T(8,128)(2,1)}, bf16[128,1024]{1,0:T(8,128)(2,1)S(1)}, u32[]{:S(2)}) copy-start(bf16[128,1024]{1,0:T(8,128)(2,1)S(1)} %get-tuple-element.117.refs_1_) | copy-start | bytes 786436
  84.8 8.6 %collective-permute-start.15 = (bf16[544,1024]{1,0:T(8,128)(2,1)S(1)}, bf16[544,1024]{1,0:T(8,128)(2,1)S(1)}, u32[]{:S(2)}, u32[]{:S(2)}) collective-permute-start(bf16[544,1024]{1,0:T(8,128)(2,1)S(1)} %get-tuple-element.107), channel_id=1, source_target_pairs={{0,1},{1,0},{2,3},{3,2},{4,5},{5,4},{6,7},{7,6},{8,9},{9,8},{10,11... | collective-permute-start | bytes 3342344 | tf_op jit(solution)/shard_map/ppermute | solution.py:497
  88.4 1.0 copy-start.8
  89.4 4.0 %copy-start.6 = (f32[2,256,512]{2,1,0:T(8,128)}, f32[2,256,512]{2,1,0:T(8,128)S(1)}, u32[]{:S(2)}) copy-start(f32[2,256,512]{2,1,0:T(8,128)S(1)} %get-tuple-element.128.refs_0_) | copy-start | bytes 3145732
  91.5 13.5 %collective-permute-start.22 = (bf16[2,256,512]{2,1,0:T(8,128)(2,1)}, bf16[2,256,512]{2,1,0:T(8,128)(2,1)}, u32[]{:S(2)}, u32[]{:S(2)}) collective-permute-start(bf16[2,256,512]{2,1,0:T(8,128)(2,1)} %bitcast.12), channel_id=1, source_target_pairs={{0,8},{8,0},{16,24},{24,16},{1,9},{9,1},{17,25},{25,17},{2,10},{10... | collective-permute-start | bytes 1572872 | tf_op jit(solution)/shard_map/ppermute | solution.py:505
  92.1 14.2 %collective-permute-start.23 = (bf16[2,256,512]{2,1,0:T(8,128)(2,1)}, bf16[2,256,512]{2,1,0:T(8,128)(2,1)}, u32[]{:S(2)}, u32[]{:S(2)}) collective-permute-start(bf16[2,256,512]{2,1,0:T(8,128)(2,1)} %bitcast.13), channel_id=1, source_target_pairs={{0,16},{8,24},{16,0},{24,8},{1,17},{9,25},{17,1},{25,9},{2,18},{10... | collective-permute-start | bytes 1572872 | tf_op jit(solution)/shard_map/ppermute | solution.py:509
  95.2 31.1 %all-to-all-start = ((bf16[4,136,1024]{2,1,0:T(8,128)(2,1)}), bf16[4,136,1024]{2,1,0:T(8,128)(2,1)S(1)}, u32[]{:S(2)}, u32[]{:S(2)}) async-start(bf16[4,136,1024]{2,1,0:T(8,128)(2,1)} %bitcast.7), calls=%async_computation | async-start | bytes 2228224 | tf_op jit(solution)/shard_map/all_to_all | solution.py:556
  99.1 0.9 copy-start.21
  100.0 1.2 copy-start.11
  100.0 1.5 %copy-start.13 = (f32[2,256,512]{2,1,0:T(8,128)S(1)}, f32[2,256,512]{2,1,0:T(8,128)}, u32[]{:S(2)}) copy-start(f32[2,256,512]{2,1,0:T(8,128)} %copy-done.12) | copy-start | bytes 3145732
  101.6 4.7 %copy-start.7 = (f32[2,256,512]{2,1,0:T(8,128)S(1)}, f32[2,256,512]{2,1,0:T(8,128)}, u32[]{:S(2)}) copy-start(f32[2,256,512]{2,1,0:T(8,128)} %copy-done.6) | copy-start | bytes 3145732
  101.6 4.7 %copy-start.9 = (f32[2,256,512]{2,1,0:T(8,128)S(1)}, f32[2,256,512]{2,1,0:T(8,128)}, u32[]{:S(2)}) copy-start(f32[2,256,512]{2,1,0:T(8,128)} %copy-done.8) | copy-start | bytes 3145732
  101.8 18.4 %collective-permute-start.18 = (bf16[256,512]{1,0:T(8,128)(2,1)S(1)}, bf16[256,512]{1,0:T(8,128)(2,1)S(1)}, u32[]{:S(2)}, u32[]{:S(2)}) collective-permute-start(bf16[256,512]{1,0:T(8,128)(2,1)S(1)} %get-tuple-element.121), channel_id=1, source_target_pairs={{0,16},{8,24},{16,0},{24,8},{1,17},{9,25},{17,1},{25,9},{2,18},{10... | collective-permute-start | bytes 786440 | tf_op jit(solution)/shard_map/ppermute | solution.py:509
  103.4 16.8 %collective-permute-start.19 = (bf16[256,512]{1,0:T(8,128)(2,1)S(1)}, bf16[256,512]{1,0:T(8,128)(2,1)S(1)}, u32[]{:S(2)}, u32[]{:S(2)}) collective-permute-start(bf16[256,512]{1,0:T(8,128)(2,1)S(1)} %get-tuple-element.123), channel_id=1, source_target_pairs={{0,8},{8,0},{16,24},{24,16},{1,9},{9,1},{17,25},{25,17},{2,10},{10... | collective-permute-start | bytes 786440 | tf_op jit(solution)/shard_map/ppermute | solution.py:505
  104.5 12.9 %collective-permute-start.20 = (bf16[128,1024]{1,0:T(8,128)(2,1)S(1)}, bf16[128,1024]{1,0:T(8,128)(2,1)S(1)}, u32[]{:S(2)}, u32[]{:S(2)}) collective-permute-start(bf16[128,1024]{1,0:T(8,128)(2,1)S(1)} %get-tuple-element.125), channel_id=1, source_target_pairs={{0,16},{8,24},{16,0},{24,8},{1,17},{9,25},{17,1},{25,9},{2,18},{10... | collective-permute-start | bytes 786440 | tf_op jit(solution)/shard_map/ppermute | solution.py:509
  105.0 14.1 %collective-permute-start.21 = (bf16[128,1024]{1,0:T(8,128)(2,1)S(1)}, bf16[128,1024]{1,0:T(8,128)(2,1)S(1)}, u32[]{:S(2)}, u32[]{:S(2)}) collective-permute-start(bf16[128,1024]{1,0:T(8,128)(2,1)S(1)} %get-tuple-element.127), channel_id=1, source_target_pairs={{0,8},{8,0},{16,24},{24,16},{1,9},{9,1},{17,25},{25,17},{2,10},{10... | collective-permute-start | bytes 786440 | tf_op jit(solution)/shard_map/ppermute | solution.py:505
  106.2 12.9 %copy-start.15 = (f32[128,1024]{1,0:T(8,128)S(1)}, f32[128,1024]{1,0:T(8,128)}, u32[]{:S(2)}) copy-start(f32[128,1024]{1,0:T(8,128)} %copy-done.14) | copy-start | bytes 1572868
  106.2 12.9 %copy-start.17 = (f32[128,1024]{1,0:T(8,128)S(1)}, f32[128,1024]{1,0:T(8,128)}, u32[]{:S(2)}) copy-start(f32[128,1024]{1,0:T(8,128)} %copy-done.16) | copy-start | bytes 1572868
  107.8 12.4 %copy-start.18 = (f32[256,512]{1,0:T(8,128)}, f32[256,512]{1,0:T(8,128)S(1)}, u32[]{:S(2)}) copy-start(f32[256,512]{1,0:T(8,128)S(1)} %get-tuple-element.138.refs_2_) | copy-start | bytes 1572868
  107.8 19.4 %collective-permute-start.24 = (bf16[256,512]{1,0:T(8,128)(2,1)S(1)}, bf16[256,512]{1,0:T(8,128)(2,1)S(1)}, u32[]{:S(2)}, u32[]{:S(2)}) collective-permute-start(bf16[256,512]{1,0:T(8,128)(2,1)S(1)} %get-tuple-element.137), channel_id=1, source_target_pairs={{0,16},{8,24},{16,0},{24,8},{1,17},{9,25},{17,1},{25,9},{2,18},{10... | collective-permute-start | bytes 786440 | tf_op jit(solution)/shard_map/ppermute | solution.py:509
  117.4 9.8 %collective-permute-start.25 = (bf16[256,512]{1,0:T(8,128)(2,1)S(1)}, bf16[256,512]{1,0:T(8,128)(2,1)S(1)}, u32[]{:S(2)}, u32[]{:S(2)}) collective-permute-start(bf16[256,512]{1,0:T(8,128)(2,1)S(1)} %get-tuple-element.139), channel_id=1, source_target_pairs={{0,8},{8,0},{16,24},{24,16},{1,9},{9,1},{17,25},{25,17},{2,10},{10... | collective-permute-start | bytes 786440 | tf_op jit(solution)/shard_map/ppermute | solution.py:505
  120.2 6.1 %copy-start.5 = (s32[128,8]{0,1:T(8,128)S(1)}, s32[128,8]{0,1:T(8,128)}, u32[]{:S(2)}) copy-start(s32[128,8]{0,1:T(8,128)} %param.8) | copy-start | bytes 12292
  126.3 1.1 copy-start.19

commit v3 on v2

--- a/solution.py
+++ b/solution.py
@@ -28,7 +28,7 @@
 
 def on_chip(body, operands, out_shape, flops, name, scalars=0, scratch=()):
     total = sum(size(s) for s in list(operands) + list(out_shape))
-    limit = min(60 * 2**20, total // 3 + sum(size(s) for s in scratch) + 4 * 2**20)
+    limit = min(60 * 2**20, total // 8 + sum(size(s) for s in scratch) + 4 * 2**20)
     return pl.pallas_call(
         body,
         in_specs=[SMEM] * scalars + [VMEM] * (len(operands) - scalars),

time: 129 us -> 127 us (0.984)
  waiting for transfers between devices: 37.8 us -> 41.5 us
  local copies, waits for them, and re-layouts: 7.41 us -> 4.61 us
  starting transfers between devices: 43 us -> 40.6 us
    ppermute x7, waiting for transfers between devices: 16.6 us -> 19.5 us  [move_z(): return lax.ppermute(v, 'expert', pairs)]
    unnamed x44, local copies, waits for them, and re-layouts: 7.41 us -> 4.61 us
    ppermute x6, waiting for transfers between devices: 8.37 us -> 11.1 us  [move_y(): return lax.ppermute(v, 'dp', pairs)]
    all_to_all x1, waiting for transfers between devices: 4.98 us -> 2.7 us  [send_home(): lax.all_to_all(parts, 'expert', split_axis=0, concat_axis=0, tiled=True,...]
    ppermute x6, starting transfers between devices: 6.13 us -> 4.7 us  [move_y(): return lax.ppermute(v, 'dp', pairs)]
  transfers between devices with their start and end apart: 27 -> 27, of which waited for: 9 -> 10; matrix products, arithmetic and copies ran while one was open for 0% -> 0% of each run, Pallas kernels for 28% -> 28%
where the time goes in v3:
time: 127 us
  waiting for transfers between devices  41.5 us (33%)
  starting transfers between devices  40.6 us (32%)
  Pallas kernels  39 us (31%)
  local copies, waits for them, and re-layouts  4.61 us (4%)
    pallas_call x20, Pallas kernels, on_chip(): pl.pallas_call(body, in_specs=[SMEM] * scalars + [VMEM] * (len(operands)...  37.3 us
    ppermute x7, waiting for transfers between devices, move_z(): return lax.ppermute(v, 'expert', pairs)  19.5 us
    ppermute x7, starting transfers between devices, move_z(): return lax.ppermute(v, 'expert', pairs)  18.9 us
    ppermute x6, waiting for transfers between devices, move_y(): return lax.ppermute(v, 'dp', pairs)  11.1 us
    ppermute x3, waiting for transfers between devices, near_rows(): send = lambda u, pairs: lax.ppermute(u, 'expert', chip_pairs(pairs))  7.49 us
    ppermute x3, starting transfers between devices, near_rows(): send = lambda u, pairs: lax.ppermute(u, 'expert', chip_pairs(pairs))  7.12 us
    ppermute x6, starting transfers between devices, move_x(): return lax.ppermute(v, 'dp', pairs)  5.73 us
    ppermute x6, starting transfers between devices, move_y(): return lax.ppermute(v, 'dp', pairs)  4.7 us
  transfers between devices with their start and end apart: 27, of which 10 were waited for; matrix products, arithmetic and copies ran while one was open for 0% of the time, Pallas kernels for 28%

profile of v3, /device:TPU:0, one launch (start us, length us, event | category | flops | bytes accessed | tf_op | source)
XLA Modules:
  0.0 126.8 jit_solution(5469617396329461085)
XLA Ops:
  0.6 1.7 %pack_tokens.1.own_ref = bf16[136,1024]{1,0:T(8,128)(2,1)} custom-call(bf16[128,1024]{1,0:T(8,128)(2,1)} %tok_hbm.1, s32[8,128]{1,0:T(8,128)} %bitcast.19, f32[8,128]{1,0:T(8,128)} %bitcast.21), custom_call_target="tpu_custom_call" | custom-call | flops 10000000000 | bytes 1048576 | tf_op jit(solution)/shard_map/pack_tokens/pallas_call | solution.py:86
  2.4 4.1 %collective-permute-start = (bf16[136,1024]{1,0:T(8,128)(2,1)}, bf16[136,1024]{1,0:T(8,128)(2,1)S(1)}, u32[]{:S(2)}, u32[]{:S(2)}) collective-permute-start(bf16[136,1024]{1,0:T(8,128)(2,1)} %pack_tokens.1.own_ref), channel_id=1, source_target_pairs={{0,4},{1,5},{2,6},{3,7},{4,0},{5,1},{6,2},{7,3},{8,12},{9,13},{10,... | collective-permute-start | bytes 835592 | tf_op jit(solution)/shard_map/ppermute | solution.py:501
  6.5 1.3 %collective-permute-start.2 = (bf16[136,1024]{1,0:T(8,128)(2,1)}, bf16[136,1024]{1,0:T(8,128)(2,1)S(1)}, u32[]{:S(2)}, u32[]{:S(2)}) collective-permute-start(bf16[136,1024]{1,0:T(8,128)(2,1)} %pack_tokens.1.own_ref), channel_id=1, source_target_pairs={{2,0},{3,1},{4,2},{5,3},{6,4},{7,5},{10,8},{11,9},{12,10},{13,11},... | collective-permute-start | bytes 835592 | tf_op jit(solution)/shard_map/ppermute | solution.py:520
  7.7 4.6 %collective-permute-start.1 = (bf16[136,1024]{1,0:T(8,128)(2,1)}, bf16[136,1024]{1,0:T(8,128)(2,1)S(1)}, u32[]{:S(2)}, u32[]{:S(2)}) collective-permute-start(bf16[136,1024]{1,0:T(8,128)(2,1)} %pack_tokens.1.own_ref), channel_id=1, source_target_pairs={{0,2},{1,3},{2,4},{3,5},{4,6},{5,7},{8,10},{9,11},{10,12},{11,13},... | collective-permute-start | bytes 835592 | tf_op jit(solution)/shard_map/ppermute | solution.py:520
  12.3 7.9 %collective-permute-done.two_ref = bf16[136,1024]{1,0:T(8,128)(2,1)S(1)} collective-permute-done((bf16[136,1024]{1,0:T(8,128)(2,1)}, bf16[136,1024]{1,0:T(8,128)(2,1)S(1)}, u32[]{:S(2)}, u32[]{:S(2)}) %collective-permute-start) | collective-permute-done | bytes 278560 | tf_op jit(solution)/shard_map/ppermute | solution.py:501
  20.2 1.3 %collective-permute-start.3 = (bf16[136,1024]{1,0:T(8,128)(2,1)S(1)}, bf16[136,1024]{1,0:T(8,128)(2,1)S(1)}, u32[]{:S(2)}, u32[]{:S(2)}) collective-permute-start(bf16[136,1024]{1,0:T(8,128)(2,1)S(1)} %collective-permute-done.two_ref), channel_id=1, source_target_pairs={{4,6},{5,7},{2,0},{3,1},{12,14},{13,15},{10,8},{11,9},{20,22},{21,... | collective-permute-start | bytes 835592 | tf_op jit(solution)/shard_map/ppermute | solution.py:520
  21.5 0.1 pad_add_fusion.place_ref.refs_0_
  21.6 7.5 %collective-permute-done.3.relayed_ref = bf16[136,1024]{1,0:T(8,128)(2,1)S(1)} collective-permute-done((bf16[136,1024]{1,0:T(8,128)(2,1)S(1)}, bf16[136,1024]{1,0:T(8,128)(2,1)S(1)}, u32[]{:S(2)}, u32[]{:S(2)}) %collective-permute-start.3) | collective-permute-done | bytes 278560 | tf_op jit(solution)/shard_map/ppermute | solution.py:520
  29.1 1.0 copy-done.3
  30.0 0.6 collect.2.near_in
  30.7 0.1 collective-permute-start.4
  30.7 0.2 copy-done.4
  31.0 2.4 %collective-permute-start.7 = (bf16[128,1024]{1,0:T(8,128)(2,1)S(1)}, bf16[128,1024]{1,0:T(8,128)(2,1)S(1)}, u32[]{:S(2)}, u32[]{:S(2)}) collective-permute-start(bf16[128,1024]{1,0:T(8,128)(2,1)S(1)} %copy-done.4), channel_id=1, source_target_pairs={{0,4},{1,5},{2,6},{3,7},{4,0},{5,1},{6,2},{7,3},{8,12},{9,13},{10,... | collective-permute-start | bytes 786440 | tf_op jit(solution)/shard_map/ppermute | solution.py:501
  33.3 2.5 %collective-permute-start.6 = (bf16[128,1024]{1,0:T(8,128)(2,1)S(1)}, bf16[128,1024]{1,0:T(8,128)(2,1)S(1)}, u32[]{:S(2)}, u32[]{:S(2)}) collective-permute-start(bf16[128,1024]{1,0:T(8,128)(2,1)S(1)} %copy-done.4), channel_id=1, source_target_pairs={{0,2},{1,3},{2,4},{3,5},{4,6},{5,7},{6,0},{7,1},{8,10},{9,11},{10,... | collective-permute-start | bytes 786440 | tf_op jit(solution)/shard_map/ppermute | solution.py:501
  35.8 1.3 %collective-permute-start.8 = (bf16[128,1024]{1,0:T(8,128)(2,1)S(1)}, bf16[128,1024]{1,0:T(8,128)(2,1)S(1)}, u32[]{:S(2)}, u32[]{:S(2)}) collective-permute-start(bf16[128,1024]{1,0:T(8,128)(2,1)S(1)} %copy-done.4), channel_id=1, source_target_pairs={{0,6},{1,7},{2,0},{3,1},{4,2},{5,3},{6,4},{7,5},{8,14},{9,15},{10,... | collective-permute-start | bytes 786440 | tf_op jit(solution)/shard_map/ppermute | solution.py:501
  37.2 9.2 %forward.1 = (bf16[512,1024]{1,0:T(8,128)(2,1)S(1)}, bf16[512,1024]{1,0:T(8,128)(2,1)S(1)}, bf16[512,1024]{1,0:T(8,128)(2,1)S(1)}, bf16[512,1024]{1,0:T(8,128)(2...) custom-call(s32[3]{0:T(128)S(1)} %pad_add_fusion.place_ref.refs_0_, ...), custom_call_target="tpu_custom_call" | custom-call | flops 10000000000 | bytes 22155276 | tf_op jit(solution)/shard_map/forward/pallas_call | solution.py:32
  46.4 5.9 %collective-permute-done.7.refs_2_ = bf16[128,1024]{1,0:T(8,128)(2,1)S(1)} collective-permute-done((bf16[128,1024]{1,0:T(8,128)(2,1)S(1)}, bf16[128,1024]{1,0:T(8,128)(2,1)S(1)}, u32[]{:S(2)}, u32[]{:S(2)}) %collective-permute-start.7) | collective-permute-done | bytes 262176 | tf_op jit(solution)/shard_map/ppermute | solution.py:501
  52.3 0.9 collective-permute-done.8.refs_3_
  53.3 0.1 collective-permute-start.9
  53.4 0.5 collective-permute-start.5
  53.9 1.8 %hidden_grads.2 = (bf16[512,1024]{1,0:T(8,128)(2,1)S(1)}, bf16[512,1024]{1,0:T(8,128)(2,1)S(1)}, f32[512,128]{1,0:T(8,128)S(1)}, f32[8,128]{1,0:T(8,128)S(1)}) custom-call(bf16[512,1024]{1,0:T(8,128)(2,1)S(1)} %collect.3.refs_0_, bf16[512,1024]{1,0:T(8,128)(2,1)S(1)} %get-tuple-element.79.refs_1_, bf16[512,1024]{1,0:T(8,128)(2,1)S(1)} %get-tuple-element.80.refs_2_, ...), custom_call_target="tpu_custom_call" | custom-call | flops 10000000000 | bytes 8654848 | tf_op jit(solution)/shard_map/hidden_grads/pallas_call | solution.py:32
  55.6 0.4 collective-permute-done.9.refs_1_.refs_0_
  56.0 2.9 %down_partials.1 = (bf16[1,2,128,1024]{3,2,1,0:T(8,128)(2,1)S(1)}, f32[2,128,1024]{2,1,0:T(8,128)S(1)}, bf16[1,2,128,1024]{3,2,1,0:T(8,128)(2,1)S(1)}, f32[2,128,1024]{2,1,0:T(8,128)S(1)}, f32[8,128]{1,0:T(8,128)S(1)}) custom-call(s32[3]{0:T(128)S(1)} %pad_add_fusion.place_ref.refs_0_, bf16[1024,1024]{1,0:T(8,128)(2,1)S(1)} %get-tuple-element.77.left_ref, ...), custom_call_target="tpu_custom_call" | custom-call | flops 10000000000 | bytes 7348236 | tf_op jit(solution)/shard_map/down_partials/pallas_call | solution.py:32
  58.9 1.4 %collective-permute-start.13 = (bf16[2,128,1024]{2,1,0:T(8,128)(2,1)S(1)}, bf16[2,128,1024]{2,1,0:T(8,128)(2,1)S(1)}, u32[]{:S(2)}, u32[]{:S(2)}) collective-permute-start(bf16[2,128,1024]{2,1,0:T(8,128)(2,1)S(1)} %bitcast.18), channel_id=1, source_target_pairs={{0,8},{8,0},{16,24},{24,16},{1,9},{9,1},{17,25},{25,17},{2,10},{10... | collective-permute-start | bytes 1572872 | tf_op jit(solution)/shard_map/ppermute | solution.py:505
  60.4 1.5 %collective-permute-start.14 = (bf16[2,128,1024]{2,1,0:T(8,128)(2,1)S(1)}, bf16[2,128,1024]{2,1,0:T(8,128)(2,1)S(1)}, u32[]{:S(2)}, u32[]{:S(2)}) collective-permute-start(bf16[2,128,1024]{2,1,0:T(8,128)(2,1)S(1)} %bitcast.17), channel_id=1, source_target_pairs={{0,16},{8,24},{16,0},{24,8},{1,17},{9,25},{17,1},{25,9},{2,18},{10... | collective-permute-start | bytes 1572872 | tf_op jit(solution)/shard_map/ppermute | solution.py:509
  61.9 0.2 out_sides.1
  62.1 1.9 %collective-permute-start.10 = (bf16[128,1024]{1,0:T(8,128)(2,1)S(1)}, bf16[128,1024]{1,0:T(8,128)(2,1)S(1)}, u32[]{:S(2)}, u32[]{:S(2)}) collective-permute-start(bf16[128,1024]{1,0:T(8,128)(2,1)S(1)} %get-tuple-element.85), channel_id=1, source_target_pairs={{0,6},{1,7},{2,0},{3,1},{4,2},{5,3},{6,4},{7,5},{8,14},{9,15},{10,... | collective-permute-start | bytes 786440 | tf_op jit(solution)/shard_map/ppermute | solution.py:501
  64.0 4.7 %collective-permute-start.11 = (bf16[128,1024]{1,0:T(8,128)(2,1)S(1)}, bf16[128,1024]{1,0:T(8,128)(2,1)S(1)}, u32[]{:S(2)}, u32[]{:S(2)}) collective-permute-start(bf16[128,1024]{1,0:T(8,128)(2,1)S(1)} %get-tuple-element.86), channel_id=1, source_target_pairs={{0,4},{1,5},{2,6},{3,7},{4,0},{5,1},{6,2},{7,3},{8,12},{9,13},{10,... | collective-permute-start | bytes 786440 | tf_op jit(solution)/shard_map/ppermute | solution.py:501
  68.7 1.9 %collective-permute-start.12 = (bf16[128,1024]{1,0:T(8,128)(2,1)S(1)}, bf16[128,1024]{1,0:T(8,128)(2,1)S(1)}, u32[]{:S(2)}, u32[]{:S(2)}) collective-permute-start(bf16[128,1024]{1,0:T(8,128)(2,1)S(1)} %get-tuple-element.87), channel_id=1, source_target_pairs={{0,2},{1,3},{2,4},{3,5},{4,6},{5,7},{6,0},{7,1},{8,10},{9,11},{10,... | collective-permute-start | bytes 786440 | tf_op jit(solution)/shard_map/ppermute | solution.py:501
  70.6 2.3 %hidden_grads.3 = (bf16[512,1024]{1,0:T(8,128)(2,1)S(1)}, bf16[512,1024]{1,0:T(8,128)(2,1)S(1)}, f32[512,128]{1,0:T(8,128)S(1)}, f32[8,128]{1,0:T(8,128)}) custom-call(bf16[512,1024]{1,0:T(8,128)(2,1)S(1)} %collective-permute-done.9.refs_1_.refs_0_, bf16[512,1024]{1,0:T(8,128)(2,1)S(1)} %get-tuple-element.90.refs_1_, ...), custom_call_target="tpu_custom_call" | custom-call | flops 10000000000 | bytes 8658944 | tf_op jit(solution)/shard_map/hidden_grads/pallas_call | solution.py:32
  72.9 2.9 %gate_partials.1 = (bf16[1,2,256,512]{3,2,1,0:T(8,128)(2,1)S(1)}, f32[2,256,512]{2,1,0:T(8,128)S(1)}, bf16[1,2,256,512]{3,2,1,0:T(8,128)(2,1)S(1)}, f32[2,256,512]{2,1,0:T(8,128)S(1)}, f32[8,128]{1,0:T(8,128)S(1)}) custom-call(s32[3]{0:T(128)S(1)} %pad_add_fusion.place_ref.refs_0_, bf16[1024,1024]{1,0:T(8,128)(2,1)S(1)} %get-tuple-element.88.left_ref, ...), custom_call_target="tpu_custom_call" | custom-call | flops 10000000000 | bytes 7344140 | tf_op jit(solution)/shard_map/gate_partials/pallas_call | solution.py:32
  75.8 0.6 collective-permute-start.16
  76.4 0.5 collective-permute-start.17
  76.9 0.2 down_first.1
  77.2 0.7 copy-done.20
  77.9 5.1 %token_partials.1 = (f32[544,1024]{1,0:T(8,128)S(1)}, bf16[544,1024]{1,0:T(8,128)(2,1)S(1)}) custom-call(s32[3]{0:T(128)S(1)} %pad_add_fusion.place_ref.refs_0_, bf16[512,1024]{1,0:T(8,128)(2,1)S(1)} %get-tuple-element.94.refs_0_.refs_1_, bf16[512,1024]{1,0:T(8,128)(2,1)S(1)} %get-tuple-element.95.refs_1_.refs_2_, ...), custom_call_target="tpu_custom_call" | custom-call | flops 10000000000 | bytes 12259340 | tf_op jit(solution)/shard_map/token_partials/pallas_call | solution.py:32
  83.0 0.1 collective-permute-start.15
  83.1 3.5 %up_partials.1 = (bf16[1,2,256,512]{3,2,1,0:T(8,128)(2,1)}, f32[2,256,512]{2,1,0:T(8,128)S(1)}, bf16[1,2,256,512]{3,2,1,0:T(8,128)(2,1)}, f32[2,256,512]{2,1,0:T(8,128)S(1)}, f32[8,128]{1,0:T(8,128)S(1)}) custom-call(s32[3]{0:T(128)S(1)} %pad_add_fusion.place_ref.refs_0_, bf16[1024,1024]{1,0:T(8,128)(2,1)S(1)} %get-tuple-element.88.left_ref, ...), custom_call_target="tpu_custom_call" | custom-call | flops 10000000000 | bytes 7348236 | tf_op jit(solution)/shard_map/up_partials/pallas_call | solution.py:32
  86.7 4.8 %collective-permute-done.11.refs_2_ = bf16[128,1024]{1,0:T(8,128)(2,1)S(1)} collective-permute-done((bf16[128,1024]{1,0:T(8,128)(2,1)S(1)}, bf16[128,1024]{1,0:T(8,128)(2,1)S(1)}, u32[]{:S(2)}, u32[]{:S(2)}) %collective-permute-start.11) | collective-permute-done | bytes 262176 | tf_op jit(solution)/shard_map/ppermute | solution.py:501
  91.5 0.5 collective-permute-start.22
  92.0 0.5 collective-permute-start.23
  92.5 0.8 out_rows.1
  93.4 1.8 %token_sides.1 = (bf16[544,1024]{1,0:T(8,128)(2,1)}, f32[8,128]{1,0:T(8,128)S(1)}) custom-call(s32[3]{0:T(128)S(1)} %pad_add_fusion.place_ref.refs_0_, f32[544,1024]{1,0:T(8,128)S(1)} %get-tuple-element.104.near_ref, bf16[544,1024]{1,0:T(8,128)(2,1)S(1)} %collective-permute-done.15.far_ref, f32[8,128]{1,0:T(8,128)S(1)} %get-tuple-element.108.refs_0_), custom_call_target="tpu_custom_call" | custom-call | flops 10000000000 | bytes 4464652 | tf_op jit(solution)/shard_map/token_sides/pallas_call | solution.py:32
  95.1 3.5 %all-to-all-start = ((bf16[4,136,1024]{2,1,0:T(8,128)(2,1)}), bf16[4,136,1024]{2,1,0:T(8,128)(2,1)S(1)}, u32[]{:S(2)}, u32[]{:S(2)}) async-start(bf16[4,136,1024]{2,1,0:T(8,128)(2,1)} %bitcast.7), calls=%async_computation | async-start | bytes 2228224 | tf_op jit(solution)/shard_map/all_to_all | solution.py:556
  98.7 0.9 copy-done.21
  99.7 1.2 copy-done.11
  100.9 0.3 copy-done.13
  101.2 0.2 gate_first.1
  101.4 1.6 %collective-permute-start.18 = (bf16[256,512]{1,0:T(8,128)(2,1)S(1)}, bf16[256,512]{1,0:T(8,128)(2,1)S(1)}, u32[]{:S(2)}, u32[]{:S(2)}) collective-permute-start(bf16[256,512]{1,0:T(8,128)(2,1)S(1)} %get-tuple-element.121), channel_id=1, source_target_pairs={{0,16},{8,24},{16,0},{24,8},{1,17},{9,25},{17,1},{25,9},{2,18},{10... | collective-permute-start | bytes 786440 | tf_op jit(solution)/shard_map/ppermute | solution.py:509
  103.0 1.5 %collective-permute-start.19 = (bf16[256,512]{1,0:T(8,128)(2,1)S(1)}, bf16[256,512]{1,0:T(8,128)(2,1)S(1)}, u32[]{:S(2)}, u32[]{:S(2)}) collective-permute-start(bf16[256,512]{1,0:T(8,128)(2,1)S(1)} %get-tuple-element.123), channel_id=1, source_target_pairs={{0,8},{8,0},{16,24},{24,16},{1,9},{9,1},{17,25},{25,17},{2,10},{10... | collective-permute-start | bytes 786440 | tf_op jit(solution)/shard_map/ppermute | solution.py:505
  104.5 0.5 collective-permute-start.20
  105.0 0.4 collective-permute-done.22.refs_1_
  105.4 0.2 collective-permute-start.21
  105.5 1.6 %collective-permute-done.23.refs_3_ = bf16[2,256,512]{2,1,0:T(8,128)(2,1)} collective-permute-done((bf16[2,256,512]{2,1,0:T(8,128)(2,1)}, bf16[2,256,512]{2,1,0:T(8,128)(2,1)}, u32[]{:S(2)}, u32[]{:S(2)}) %collective-permute-start.23) | collective-permute-done | bytes 524320 | tf_op jit(solution)/shard_map/ppermute | solution.py:509
  107.1 1.5 %up_first.1 = (f32[256,512]{1,0:T(8,128)S(1)}, bf16[256,512]{1,0:T(8,128)(2,1)S(1)}, f32[256,512]{1,0:T(8,128)S(1)}, bf16[256,512]{1,0:T(8,128)(2,1)S(1)}, f32[8,128]{1,0:T(8,128)S(1)}) custom-call(f32[2,256,512]{2,1,0:T(8,128)S(1)} %copy-done.7, bf16[2,256,512]{2,1,0:T(8,128)(2,1)} %collective-permute-done.22.refs_1_, f32[2,256,512]{2,1,0:T(8,128)S(1)} %copy-done.9, ...), custom_call_target="tpu_custom_call" | custom-call | flops 10000000000 | bytes 4726784 | tf_op jit(solution)/shard_map/up_first/pallas_call | solution.py:32
  108.7 0.1 collective-permute-start.24
  108.8 9.5 %collective-permute-done.20.refs_1_ = bf16[128,1024]{1,0:T(8,128)(2,1)S(1)} collective-permute-done((bf16[128,1024]{1,0:T(8,128)(2,1)S(1)}, bf16[128,1024]{1,0:T(8,128)(2,1)S(1)}, u32[]{:S(2)}, u32[]{:S(2)}) %collective-permute-start.20) | collective-permute-done | bytes 262176 | tf_op jit(solution)/shard_map/ppermute | solution.py:509
  118.2 1.5 %collective-permute-start.25 = (bf16[256,512]{1,0:T(8,128)(2,1)S(1)}, bf16[256,512]{1,0:T(8,128)(2,1)S(1)}, u32[]{:S(2)}, u32[]{:S(2)}) collective-permute-start(bf16[256,512]{1,0:T(8,128)(2,1)S(1)} %get-tuple-element.139), channel_id=1, source_target_pairs={{0,8},{8,0},{16,24},{24,16},{1,9},{9,1},{17,25},{25,17},{2,10},{10... | collective-permute-start | bytes 786440 | tf_op jit(solution)/shard_map/ppermute | solution.py:505
  119.7 1.1 down_second.1
  120.9 1.1 gate_second.1
  121.9 2.7 %all-to-all-done = bf16[4,136,1024]{2,1,0:T(8,128)(2,1)S(1)} async-done(((bf16[4,136,1024]{2,1,0:T(8,128)(2,1)}), bf16[4,136,1024]{2,1,0:T(8,128)(2,1)S(1)}, u32[]{:S(2)}, u32[]{:S(2)}) %all-to-all-start) | async-done | bytes 1114144 | tf_op jit(solution)/shard_map/all_to_all | solution.py:556
  124.6 0.8 token_rows.1
  125.5 0.2 copy-done.19
  125.7 1.1 up_second.1
  (57 shorter events, 0.2 us)
Async XLA Ops:
  2.4 17.8 %collective-permute-start = (bf16[136,1024]{1,0:T(8,128)(2,1)}, bf16[136,1024]{1,0:T(8,128)(2,1)S(1)}, u32[]{:S(2)}, u32[]{:S(2)}) collective-permute-start(bf16[136,1024]{1,0:T(8,128)(2,1)} %pack_tokens.1.own_ref), channel_id=1, source_target_pairs={{0,4},{1,5},{2,6},{3,7},{4,0},{5,1},{6,2},{7,3},{8,12},{9,13},{10,... | collective-permute-start | bytes 835592 | tf_op jit(solution)/shard_map/ppermute | solution.py:501
  6.5 15.1 %collective-permute-start.2 = (bf16[136,1024]{1,0:T(8,128)(2,1)}, bf16[136,1024]{1,0:T(8,128)(2,1)S(1)}, u32[]{:S(2)}, u32[]{:S(2)}) collective-permute-start(bf16[136,1024]{1,0:T(8,128)(2,1)} %pack_tokens.1.own_ref), channel_id=1, source_target_pairs={{2,0},{3,1},{4,2},{5,3},{6,4},{7,5},{10,8},{11,9},{12,10},{13,11},... | collective-permute-start | bytes 835592 | tf_op jit(solution)/shard_map/ppermute | solution.py:520
  7.7 13.8 %collective-permute-start.1 = (bf16[136,1024]{1,0:T(8,128)(2,1)}, bf16[136,1024]{1,0:T(8,128)(2,1)S(1)}, u32[]{:S(2)}, u32[]{:S(2)}) collective-permute-start(bf16[136,1024]{1,0:T(8,128)(2,1)} %pack_tokens.1.own_ref), channel_id=1, source_target_pairs={{0,2},{1,3},{2,4},{3,5},{4,6},{5,7},{8,10},{9,11},{10,12},{11,13},... | collective-permute-start | bytes 835592 | tf_op jit(solution)/shard_map/ppermute | solution.py:520
  20.2 8.9 %collective-permute-start.3 = (bf16[136,1024]{1,0:T(8,128)(2,1)S(1)}, bf16[136,1024]{1,0:T(8,128)(2,1)S(1)}, u32[]{:S(2)}, u32[]{:S(2)}) collective-permute-start(bf16[136,1024]{1,0:T(8,128)(2,1)S(1)} %collective-permute-done.two_ref), channel_id=1, source_target_pairs={{4,6},{5,7},{2,0},{3,1},{12,14},{13,15},{10,8},{11,9},{20,22},{21,... | collective-permute-start | bytes 835592 | tf_op jit(solution)/shard_map/ppermute | solution.py:520
  21.6 15.6 %copy-start = (bf16[2,512,1024]{2,1,0:T(8,128)(2,1)S(1)}, bf16[2,512,1024]{2,1,0:T(8,128)(2,1)}, u32[]{:S(2)}) copy-start(bf16[2,512,1024]{2,1,0:T(8,128)(2,1)} %refs_4_.3) | copy-start | bytes 6291460
  21.6 15.6 %copy-start.1 = (bf16[2,1024,512]{2,1,0:T(8,128)(2,1)S(1)}, bf16[2,1024,512]{2,1,0:T(8,128)(2,1)}, u32[]{:S(2)}) copy-start(bf16[2,1024,512]{2,1,0:T(8,128)(2,1)} %refs_7_.1) | copy-start | bytes 6291460
  21.6 15.6 %copy-start.2 = (bf16[2,1024,512]{2,1,0:T(8,128)(2,1)S(1)}, bf16[2,1024,512]{2,1,0:T(8,128)(2,1)}, u32[]{:S(2)}) copy-start(bf16[2,1024,512]{2,1,0:T(8,128)(2,1)} %refs_8_.1) | copy-start | bytes 6291460
  29.1 1.0 copy-start.3
  30.0 0.9 copy-start.4
  30.7 6.5 %collective-permute-start.4 = (bf16[544,1024]{1,0:T(8,128)(2,1)S(1)}, bf16[544,1024]{1,0:T(8,128)(2,1)S(1)}, u32[]{:S(2)}, u32[]{:S(2)}) collective-permute-start(bf16[544,1024]{1,0:T(8,128)(2,1)S(1)} %collect.2.near_in), channel_id=1, source_target_pairs={{0,1},{1,0},{2,3},{3,2},{4,5},{5,4},{6,7},{7,6},{8,9},{9,8},{10,11... | collective-permute-start | bytes 3342344 | tf_op jit(solution)/shard_map/ppermute | solution.py:497
  31.0 21.3 %collective-permute-start.7 = (bf16[128,1024]{1,0:T(8,128)(2,1)S(1)}, bf16[128,1024]{1,0:T(8,128)(2,1)S(1)}, u32[]{:S(2)}, u32[]{:S(2)}) collective-permute-start(bf16[128,1024]{1,0:T(8,128)(2,1)S(1)} %copy-done.4), channel_id=1, source_target_pairs={{0,4},{1,5},{2,6},{3,7},{4,0},{5,1},{6,2},{7,3},{8,12},{9,13},{10,... | collective-permute-start | bytes 786440 | tf_op jit(solution)/shard_map/ppermute | solution.py:501
  33.3 19.0 %collective-permute-start.6 = (bf16[128,1024]{1,0:T(8,128)(2,1)S(1)}, bf16[128,1024]{1,0:T(8,128)(2,1)S(1)}, u32[]{:S(2)}, u32[]{:S(2)}) collective-permute-start(bf16[128,1024]{1,0:T(8,128)(2,1)S(1)} %copy-done.4), channel_id=1, source_target_pairs={{0,2},{1,3},{2,4},{3,5},{4,6},{5,7},{6,0},{7,1},{8,10},{9,11},{10,... | collective-permute-start | bytes 786440 | tf_op jit(solution)/shard_map/ppermute | solution.py:501
  35.8 17.4 %collective-permute-start.8 = (bf16[128,1024]{1,0:T(8,128)(2,1)S(1)}, bf16[128,1024]{1,0:T(8,128)(2,1)S(1)}, u32[]{:S(2)}, u32[]{:S(2)}) collective-permute-start(bf16[128,1024]{1,0:T(8,128)(2,1)S(1)} %copy-done.4), channel_id=1, source_target_pairs={{0,6},{1,7},{2,0},{3,1},{4,2},{5,3},{6,4},{7,5},{8,14},{9,15},{10,... | collective-permute-start | bytes 786440 | tf_op jit(solution)/shard_map/ppermute | solution.py:501
  53.3 2.7 %collective-permute-start.9 = (bf16[512,1024]{1,0:T(8,128)(2,1)S(1)}, bf16[512,1024]{1,0:T(8,128)(2,1)S(1)}, u32[]{:S(2)}, u32[]{:S(2)}) collective-permute-start(bf16[512,1024]{1,0:T(8,128)(2,1)S(1)} %collect.3.refs_0_), channel_id=1, source_target_pairs={{0,1},{1,0},{2,3},{3,2},{4,5},{5,4},{6,7},{7,6},{8,9},{9,8},{10,11... | collective-permute-start | bytes 3145736 | tf_op jit(solution)/shard_map/ppermute | solution.py:497
  53.4 8.5 %collective-permute-start.5 = (bf16[512,1024]{1,0:T(8,128)(2,1)S(1)}, bf16[512,1024]{1,0:T(8,128)(2,1)S(1)}, u32[]{:S(2)}, u32[]{:S(2)}) collective-permute-start(bf16[512,1024]{1,0:T(8,128)(2,1)S(1)} %get-tuple-element.76), channel_id=1, source_target_pairs={{0,1},{1,0},{2,3},{3,2},{4,5},{5,4},{6,7},{7,6},{8,9},{9,8},{10,11... | collective-permute-start | bytes 3145736 | tf_op jit(solution)/shard_map/ppermute | solution.py:497
  58.9 17.5 %collective-permute-start.13 = (bf16[2,128,1024]{2,1,0:T(8,128)(2,1)S(1)}, bf16[2,128,1024]{2,1,0:T(8,128)(2,1)S(1)}, u32[]{:S(2)}, u32[]{:S(2)}) collective-permute-start(bf16[2,128,1024]{2,1,0:T(8,128)(2,1)S(1)} %bitcast.18), channel_id=1, source_target_pairs={{0,8},{8,0},{16,24},{24,16},{1,9},{9,1},{17,25},{25,17},{2,10},{10... | collective-permute-start | bytes 1572872 | tf_op jit(solution)/shard_map/ppermute | solution.py:505
  60.4 16.6 %collective-permute-start.14 = (bf16[2,128,1024]{2,1,0:T(8,128)(2,1)S(1)}, bf16[2,128,1024]{2,1,0:T(8,128)(2,1)S(1)}, u32[]{:S(2)}, u32[]{:S(2)}) collective-permute-start(bf16[2,128,1024]{2,1,0:T(8,128)(2,1)S(1)} %bitcast.17), channel_id=1, source_target_pairs={{0,16},{8,24},{16,0},{24,8},{1,17},{9,25},{17,1},{25,9},{2,18},{10... | collective-permute-start | bytes 1572872 | tf_op jit(solution)/shard_map/ppermute | solution.py:509
  62.1 13.8 %collective-permute-start.10 = (bf16[128,1024]{1,0:T(8,128)(2,1)S(1)}, bf16[128,1024]{1,0:T(8,128)(2,1)S(1)}, u32[]{:S(2)}, u32[]{:S(2)}) collective-permute-start(bf16[128,1024]{1,0:T(8,128)(2,1)S(1)} %get-tuple-element.85), channel_id=1, source_target_pairs={{0,6},{1,7},{2,0},{3,1},{4,2},{5,3},{6,4},{7,5},{8,14},{9,15},{10,... | collective-permute-start | bytes 786440 | tf_op jit(solution)/shard_map/ppermute | solution.py:501
  64.0 27.5 %collective-permute-start.11 = (bf16[128,1024]{1,0:T(8,128)(2,1)S(1)}, bf16[128,1024]{1,0:T(8,128)(2,1)S(1)}, u32[]{:S(2)}, u32[]{:S(2)}) collective-permute-start(bf16[128,1024]{1,0:T(8,128)(2,1)S(1)} %get-tuple-element.86), channel_id=1, source_target_pairs={{0,4},{1,5},{2,6},{3,7},{4,0},{5,1},{6,2},{7,3},{8,12},{9,13},{10,... | collective-permute-start | bytes 786440 | tf_op jit(solution)/shard_map/ppermute | solution.py:501
  68.7 23.4 %collective-permute-start.12 = (bf16[128,1024]{1,0:T(8,128)(2,1)S(1)}, bf16[128,1024]{1,0:T(8,128)(2,1)S(1)}, u32[]{:S(2)}, u32[]{:S(2)}) collective-permute-start(bf16[128,1024]{1,0:T(8,128)(2,1)S(1)} %get-tuple-element.87), channel_id=1, source_target_pairs={{0,2},{1,3},{2,4},{3,5},{4,6},{5,7},{6,0},{7,1},{8,10},{9,11},{10,... | collective-permute-start | bytes 786440 | tf_op jit(solution)/shard_map/ppermute | solution.py:501
  75.8 1.4 %copy-start.10 = (f32[2,256,512]{2,1,0:T(8,128)}, f32[2,256,512]{2,1,0:T(8,128)S(1)}, u32[]{:S(2)}) copy-start(f32[2,256,512]{2,1,0:T(8,128)S(1)} %get-tuple-element.112.refs_0_) | copy-start | bytes 3145732
  75.8 1.4 %copy-start.12 = (f32[2,256,512]{2,1,0:T(8,128)}, f32[2,256,512]{2,1,0:T(8,128)S(1)}, u32[]{:S(2)}) copy-start(f32[2,256,512]{2,1,0:T(8,128)S(1)} %get-tuple-element.114.refs_2_) | copy-start | bytes 3145732
  75.8 23.9 %collective-permute-start.16 = (bf16[2,256,512]{2,1,0:T(8,128)(2,1)S(1)}, bf16[2,256,512]{2,1,0:T(8,128)(2,1)S(1)}, u32[]{:S(2)}, u32[]{:S(2)}) collective-permute-start(bf16[2,256,512]{2,1,0:T(8,128)(2,1)S(1)} %bitcast.16), channel_id=1, source_target_pairs={{0,8},{8,0},{16,24},{24,16},{1,9},{9,1},{17,25},{25,17},{2,10},{10... | collective-permute-start | bytes 1572872 | tf_op jit(solution)/shard_map/ppermute | solution.py:505
  76.4 23.3 %collective-permute-start.17 = (bf16[2,256,512]{2,1,0:T(8,128)(2,1)S(1)}, bf16[2,256,512]{2,1,0:T(8,128)(2,1)S(1)}, u32[]{:S(2)}, u32[]{:S(2)}) collective-permute-start(bf16[2,256,512]{2,1,0:T(8,128)(2,1)S(1)} %bitcast.15), channel_id=1, source_target_pairs={{0,16},{8,24},{16,0},{24,8},{1,17},{9,25},{17,1},{25,9},{2,18},{10... | collective-permute-start | bytes 1572872 | tf_op jit(solution)/shard_map/ppermute | solution.py:509
  77.2 0.7 copy-start.20
  77.9 5.1 %copy-start.14 = (f32[128,1024]{1,0:T(8,128)}, f32[128,1024]{1,0:T(8,128)S(1)}, u32[]{:S(2)}) copy-start(f32[128,1024]{1,0:T(8,128)S(1)} %get-tuple-element.124.refs_0_) | copy-start | bytes 1572868
  77.9 5.1 %copy-start.16 = (f32[128,1024]{1,0:T(8,128)}, f32[128,1024]{1,0:T(8,128)S(1)}, u32[]{:S(2)}) copy-start(f32[128,1024]{1,0:T(8,128)S(1)} %get-tuple-element.126.refs_2_) | copy-start | bytes 1572868
  83.0 10.3 %collective-permute-start.15 = (bf16[544,1024]{1,0:T(8,128)(2,1)S(1)}, bf16[544,1024]{1,0:T(8,128)(2,1)S(1)}, u32[]{:S(2)}, u32[]{:S(2)}) collective-permute-start(bf16[544,1024]{1,0:T(8,128)(2,1)S(1)} %get-tuple-element.107), channel_id=1, source_target_pairs={{0,1},{1,0},{2,3},{3,2},{4,5},{5,4},{6,7},{7,6},{8,9},{9,8},{10,11... | collective-permute-start | bytes 3342344 | tf_op jit(solution)/shard_map/ppermute | solution.py:497
  86.7 6.7 %copy-start.6 = (f32[2,256,512]{2,1,0:T(8,128)}, f32[2,256,512]{2,1,0:T(8,128)S(1)}, u32[]{:S(2)}) copy-start(f32[2,256,512]{2,1,0:T(8,128)S(1)} %get-tuple-element.128.refs_0_) | copy-start | bytes 3145732
  86.7 6.7 %copy-start.8 = (f32[2,256,512]{2,1,0:T(8,128)}, f32[2,256,512]{2,1,0:T(8,128)S(1)}, u32[]{:S(2)}) copy-start(f32[2,256,512]{2,1,0:T(8,128)S(1)} %get-tuple-element.130.refs_2_) | copy-start | bytes 3145732
  91.5 13.9 %collective-permute-start.22 = (bf16[2,256,512]{2,1,0:T(8,128)(2,1)}, bf16[2,256,512]{2,1,0:T(8,128)(2,1)}, u32[]{:S(2)}, u32[]{:S(2)}) collective-permute-start(bf16[2,256,512]{2,1,0:T(8,128)(2,1)} %bitcast.12), channel_id=1, source_target_pairs={{0,8},{8,0},{16,24},{24,16},{1,9},{9,1},{17,25},{25,17},{2,10},{10... | collective-permute-start | bytes 1572872 | tf_op jit(solution)/shard_map/ppermute | solution.py:505
  92.0 15.1 %collective-permute-start.23 = (bf16[2,256,512]{2,1,0:T(8,128)(2,1)}, bf16[2,256,512]{2,1,0:T(8,128)(2,1)}, u32[]{:S(2)}, u32[]{:S(2)}) collective-permute-start(bf16[2,256,512]{2,1,0:T(8,128)(2,1)} %bitcast.13), channel_id=1, source_target_pairs={{0,16},{8,24},{16,0},{24,8},{1,17},{9,25},{17,1},{25,9},{2,18},{10... | collective-permute-start | bytes 1572872 | tf_op jit(solution)/shard_map/ppermute | solution.py:509
  95.1 29.5 %all-to-all-start = ((bf16[4,136,1024]{2,1,0:T(8,128)(2,1)}), bf16[4,136,1024]{2,1,0:T(8,128)(2,1)S(1)}, u32[]{:S(2)}, u32[]{:S(2)}) async-start(bf16[4,136,1024]{2,1,0:T(8,128)(2,1)} %bitcast.7), calls=%async_computation | async-start | bytes 2228224 | tf_op jit(solution)/shard_map/all_to_all | solution.py:556
  98.7 1.0 copy-start.21
  99.6 1.2 copy-start.11
  99.6 1.5 %copy-start.13 = (f32[2,256,512]{2,1,0:T(8,128)S(1)}, f32[2,256,512]{2,1,0:T(8,128)}, u32[]{:S(2)}) copy-start(f32[2,256,512]{2,1,0:T(8,128)} %copy-done.12) | copy-start | bytes 3145732
  101.2 5.9 %copy-start.7 = (f32[2,256,512]{2,1,0:T(8,128)S(1)}, f32[2,256,512]{2,1,0:T(8,128)}, u32[]{:S(2)}) copy-start(f32[2,256,512]{2,1,0:T(8,128)} %copy-done.6) | copy-start | bytes 3145732
  101.2 5.9 %copy-start.9 = (f32[2,256,512]{2,1,0:T(8,128)S(1)}, f32[2,256,512]{2,1,0:T(8,128)}, u32[]{:S(2)}) copy-start(f32[2,256,512]{2,1,0:T(8,128)} %copy-done.8) | copy-start | bytes 3145732
  101.4 19.4 %collective-permute-start.18 = (bf16[256,512]{1,0:T(8,128)(2,1)S(1)}, bf16[256,512]{1,0:T(8,128)(2,1)S(1)}, u32[]{:S(2)}, u32[]{:S(2)}) collective-permute-start(bf16[256,512]{1,0:T(8,128)(2,1)S(1)} %get-tuple-element.121), channel_id=1, source_target_pairs={{0,16},{8,24},{16,0},{24,8},{1,17},{9,25},{17,1},{25,9},{2,18},{10... | collective-permute-start | bytes 786440 | tf_op jit(solution)/shard_map/ppermute | solution.py:509
  103.0 17.9 %collective-permute-start.19 = (bf16[256,512]{1,0:T(8,128)(2,1)S(1)}, bf16[256,512]{1,0:T(8,128)(2,1)S(1)}, u32[]{:S(2)}, u32[]{:S(2)}) collective-permute-start(bf16[256,512]{1,0:T(8,128)(2,1)S(1)} %get-tuple-element.123), channel_id=1, source_target_pairs={{0,8},{8,0},{16,24},{24,16},{1,9},{9,1},{17,25},{25,17},{2,10},{10... | collective-permute-start | bytes 786440 | tf_op jit(solution)/shard_map/ppermute | solution.py:505
  104.5 13.8 %collective-permute-start.20 = (bf16[128,1024]{1,0:T(8,128)(2,1)S(1)}, bf16[128,1024]{1,0:T(8,128)(2,1)S(1)}, u32[]{:S(2)}, u32[]{:S(2)}) collective-permute-start(bf16[128,1024]{1,0:T(8,128)(2,1)S(1)} %get-tuple-element.125), channel_id=1, source_target_pairs={{0,16},{8,24},{16,0},{24,8},{1,17},{9,25},{17,1},{25,9},{2,18},{10... | collective-permute-start | bytes 786440 | tf_op jit(solution)/shard_map/ppermute | solution.py:509
  105.4 14.4 %collective-permute-start.21 = (bf16[128,1024]{1,0:T(8,128)(2,1)S(1)}, bf16[128,1024]{1,0:T(8,128)(2,1)S(1)}, u32[]{:S(2)}, u32[]{:S(2)}) collective-permute-start(bf16[128,1024]{1,0:T(8,128)(2,1)S(1)} %get-tuple-element.127), channel_id=1, source_target_pairs={{0,8},{8,0},{16,24},{24,16},{1,9},{9,1},{17,25},{25,17},{2,10},{10... | collective-permute-start | bytes 786440 | tf_op jit(solution)/shard_map/ppermute | solution.py:505
  107.1 12.6 %copy-start.15 = (f32[128,1024]{1,0:T(8,128)S(1)}, f32[128,1024]{1,0:T(8,128)}, u32[]{:S(2)}) copy-start(f32[128,1024]{1,0:T(8,128)} %copy-done.14) | copy-start | bytes 1572868
  107.1 12.6 %copy-start.17 = (f32[128,1024]{1,0:T(8,128)S(1)}, f32[128,1024]{1,0:T(8,128)}, u32[]{:S(2)}) copy-start(f32[128,1024]{1,0:T(8,128)} %copy-done.16) | copy-start | bytes 1572868
  108.7 12.2 %copy-start.18 = (f32[256,512]{1,0:T(8,128)}, f32[256,512]{1,0:T(8,128)S(1)}, u32[]{:S(2)}) copy-start(f32[256,512]{1,0:T(8,128)S(1)} %get-tuple-element.138.refs_2_) | copy-start | bytes 1572868
  108.7 16.8 %collective-permute-start.24 = (bf16[256,512]{1,0:T(8,128)(2,1)S(1)}, bf16[256,512]{1,0:T(8,128)(2,1)S(1)}, u32[]{:S(2)}, u32[]{:S(2)}) collective-permute-start(bf16[256,512]{1,0:T(8,128)(2,1)S(1)} %get-tuple-element.137), channel_id=1, source_target_pairs={{0,16},{8,24},{16,0},{24,8},{1,17},{9,25},{17,1},{25,9},{2,18},{10... | collective-permute-start | bytes 786440 | tf_op jit(solution)/shard_map/ppermute | solution.py:509
  118.2 7.2 %collective-permute-start.25 = (bf16[256,512]{1,0:T(8,128)(2,1)S(1)}, bf16[256,512]{1,0:T(8,128)(2,1)S(1)}, u32[]{:S(2)}, u32[]{:S(2)}) collective-permute-start(bf16[256,512]{1,0:T(8,128)(2,1)S(1)} %get-tuple-element.139), channel_id=1, source_target_pairs={{0,8},{8,0},{16,24},{24,16},{1,9},{9,1},{17,25},{25,17},{2,10},{10... | collective-permute-start | bytes 786440 | tf_op jit(solution)/shard_map/ppermute | solution.py:505
  120.8 3.8 %copy-start.5 = (s32[128,8]{0,1:T(8,128)S(1)}, s32[128,8]{0,1:T(8,128)}, u32[]{:S(2)}) copy-start(s32[128,8]{0,1:T(8,128)} %param.8) | copy-start | bytes 12292
  124.6 1.1 copy-start.19

commit v4 on v3

--- a/solution.py
+++ b/solution.py
@@ -603,7 +603,7 @@
     token_grads, route_grads_t, rows_done = sum_rows_and_routes(
         tg_got, routes.T, nz, e_total, "token_rows"
     )
-    up_grads, _ = add_second(up_totals, up_got, n, "up_second", gate_done, rows_done)
+    up_grads, _ = add_second(up_totals, up_got, n, "up_second", gate_done)
     route_grads = route_grads_t.T
 
     return (layer_out, token_grads, route_grads, gate_grads, up_grads, down_grads)

time: 127 us -> 127 us (level)
    all_to_all x1, waiting for transfers between devices: 2.7 us -> 0.01 us  [send_home(): lax.all_to_all(parts, 'expert', split_axis=0, concat_axis=0, tiled=True,...]
    ppermute x6, waiting for transfers between devices: 0.38 us -> 3.08 us  [move_x(): return lax.ppermute(v, 'dp', pairs)]
    unnamed x44 -> x40, local copies, waits for them, and re-layouts: 4.61 us -> 4.37 us
where the time goes in v4:
time: 127 us
  waiting for transfers between devices  41.6 us (33%)
  starting transfers between devices  40.6 us (32%)
  Pallas kernels  39 us (31%)
  local copies, waits for them, and re-layouts  4.38 us (3%)
    pallas_call x20, Pallas kernels, on_chip(): pl.pallas_call(body, in_specs=[SMEM] * scalars + [VMEM] * (len(operands)...  37.3 us
    ppermute x7, waiting for transfers between devices, move_z(): return lax.ppermute(v, 'expert', pairs)  19.5 us
    ppermute x7, starting transfers between devices, move_z(): return lax.ppermute(v, 'expert', pairs)  18.9 us
    ppermute x6, waiting for transfers between devices, move_y(): return lax.ppermute(v, 'dp', pairs)  11.1 us
    ppermute x3, waiting for transfers between devices, near_rows(): send = lambda u, pairs: lax.ppermute(u, 'expert', chip_pairs(pairs))  7.49 us
    ppermute x3, starting transfers between devices, near_rows(): send = lambda u, pairs: lax.ppermute(u, 'expert', chip_pairs(pairs))  7.12 us
    ppermute x6, starting transfers between devices, move_x(): return lax.ppermute(v, 'dp', pairs)  5.71 us
    ppermute x6, starting transfers between devices, move_y(): return lax.ppermute(v, 'dp', pairs)  4.7 us
  transfers between devices with their start and end apart: 27, of which 10 were waited for; matrix products, arithmetic and copies ran while one was open for 0% of the time, Pallas kernels for 28%

profile of v4, /device:TPU:0, one launch (start us, length us, event | category | flops | bytes accessed | tf_op | source)
XLA Modules:
  0.0 126.6 jit_solution(9221182264158193150)
XLA Ops:
  0.6 1.7 %pack_tokens.1.own_ref = bf16[136,1024]{1,0:T(8,128)(2,1)} custom-call(bf16[128,1024]{1,0:T(8,128)(2,1)} %tok_hbm.1, s32[8,128]{1,0:T(8,128)} %bitcast.19, f32[8,128]{1,0:T(8,128)} %bitcast.21), custom_call_target="tpu_custom_call" | custom-call | flops 10000000000 | bytes 1048576 | tf_op jit(solution)/shard_map/pack_tokens/pallas_call | solution.py:86
  2.4 4.1 %collective-permute-start = (bf16[136,1024]{1,0:T(8,128)(2,1)}, bf16[136,1024]{1,0:T(8,128)(2,1)S(1)}, u32[]{:S(2)}, u32[]{:S(2)}) collective-permute-start(bf16[136,1024]{1,0:T(8,128)(2,1)} %pack_tokens.1.own_ref), channel_id=1, source_target_pairs={{0,4},{1,5},{2,6},{3,7},{4,0},{5,1},{6,2},{7,3},{8,12},{9,13},{10,... | collective-permute-start | bytes 835592 | tf_op jit(solution)/shard_map/ppermute | solution.py:501
  6.5 1.3 %collective-permute-start.2 = (bf16[136,1024]{1,0:T(8,128)(2,1)}, bf16[136,1024]{1,0:T(8,128)(2,1)S(1)}, u32[]{:S(2)}, u32[]{:S(2)}) collective-permute-start(bf16[136,1024]{1,0:T(8,128)(2,1)} %pack_tokens.1.own_ref), channel_id=1, source_target_pairs={{2,0},{3,1},{4,2},{5,3},{6,4},{7,5},{10,8},{11,9},{12,10},{13,11},... | collective-permute-start | bytes 835592 | tf_op jit(solution)/shard_map/ppermute | solution.py:520
  7.7 4.6 %collective-permute-start.1 = (bf16[136,1024]{1,0:T(8,128)(2,1)}, bf16[136,1024]{1,0:T(8,128)(2,1)S(1)}, u32[]{:S(2)}, u32[]{:S(2)}) collective-permute-start(bf16[136,1024]{1,0:T(8,128)(2,1)} %pack_tokens.1.own_ref), channel_id=1, source_target_pairs={{0,2},{1,3},{2,4},{3,5},{4,6},{5,7},{8,10},{9,11},{10,12},{11,13},... | collective-permute-start | bytes 835592 | tf_op jit(solution)/shard_map/ppermute | solution.py:520
  12.3 7.9 %collective-permute-done.two_ref = bf16[136,1024]{1,0:T(8,128)(2,1)S(1)} collective-permute-done((bf16[136,1024]{1,0:T(8,128)(2,1)}, bf16[136,1024]{1,0:T(8,128)(2,1)S(1)}, u32[]{:S(2)}, u32[]{:S(2)}) %collective-permute-start) | collective-permute-done | bytes 278560 | tf_op jit(solution)/shard_map/ppermute | solution.py:501
  20.2 1.3 %collective-permute-start.3 = (bf16[136,1024]{1,0:T(8,128)(2,1)S(1)}, bf16[136,1024]{1,0:T(8,128)(2,1)S(1)}, u32[]{:S(2)}, u32[]{:S(2)}) collective-permute-start(bf16[136,1024]{1,0:T(8,128)(2,1)S(1)} %collective-permute-done.two_ref), channel_id=1, source_target_pairs={{4,6},{5,7},{2,0},{3,1},{12,14},{13,15},{10,8},{11,9},{20,22},{21,... | collective-permute-start | bytes 835592 | tf_op jit(solution)/shard_map/ppermute | solution.py:520
  21.5 0.1 pad_add_fusion.place_ref.refs_0_
  21.6 7.5 %collective-permute-done.3.relayed_ref = bf16[136,1024]{1,0:T(8,128)(2,1)S(1)} collective-permute-done((bf16[136,1024]{1,0:T(8,128)(2,1)S(1)}, bf16[136,1024]{1,0:T(8,128)(2,1)S(1)}, u32[]{:S(2)}, u32[]{:S(2)}) %collective-permute-start.3) | collective-permute-done | bytes 278560 | tf_op jit(solution)/shard_map/ppermute | solution.py:520
  29.1 1.0 copy-done.3
  30.0 0.6 collect.2.near_in
  30.7 0.1 collective-permute-start.4
  30.7 0.2 copy-done.4
  31.0 2.4 %collective-permute-start.7 = (bf16[128,1024]{1,0:T(8,128)(2,1)S(1)}, bf16[128,1024]{1,0:T(8,128)(2,1)S(1)}, u32[]{:S(2)}, u32[]{:S(2)}) collective-permute-start(bf16[128,1024]{1,0:T(8,128)(2,1)S(1)} %copy-done.4), channel_id=1, source_target_pairs={{0,4},{1,5},{2,6},{3,7},{4,0},{5,1},{6,2},{7,3},{8,12},{9,13},{10,... | collective-permute-start | bytes 786440 | tf_op jit(solution)/shard_map/ppermute | solution.py:501
  33.3 2.5 %collective-permute-start.6 = (bf16[128,1024]{1,0:T(8,128)(2,1)S(1)}, bf16[128,1024]{1,0:T(8,128)(2,1)S(1)}, u32[]{:S(2)}, u32[]{:S(2)}) collective-permute-start(bf16[128,1024]{1,0:T(8,128)(2,1)S(1)} %copy-done.4), channel_id=1, source_target_pairs={{0,2},{1,3},{2,4},{3,5},{4,6},{5,7},{6,0},{7,1},{8,10},{9,11},{10,... | collective-permute-start | bytes 786440 | tf_op jit(solution)/shard_map/ppermute | solution.py:501
  35.8 1.3 %collective-permute-start.8 = (bf16[128,1024]{1,0:T(8,128)(2,1)S(1)}, bf16[128,1024]{1,0:T(8,128)(2,1)S(1)}, u32[]{:S(2)}, u32[]{:S(2)}) collective-permute-start(bf16[128,1024]{1,0:T(8,128)(2,1)S(1)} %copy-done.4), channel_id=1, source_target_pairs={{0,6},{1,7},{2,0},{3,1},{4,2},{5,3},{6,4},{7,5},{8,14},{9,15},{10,... | collective-permute-start | bytes 786440 | tf_op jit(solution)/shard_map/ppermute | solution.py:501
  37.2 9.2 %forward.1 = (bf16[512,1024]{1,0:T(8,128)(2,1)S(1)}, bf16[512,1024]{1,0:T(8,128)(2,1)S(1)}, bf16[512,1024]{1,0:T(8,128)(2,1)S(1)}, bf16[512,1024]{1,0:T(8,128)(2...) custom-call(s32[3]{0:T(128)S(1)} %pad_add_fusion.place_ref.refs_0_, ...), custom_call_target="tpu_custom_call" | custom-call | flops 10000000000 | bytes 22155276 | tf_op jit(solution)/shard_map/forward/pallas_call | solution.py:32
  46.4 5.9 %collective-permute-done.7.refs_2_ = bf16[128,1024]{1,0:T(8,128)(2,1)S(1)} collective-permute-done((bf16[128,1024]{1,0:T(8,128)(2,1)S(1)}, bf16[128,1024]{1,0:T(8,128)(2,1)S(1)}, u32[]{:S(2)}, u32[]{:S(2)}) %collective-permute-start.7) | collective-permute-done | bytes 262176 | tf_op jit(solution)/shard_map/ppermute | solution.py:501
  52.3 0.9 collective-permute-done.8.refs_3_
  53.2 0.1 collect.3.refs_0_
  53.3 0.1 collective-permute-start.9
  53.4 0.5 collective-permute-start.5
  53.9 1.8 %hidden_grads.2 = (bf16[512,1024]{1,0:T(8,128)(2,1)S(1)}, bf16[512,1024]{1,0:T(8,128)(2,1)S(1)}, f32[512,128]{1,0:T(8,128)S(1)}, f32[8,128]{1,0:T(8,128)S(1)}) custom-call(bf16[512,1024]{1,0:T(8,128)(2,1)S(1)} %collect.3.refs_0_, bf16[512,1024]{1,0:T(8,128)(2,1)S(1)} %get-tuple-element.78.refs_1_, bf16[512,1024]{1,0:T(8,128)(2,1)S(1)} %get-tuple-element.79.refs_2_, ...), custom_call_target="tpu_custom_call" | custom-call | flops 10000000000 | bytes 8654848 | tf_op jit(solution)/shard_map/hidden_grads/pallas_call | solution.py:32
  55.6 0.4 collective-permute-done.9.refs_1_.refs_0_
  56.0 2.9 %down_partials.1 = (bf16[1,2,128,1024]{3,2,1,0:T(8,128)(2,1)S(1)}, f32[2,128,1024]{2,1,0:T(8,128)S(1)}, bf16[1,2,128,1024]{3,2,1,0:T(8,128)(2,1)S(1)}, f32[2,128,1024]{2,1,0:T(8,128)S(1)}, f32[8,128]{1,0:T(8,128)S(1)}) custom-call(s32[3]{0:T(128)S(1)} %pad_add_fusion.place_ref.refs_0_, bf16[1024,1024]{1,0:T(8,128)(2,1)S(1)} %get-tuple-element.76.left_ref, ...), custom_call_target="tpu_custom_call" | custom-call | flops 10000000000 | bytes 7348236 | tf_op jit(solution)/shard_map/down_partials/pallas_call | solution.py:32
  58.9 1.4 %collective-permute-start.13 = (bf16[2,128,1024]{2,1,0:T(8,128)(2,1)S(1)}, bf16[2,128,1024]{2,1,0:T(8,128)(2,1)S(1)}, u32[]{:S(2)}, u32[]{:S(2)}) collective-permute-start(bf16[2,128,1024]{2,1,0:T(8,128)(2,1)S(1)} %bitcast.18), channel_id=1, source_target_pairs={{0,8},{8,0},{16,24},{24,16},{1,9},{9,1},{17,25},{25,17},{2,10},{10... | collective-permute-start | bytes 1572872 | tf_op jit(solution)/shard_map/ppermute | solution.py:505
  60.4 1.5 %collective-permute-start.14 = (bf16[2,128,1024]{2,1,0:T(8,128)(2,1)S(1)}, bf16[2,128,1024]{2,1,0:T(8,128)(2,1)S(1)}, u32[]{:S(2)}, u32[]{:S(2)}) collective-permute-start(bf16[2,128,1024]{2,1,0:T(8,128)(2,1)S(1)} %bitcast.17), channel_id=1, source_target_pairs={{0,16},{8,24},{16,0},{24,8},{1,17},{9,25},{17,1},{25,9},{2,18},{10... | collective-permute-start | bytes 1572872 | tf_op jit(solution)/shard_map/ppermute | solution.py:509
  61.9 0.2 out_sides.1
  62.1 1.9 %collective-permute-start.10 = (bf16[128,1024]{1,0:T(8,128)(2,1)S(1)}, bf16[128,1024]{1,0:T(8,128)(2,1)S(1)}, u32[]{:S(2)}, u32[]{:S(2)}) collective-permute-start(bf16[128,1024]{1,0:T(8,128)(2,1)S(1)} %get-tuple-element.84), channel_id=1, source_target_pairs={{0,6},{1,7},{2,0},{3,1},{4,2},{5,3},{6,4},{7,5},{8,14},{9,15},{10,... | collective-permute-start | bytes 786440 | tf_op jit(solution)/shard_map/ppermute | solution.py:501
  64.0 4.7 %collective-permute-start.11 = (bf16[128,1024]{1,0:T(8,128)(2,1)S(1)}, bf16[128,1024]{1,0:T(8,128)(2,1)S(1)}, u32[]{:S(2)}, u32[]{:S(2)}) collective-permute-start(bf16[128,1024]{1,0:T(8,128)(2,1)S(1)} %get-tuple-element.85), channel_id=1, source_target_pairs={{0,4},{1,5},{2,6},{3,7},{4,0},{5,1},{6,2},{7,3},{8,12},{9,13},{10,... | collective-permute-start | bytes 786440 | tf_op jit(solution)/shard_map/ppermute | solution.py:501
  68.7 1.9 %collective-permute-start.12 = (bf16[128,1024]{1,0:T(8,128)(2,1)S(1)}, bf16[128,1024]{1,0:T(8,128)(2,1)S(1)}, u32[]{:S(2)}, u32[]{:S(2)}) collective-permute-start(bf16[128,1024]{1,0:T(8,128)(2,1)S(1)} %get-tuple-element.86), channel_id=1, source_target_pairs={{0,2},{1,3},{2,4},{3,5},{4,6},{5,7},{6,0},{7,1},{8,10},{9,11},{10,... | collective-permute-start | bytes 786440 | tf_op jit(solution)/shard_map/ppermute | solution.py:501
  70.6 2.3 %hidden_grads.3 = (bf16[512,1024]{1,0:T(8,128)(2,1)S(1)}, bf16[512,1024]{1,0:T(8,128)(2,1)S(1)}, f32[512,128]{1,0:T(8,128)S(1)}, f32[8,128]{1,0:T(8,128)}) custom-call(bf16[512,1024]{1,0:T(8,128)(2,1)S(1)} %collective-permute-done.9.refs_1_.refs_0_, bf16[512,1024]{1,0:T(8,128)(2,1)S(1)} %get-tuple-element.89.refs_1_, ...), custom_call_target="tpu_custom_call" | custom-call | flops 10000000000 | bytes 8658944 | tf_op jit(solution)/shard_map/hidden_grads/pallas_call | solution.py:32
  72.9 2.9 %gate_partials.1 = (bf16[1,2,256,512]{3,2,1,0:T(8,128)(2,1)S(1)}, f32[2,256,512]{2,1,0:T(8,128)S(1)}, bf16[1,2,256,512]{3,2,1,0:T(8,128)(2,1)S(1)}, f32[2,256,512]{2,1,0:T(8,128)S(1)}, f32[8,128]{1,0:T(8,128)S(1)}) custom-call(s32[3]{0:T(128)S(1)} %pad_add_fusion.place_ref.refs_0_, bf16[1024,1024]{1,0:T(8,128)(2,1)S(1)} %get-tuple-element.87.left_ref, ...), custom_call_target="tpu_custom_call" | custom-call | flops 10000000000 | bytes 7344140 | tf_op jit(solution)/shard_map/gate_partials/pallas_call | solution.py:32
  75.8 0.6 collective-permute-start.16
  76.4 0.5 collective-permute-start.17
  76.9 0.2 down_first.1
  77.2 0.7 copy-done.18
  77.9 5.1 %token_partials.1 = (f32[544,1024]{1,0:T(8,128)S(1)}, bf16[544,1024]{1,0:T(8,128)(2,1)S(1)}) custom-call(s32[3]{0:T(128)S(1)} %pad_add_fusion.place_ref.refs_0_, bf16[512,1024]{1,0:T(8,128)(2,1)S(1)} %get-tuple-element.93.refs_0_.refs_1_, bf16[512,1024]{1,0:T(8,128)(2,1)S(1)} %get-tuple-element.94.refs_1_.refs_2_, ...), custom_call_target="tpu_custom_call" | custom-call | flops 10000000000 | bytes 12259340 | tf_op jit(solution)/shard_map/token_partials/pallas_call | solution.py:32
  83.0 0.1 collective-permute-start.15
  83.1 3.5 %up_partials.1 = (bf16[1,2,256,512]{3,2,1,0:T(8,128)(2,1)}, f32[2,256,512]{2,1,0:T(8,128)S(1)}, bf16[1,2,256,512]{3,2,1,0:T(8,128)(2,1)}, f32[2,256,512]{2,1,0:T(8,128)S(1)}, f32[8,128]{1,0:T(8,128)S(1)}) custom-call(s32[3]{0:T(128)S(1)} %pad_add_fusion.place_ref.refs_0_, bf16[1024,1024]{1,0:T(8,128)(2,1)S(1)} %get-tuple-element.87.left_ref, ...), custom_call_target="tpu_custom_call" | custom-call | flops 10000000000 | bytes 7348236 | tf_op jit(solution)/shard_map/up_partials/pallas_call | solution.py:32
  86.7 4.8 %collective-permute-done.11.refs_2_ = bf16[128,1024]{1,0:T(8,128)(2,1)S(1)} collective-permute-done((bf16[128,1024]{1,0:T(8,128)(2,1)S(1)}, bf16[128,1024]{1,0:T(8,128)(2,1)S(1)}, u32[]{:S(2)}, u32[]{:S(2)}) %collective-permute-start.11) | collective-permute-done | bytes 262176 | tf_op jit(solution)/shard_map/ppermute | solution.py:501
  91.5 0.5 collective-permute-start.22
  92.0 0.5 collective-permute-start.23
  92.5 0.8 out_rows.1
  93.4 1.8 %token_sides.1 = (bf16[544,1024]{1,0:T(8,128)(2,1)}, f32[8,128]{1,0:T(8,128)S(1)}) custom-call(s32[3]{0:T(128)S(1)} %pad_add_fusion.place_ref.refs_0_, f32[544,1024]{1,0:T(8,128)S(1)} %get-tuple-element.103.near_ref, bf16[544,1024]{1,0:T(8,128)(2,1)S(1)} %collective-permute-done.15.far_ref, f32[8,128]{1,0:T(8,128)S(1)} %get-tuple-element.107.refs_0_), custom_call_target="tpu_custom_call" | custom-call | flops 10000000000 | bytes 4464652 | tf_op jit(solution)/shard_map/token_sides/pallas_call | solution.py:32
  95.1 3.5 %all-to-all-start = ((bf16[4,136,1024]{2,1,0:T(8,128)(2,1)}), bf16[4,136,1024]{2,1,0:T(8,128)(2,1)S(1)}, u32[]{:S(2)}, u32[]{:S(2)}) async-start(bf16[4,136,1024]{2,1,0:T(8,128)(2,1)} %bitcast.7), calls=%async_computation | async-start | bytes 2228224 | tf_op jit(solution)/shard_map/all_to_all | solution.py:556
  98.7 0.9 copy-done.19
  99.7 1.2 copy-done.11
  100.8 0.3 copy-done.13
  101.2 0.2 gate_first.1
  101.4 1.6 %collective-permute-start.18 = (bf16[256,512]{1,0:T(8,128)(2,1)S(1)}, bf16[256,512]{1,0:T(8,128)(2,1)S(1)}, u32[]{:S(2)}, u32[]{:S(2)}) collective-permute-start(bf16[256,512]{1,0:T(8,128)(2,1)S(1)} %get-tuple-element.120), channel_id=1, source_target_pairs={{0,16},{8,24},{16,0},{24,8},{1,17},{9,25},{17,1},{25,9},{2,18},{10... | collective-permute-start | bytes 786440 | tf_op jit(solution)/shard_map/ppermute | solution.py:509
  103.0 1.5 %collective-permute-start.19 = (bf16[256,512]{1,0:T(8,128)(2,1)S(1)}, bf16[256,512]{1,0:T(8,128)(2,1)S(1)}, u32[]{:S(2)}, u32[]{:S(2)}) collective-permute-start(bf16[256,512]{1,0:T(8,128)(2,1)S(1)} %get-tuple-element.122), channel_id=1, source_target_pairs={{0,8},{8,0},{16,24},{24,16},{1,9},{9,1},{17,25},{25,17},{2,10},{10... | collective-permute-start | bytes 786440 | tf_op jit(solution)/shard_map/ppermute | solution.py:505
  104.5 0.5 collective-permute-start.20
  105.0 0.4 collective-permute-done.22.refs_1_
  105.4 0.2 collective-permute-start.21
  105.5 1.6 %collective-permute-done.23.refs_3_ = bf16[2,256,512]{2,1,0:T(8,128)(2,1)} collective-permute-done((bf16[2,256,512]{2,1,0:T(8,128)(2,1)}, bf16[2,256,512]{2,1,0:T(8,128)(2,1)}, u32[]{:S(2)}, u32[]{:S(2)}) %collective-permute-start.23) | collective-permute-done | bytes 524320 | tf_op jit(solution)/shard_map/ppermute | solution.py:509
  107.1 1.5 %up_first.1 = (f32[256,512]{1,0:T(8,128)S(1)}, bf16[256,512]{1,0:T(8,128)(2,1)S(1)}, f32[256,512]{1,0:T(8,128)S(1)}, bf16[256,512]{1,0:T(8,128)(2,1)S(1)}, f32[8,128]{1,0:T(8,128)S(1)}) custom-call(f32[2,256,512]{2,1,0:T(8,128)S(1)} %copy-done.7, bf16[2,256,512]{2,1,0:T(8,128)(2,1)} %collective-permute-done.22.refs_1_, f32[2,256,512]{2,1,0:T(8,128)S(1)} %copy-done.9, ...), custom_call_target="tpu_custom_call" | custom-call | flops 10000000000 | bytes 4726784 | tf_op jit(solution)/shard_map/up_first/pallas_call | solution.py:32
  108.7 0.1 collective-permute-start.24
  108.7 9.5 %collective-permute-done.20.refs_1_ = bf16[128,1024]{1,0:T(8,128)(2,1)S(1)} collective-permute-done((bf16[128,1024]{1,0:T(8,128)(2,1)S(1)}, bf16[128,1024]{1,0:T(8,128)(2,1)S(1)}, u32[]{:S(2)}, u32[]{:S(2)}) %collective-permute-start.20) | collective-permute-done | bytes 262176 | tf_op jit(solution)/shard_map/ppermute | solution.py:509
  118.2 1.5 %collective-permute-start.25 = (bf16[256,512]{1,0:T(8,128)(2,1)S(1)}, bf16[256,512]{1,0:T(8,128)(2,1)S(1)}, u32[]{:S(2)}, u32[]{:S(2)}) collective-permute-start(bf16[256,512]{1,0:T(8,128)(2,1)S(1)} %get-tuple-element.138), channel_id=1, source_target_pairs={{0,8},{8,0},{16,24},{24,16},{1,9},{9,1},{17,25},{25,17},{2,10},{10... | collective-permute-start | bytes 786440 | tf_op jit(solution)/shard_map/ppermute | solution.py:505
  119.8 1.1 down_second.1
  120.8 1.1 gate_second.1
  121.9 2.7 %collective-permute-done.25.refs_3_ = bf16[256,512]{1,0:T(8,128)(2,1)S(1)} collective-permute-done((bf16[256,512]{1,0:T(8,128)(2,1)S(1)}, bf16[256,512]{1,0:T(8,128)(2,1)S(1)}, u32[]{:S(2)}, u32[]{:S(2)}) %collective-permute-start.25) | collective-permute-done | bytes 262176 | tf_op jit(solution)/shard_map/ppermute | solution.py:505
  124.6 1.1 up_second.1
  125.7 0.9 token_rows.1
  (53 shorter events, 0.2 us)
Async XLA Ops:
  2.4 17.8 %collective-permute-start = (bf16[136,1024]{1,0:T(8,128)(2,1)}, bf16[136,1024]{1,0:T(8,128)(2,1)S(1)}, u32[]{:S(2)}, u32[]{:S(2)}) collective-permute-start(bf16[136,1024]{1,0:T(8,128)(2,1)} %pack_tokens.1.own_ref), channel_id=1, source_target_pairs={{0,4},{1,5},{2,6},{3,7},{4,0},{5,1},{6,2},{7,3},{8,12},{9,13},{10,... | collective-permute-start | bytes 835592 | tf_op jit(solution)/shard_map/ppermute | solution.py:501
  6.5 15.1 %collective-permute-start.2 = (bf16[136,1024]{1,0:T(8,128)(2,1)}, bf16[136,1024]{1,0:T(8,128)(2,1)S(1)}, u32[]{:S(2)}, u32[]{:S(2)}) collective-permute-start(bf16[136,1024]{1,0:T(8,128)(2,1)} %pack_tokens.1.own_ref), channel_id=1, source_target_pairs={{2,0},{3,1},{4,2},{5,3},{6,4},{7,5},{10,8},{11,9},{12,10},{13,11},... | collective-permute-start | bytes 835592 | tf_op jit(solution)/shard_map/ppermute | solution.py:520
  7.7 13.8 %collective-permute-start.1 = (bf16[136,1024]{1,0:T(8,128)(2,1)}, bf16[136,1024]{1,0:T(8,128)(2,1)S(1)}, u32[]{:S(2)}, u32[]{:S(2)}) collective-permute-start(bf16[136,1024]{1,0:T(8,128)(2,1)} %pack_tokens.1.own_ref), channel_id=1, source_target_pairs={{0,2},{1,3},{2,4},{3,5},{4,6},{5,7},{8,10},{9,11},{10,12},{11,13},... | collective-permute-start | bytes 835592 | tf_op jit(solution)/shard_map/ppermute | solution.py:520
  20.2 8.9 %collective-permute-start.3 = (bf16[136,1024]{1,0:T(8,128)(2,1)S(1)}, bf16[136,1024]{1,0:T(8,128)(2,1)S(1)}, u32[]{:S(2)}, u32[]{:S(2)}) collective-permute-start(bf16[136,1024]{1,0:T(8,128)(2,1)S(1)} %collective-permute-done.two_ref), channel_id=1, source_target_pairs={{4,6},{5,7},{2,0},{3,1},{12,14},{13,15},{10,8},{11,9},{20,22},{21,... | collective-permute-start | bytes 835592 | tf_op jit(solution)/shard_map/ppermute | solution.py:520
  21.6 15.6 %copy-start = (bf16[2,512,1024]{2,1,0:T(8,128)(2,1)S(1)}, bf16[2,512,1024]{2,1,0:T(8,128)(2,1)}, u32[]{:S(2)}) copy-start(bf16[2,512,1024]{2,1,0:T(8,128)(2,1)} %refs_4_.3) | copy-start | bytes 6291460
  21.6 15.6 %copy-start.1 = (bf16[2,1024,512]{2,1,0:T(8,128)(2,1)S(1)}, bf16[2,1024,512]{2,1,0:T(8,128)(2,1)}, u32[]{:S(2)}) copy-start(bf16[2,1024,512]{2,1,0:T(8,128)(2,1)} %refs_7_.1) | copy-start | bytes 6291460
  21.6 15.6 %copy-start.2 = (bf16[2,1024,512]{2,1,0:T(8,128)(2,1)S(1)}, bf16[2,1024,512]{2,1,0:T(8,128)(2,1)}, u32[]{:S(2)}) copy-start(bf16[2,1024,512]{2,1,0:T(8,128)(2,1)} %refs_8_.1) | copy-start | bytes 6291460
  29.1 1.0 copy-start.3
  30.0 0.9 copy-start.4
  30.7 6.5 %collective-permute-start.4 = (bf16[544,1024]{1,0:T(8,128)(2,1)S(1)}, bf16[544,1024]{1,0:T(8,128)(2,1)S(1)}, u32[]{:S(2)}, u32[]{:S(2)}) collective-permute-start(bf16[544,1024]{1,0:T(8,128)(2,1)S(1)} %collect.2.near_in), channel_id=1, source_target_pairs={{0,1},{1,0},{2,3},{3,2},{4,5},{5,4},{6,7},{7,6},{8,9},{9,8},{10,11... | collective-permute-start | bytes 3342344 | tf_op jit(solution)/shard_map/ppermute | solution.py:497
  31.0 21.3 %collective-permute-start.7 = (bf16[128,1024]{1,0:T(8,128)(2,1)S(1)}, bf16[128,1024]{1,0:T(8,128)(2,1)S(1)}, u32[]{:S(2)}, u32[]{:S(2)}) collective-permute-start(bf16[128,1024]{1,0:T(8,128)(2,1)S(1)} %copy-done.4), channel_id=1, source_target_pairs={{0,4},{1,5},{2,6},{3,7},{4,0},{5,1},{6,2},{7,3},{8,12},{9,13},{10,... | collective-permute-start | bytes 786440 | tf_op jit(solution)/shard_map/ppermute | solution.py:501
  33.3 19.0 %collective-permute-start.6 = (bf16[128,1024]{1,0:T(8,128)(2,1)S(1)}, bf16[128,1024]{1,0:T(8,128)(2,1)S(1)}, u32[]{:S(2)}, u32[]{:S(2)}) collective-permute-start(bf16[128,1024]{1,0:T(8,128)(2,1)S(1)} %copy-done.4), channel_id=1, source_target_pairs={{0,2},{1,3},{2,4},{3,5},{4,6},{5,7},{6,0},{7,1},{8,10},{9,11},{10,... | collective-permute-start | bytes 786440 | tf_op jit(solution)/shard_map/ppermute | solution.py:501
  35.8 17.4 %collective-permute-start.8 = (bf16[128,1024]{1,0:T(8,128)(2,1)S(1)}, bf16[128,1024]{1,0:T(8,128)(2,1)S(1)}, u32[]{:S(2)}, u32[]{:S(2)}) collective-permute-start(bf16[128,1024]{1,0:T(8,128)(2,1)S(1)} %copy-done.4), channel_id=1, source_target_pairs={{0,6},{1,7},{2,0},{3,1},{4,2},{5,3},{6,4},{7,5},{8,14},{9,15},{10,... | collective-permute-start | bytes 786440 | tf_op jit(solution)/shard_map/ppermute | solution.py:501
  53.3 2.7 %collective-permute-start.9 = (bf16[512,1024]{1,0:T(8,128)(2,1)S(1)}, bf16[512,1024]{1,0:T(8,128)(2,1)S(1)}, u32[]{:S(2)}, u32[]{:S(2)}) collective-permute-start(bf16[512,1024]{1,0:T(8,128)(2,1)S(1)} %collect.3.refs_0_), channel_id=1, source_target_pairs={{0,1},{1,0},{2,3},{3,2},{4,5},{5,4},{6,7},{7,6},{8,9},{9,8},{10,11... | collective-permute-start | bytes 3145736 | tf_op jit(solution)/shard_map/ppermute | solution.py:497
  53.4 8.5 %collective-permute-start.5 = (bf16[512,1024]{1,0:T(8,128)(2,1)S(1)}, bf16[512,1024]{1,0:T(8,128)(2,1)S(1)}, u32[]{:S(2)}, u32[]{:S(2)}) collective-permute-start(bf16[512,1024]{1,0:T(8,128)(2,1)S(1)} %get-tuple-element.75), channel_id=1, source_target_pairs={{0,1},{1,0},{2,3},{3,2},{4,5},{5,4},{6,7},{7,6},{8,9},{9,8},{10,11... | collective-permute-start | bytes 3145736 | tf_op jit(solution)/shard_map/ppermute | solution.py:497
  58.9 17.5 %collective-permute-start.13 = (bf16[2,128,1024]{2,1,0:T(8,128)(2,1)S(1)}, bf16[2,128,1024]{2,1,0:T(8,128)(2,1)S(1)}, u32[]{:S(2)}, u32[]{:S(2)}) collective-permute-start(bf16[2,128,1024]{2,1,0:T(8,128)(2,1)S(1)} %bitcast.18), channel_id=1, source_target_pairs={{0,8},{8,0},{16,24},{24,16},{1,9},{9,1},{17,25},{25,17},{2,10},{10... | collective-permute-start | bytes 1572872 | tf_op jit(solution)/shard_map/ppermute | solution.py:505
  60.4 16.6 %collective-permute-start.14 = (bf16[2,128,1024]{2,1,0:T(8,128)(2,1)S(1)}, bf16[2,128,1024]{2,1,0:T(8,128)(2,1)S(1)}, u32[]{:S(2)}, u32[]{:S(2)}) collective-permute-start(bf16[2,128,1024]{2,1,0:T(8,128)(2,1)S(1)} %bitcast.17), channel_id=1, source_target_pairs={{0,16},{8,24},{16,0},{24,8},{1,17},{9,25},{17,1},{25,9},{2,18},{10... | collective-permute-start | bytes 1572872 | tf_op jit(solution)/shard_map/ppermute | solution.py:509
  62.1 13.8 %collective-permute-start.10 = (bf16[128,1024]{1,0:T(8,128)(2,1)S(1)}, bf16[128,1024]{1,0:T(8,128)(2,1)S(1)}, u32[]{:S(2)}, u32[]{:S(2)}) collective-permute-start(bf16[128,1024]{1,0:T(8,128)(2,1)S(1)} %get-tuple-element.84), channel_id=1, source_target_pairs={{0,6},{1,7},{2,0},{3,1},{4,2},{5,3},{6,4},{7,5},{8,14},{9,15},{10,... | collective-permute-start | bytes 786440 | tf_op jit(solution)/shard_map/ppermute | solution.py:501
  64.0 27.5 %collective-permute-start.11 = (bf16[128,1024]{1,0:T(8,128)(2,1)S(1)}, bf16[128,1024]{1,0:T(8,128)(2,1)S(1)}, u32[]{:S(2)}, u32[]{:S(2)}) collective-permute-start(bf16[128,1024]{1,0:T(8,128)(2,1)S(1)} %get-tuple-element.85), channel_id=1, source_target_pairs={{0,4},{1,5},{2,6},{3,7},{4,0},{5,1},{6,2},{7,3},{8,12},{9,13},{10,... | collective-permute-start | bytes 786440 | tf_op jit(solution)/shard_map/ppermute | solution.py:501
  68.7 23.4 %collective-permute-start.12 = (bf16[128,1024]{1,0:T(8,128)(2,1)S(1)}, bf16[128,1024]{1,0:T(8,128)(2,1)S(1)}, u32[]{:S(2)}, u32[]{:S(2)}) collective-permute-start(bf16[128,1024]{1,0:T(8,128)(2,1)S(1)} %get-tuple-element.86), channel_id=1, source_target_pairs={{0,2},{1,3},{2,4},{3,5},{4,6},{5,7},{6,0},{7,1},{8,10},{9,11},{10,... | collective-permute-start | bytes 786440 | tf_op jit(solution)/shard_map/ppermute | solution.py:501
  75.8 1.4 %copy-start.10 = (f32[2,256,512]{2,1,0:T(8,128)}, f32[2,256,512]{2,1,0:T(8,128)S(1)}, u32[]{:S(2)}) copy-start(f32[2,256,512]{2,1,0:T(8,128)S(1)} %get-tuple-element.111.refs_0_) | copy-start | bytes 3145732
  75.8 1.4 %copy-start.12 = (f32[2,256,512]{2,1,0:T(8,128)}, f32[2,256,512]{2,1,0:T(8,128)S(1)}, u32[]{:S(2)}) copy-start(f32[2,256,512]{2,1,0:T(8,128)S(1)} %get-tuple-element.113.refs_2_) | copy-start | bytes 3145732
  75.8 23.9 %collective-permute-start.16 = (bf16[2,256,512]{2,1,0:T(8,128)(2,1)S(1)}, bf16[2,256,512]{2,1,0:T(8,128)(2,1)S(1)}, u32[]{:S(2)}, u32[]{:S(2)}) collective-permute-start(bf16[2,256,512]{2,1,0:T(8,128)(2,1)S(1)} %bitcast.16), channel_id=1, source_target_pairs={{0,8},{8,0},{16,24},{24,16},{1,9},{9,1},{17,25},{25,17},{2,10},{10... | collective-permute-start | bytes 1572872 | tf_op jit(solution)/shard_map/ppermute | solution.py:505
  76.4 23.3 %collective-permute-start.17 = (bf16[2,256,512]{2,1,0:T(8,128)(2,1)S(1)}, bf16[2,256,512]{2,1,0:T(8,128)(2,1)S(1)}, u32[]{:S(2)}, u32[]{:S(2)}) collective-permute-start(bf16[2,256,512]{2,1,0:T(8,128)(2,1)S(1)} %bitcast.15), channel_id=1, source_target_pairs={{0,16},{8,24},{16,0},{24,8},{1,17},{9,25},{17,1},{25,9},{2,18},{10... | collective-permute-start | bytes 1572872 | tf_op jit(solution)/shard_map/ppermute | solution.py:509
  77.2 0.7 copy-start.18
  77.9 5.1 %copy-start.14 = (f32[128,1024]{1,0:T(8,128)}, f32[128,1024]{1,0:T(8,128)S(1)}, u32[]{:S(2)}) copy-start(f32[128,1024]{1,0:T(8,128)S(1)} %get-tuple-element.123.refs_0_) | copy-start | bytes 1572868
  77.9 5.1 %copy-start.16 = (f32[128,1024]{1,0:T(8,128)}, f32[128,1024]{1,0:T(8,128)S(1)}, u32[]{:S(2)}) copy-start(f32[128,1024]{1,0:T(8,128)S(1)} %get-tuple-element.125.refs_2_) | copy-start | bytes 1572868
  83.0 10.3 %collective-permute-start.15 = (bf16[544,1024]{1,0:T(8,128)(2,1)S(1)}, bf16[544,1024]{1,0:T(8,128)(2,1)S(1)}, u32[]{:S(2)}, u32[]{:S(2)}) collective-permute-start(bf16[544,1024]{1,0:T(8,128)(2,1)S(1)} %get-tuple-element.106), channel_id=1, source_target_pairs={{0,1},{1,0},{2,3},{3,2},{4,5},{5,4},{6,7},{7,6},{8,9},{9,8},{10,11... | collective-permute-start | bytes 3342344 | tf_op jit(solution)/shard_map/ppermute | solution.py:497
  86.7 6.7 %copy-start.6 = (f32[2,256,512]{2,1,0:T(8,128)}, f32[2,256,512]{2,1,0:T(8,128)S(1)}, u32[]{:S(2)}) copy-start(f32[2,256,512]{2,1,0:T(8,128)S(1)} %get-tuple-element.127.refs_0_) | copy-start | bytes 3145732
  86.7 6.7 %copy-start.8 = (f32[2,256,512]{2,1,0:T(8,128)}, f32[2,256,512]{2,1,0:T(8,128)S(1)}, u32[]{:S(2)}) copy-start(f32[2,256,512]{2,1,0:T(8,128)S(1)} %get-tuple-element.129.refs_2_) | copy-start | bytes 3145732
  91.5 13.9 %collective-permute-start.22 = (bf16[2,256,512]{2,1,0:T(8,128)(2,1)}, bf16[2,256,512]{2,1,0:T(8,128)(2,1)}, u32[]{:S(2)}, u32[]{:S(2)}) collective-permute-start(bf16[2,256,512]{2,1,0:T(8,128)(2,1)} %bitcast.12), channel_id=1, source_target_pairs={{0,8},{8,0},{16,24},{24,16},{1,9},{9,1},{17,25},{25,17},{2,10},{10... | collective-permute-start | bytes 1572872 | tf_op jit(solution)/shard_map/ppermute | solution.py:505
  92.0 15.1 %collective-permute-start.23 = (bf16[2,256,512]{2,1,0:T(8,128)(2,1)}, bf16[2,256,512]{2,1,0:T(8,128)(2,1)}, u32[]{:S(2)}, u32[]{:S(2)}) collective-permute-start(bf16[2,256,512]{2,1,0:T(8,128)(2,1)} %bitcast.13), channel_id=1, source_target_pairs={{0,16},{8,24},{16,0},{24,8},{1,17},{9,25},{17,1},{25,9},{2,18},{10... | collective-permute-start | bytes 1572872 | tf_op jit(solution)/shard_map/ppermute | solution.py:509
  95.1 30.6 %all-to-all-start = ((bf16[4,136,1024]{2,1,0:T(8,128)(2,1)}), bf16[4,136,1024]{2,1,0:T(8,128)(2,1)S(1)}, u32[]{:S(2)}, u32[]{:S(2)}) async-start(bf16[4,136,1024]{2,1,0:T(8,128)(2,1)} %bitcast.7), calls=%async_computation | async-start | bytes 2228224 | tf_op jit(solution)/shard_map/all_to_all | solution.py:556
  98.7 1.0 copy-start.19
  99.6 1.2 copy-start.11
  99.6 1.5 %copy-start.13 = (f32[2,256,512]{2,1,0:T(8,128)S(1)}, f32[2,256,512]{2,1,0:T(8,128)}, u32[]{:S(2)}) copy-start(f32[2,256,512]{2,1,0:T(8,128)} %copy-done.12) | copy-start | bytes 3145732
  101.2 6.0 %copy-start.7 = (f32[2,256,512]{2,1,0:T(8,128)S(1)}, f32[2,256,512]{2,1,0:T(8,128)}, u32[]{:S(2)}) copy-start(f32[2,256,512]{2,1,0:T(8,128)} %copy-done.6) | copy-start | bytes 3145732
  101.2 6.0 %copy-start.9 = (f32[2,256,512]{2,1,0:T(8,128)S(1)}, f32[2,256,512]{2,1,0:T(8,128)}, u32[]{:S(2)}) copy-start(f32[2,256,512]{2,1,0:T(8,128)} %copy-done.8) | copy-start | bytes 3145732
  101.4 19.4 %collective-permute-start.18 = (bf16[256,512]{1,0:T(8,128)(2,1)S(1)}, bf16[256,512]{1,0:T(8,128)(2,1)S(1)}, u32[]{:S(2)}, u32[]{:S(2)}) collective-permute-start(bf16[256,512]{1,0:T(8,128)(2,1)S(1)} %get-tuple-element.120), channel_id=1, source_target_pairs={{0,16},{8,24},{16,0},{24,8},{1,17},{9,25},{17,1},{25,9},{2,18},{10... | collective-permute-start | bytes 786440 | tf_op jit(solution)/shard_map/ppermute | solution.py:509
  103.0 17.9 %collective-permute-start.19 = (bf16[256,512]{1,0:T(8,128)(2,1)S(1)}, bf16[256,512]{1,0:T(8,128)(2,1)S(1)}, u32[]{:S(2)}, u32[]{:S(2)}) collective-permute-start(bf16[256,512]{1,0:T(8,128)(2,1)S(1)} %get-tuple-element.122), channel_id=1, source_target_pairs={{0,8},{8,0},{16,24},{24,16},{1,9},{9,1},{17,25},{25,17},{2,10},{10... | collective-permute-start | bytes 786440 | tf_op jit(solution)/shard_map/ppermute | solution.py:505
  104.5 13.8 %collective-permute-start.20 = (bf16[128,1024]{1,0:T(8,128)(2,1)S(1)}, bf16[128,1024]{1,0:T(8,128)(2,1)S(1)}, u32[]{:S(2)}, u32[]{:S(2)}) collective-permute-start(bf16[128,1024]{1,0:T(8,128)(2,1)S(1)} %get-tuple-element.124), channel_id=1, source_target_pairs={{0,16},{8,24},{16,0},{24,8},{1,17},{9,25},{17,1},{25,9},{2,18},{10... | collective-permute-start | bytes 786440 | tf_op jit(solution)/shard_map/ppermute | solution.py:509
  105.4 14.4 %collective-permute-start.21 = (bf16[128,1024]{1,0:T(8,128)(2,1)S(1)}, bf16[128,1024]{1,0:T(8,128)(2,1)S(1)}, u32[]{:S(2)}, u32[]{:S(2)}) collective-permute-start(bf16[128,1024]{1,0:T(8,128)(2,1)S(1)} %get-tuple-element.126), channel_id=1, source_target_pairs={{0,8},{8,0},{16,24},{24,16},{1,9},{9,1},{17,25},{25,17},{2,10},{10... | collective-permute-start | bytes 786440 | tf_op jit(solution)/shard_map/ppermute | solution.py:505
  107.1 12.6 %copy-start.15 = (f32[128,1024]{1,0:T(8,128)S(1)}, f32[128,1024]{1,0:T(8,128)}, u32[]{:S(2)}) copy-start(f32[128,1024]{1,0:T(8,128)} %copy-done.14) | copy-start | bytes 1572868
  107.1 12.6 %copy-start.17 = (f32[128,1024]{1,0:T(8,128)S(1)}, f32[128,1024]{1,0:T(8,128)}, u32[]{:S(2)}) copy-start(f32[128,1024]{1,0:T(8,128)} %copy-done.16) | copy-start | bytes 1572868
  108.7 13.3 %collective-permute-start.24 = (bf16[256,512]{1,0:T(8,128)(2,1)S(1)}, bf16[256,512]{1,0:T(8,128)(2,1)S(1)}, u32[]{:S(2)}, u32[]{:S(2)}) collective-permute-start(bf16[256,512]{1,0:T(8,128)(2,1)S(1)} %get-tuple-element.136), channel_id=1, source_target_pairs={{0,16},{8,24},{16,0},{24,8},{1,17},{9,25},{17,1},{25,9},{2,18},{10... | collective-permute-start | bytes 786440 | tf_op jit(solution)/shard_map/ppermute | solution.py:509
  118.2 6.4 %collective-permute-start.25 = (bf16[256,512]{1,0:T(8,128)(2,1)S(1)}, bf16[256,512]{1,0:T(8,128)(2,1)S(1)}, u32[]{:S(2)}, u32[]{:S(2)}) collective-permute-start(bf16[256,512]{1,0:T(8,128)(2,1)S(1)} %get-tuple-element.138), channel_id=1, source_target_pairs={{0,8},{8,0},{16,24},{24,16},{1,9},{9,1},{17,25},{25,17},{2,10},{10... | collective-permute-start | bytes 786440 | tf_op jit(solution)/shard_map/ppermute | solution.py:505
  124.6 1.1 copy-start.5
